TPU v7x, 256 devices: a whole 4x4x8 slice. The times are simulated.
256 devices in a mesh: section: 16 (over x, y), col: 16 (over z, core).
Axes of the slice: x: 4, y: 4, z: 8, core: 2. Of those that a mesh axis runs over, the one named last changes fastest.
Arguments:
- features: bfloat16 [4, 32, 65536], P(None, 'section', 'col'), may hold values from -48 to 48
- weights: bfloat16 [16, 512, 4, 128, 128], P('section', 'col'), may hold values from -0.375 to 0.375
- sources: int32 [16, 512, 4], P('section', 'col'), may hold values from 0 to 511, as said below
- bias: float32 [16, 65536], P('section', 'col'), may hold values from -0.3 to 0.3
- batch_rows: int32 [4], replicated, may hold values from 1 to 32, as said below
Outputs:
- final_act: bfloat16 [4, 32, 65536], P(None, 'section', 'col')
Inputs may be any that keep to these rules, and one draw needn't show every extreme that they name: In every layer, the sources of all block columns c with c // 32 = d name exactly 2 distinct blocks b with b // 32 = e, for every pair d, e. `batch_rows`: some micro-batch has exactly 32 live rows.
All inputs are finite; a program needn't handle non-finite values.
Results may differ from a plain program's by a relative error of at most 0.033.
Values may be sent and summed in bfloat16 or wider, within the bound.
A program may use at most 64 MiB of HBM per device.

v0:
```python
import jax
import jax.numpy as jnp
from jax import lax
from jax.sharding import PartitionSpec as P

CAP = 2


def from_behind(x, axis, by):
    size = lax.axis_size(axis)
    pairs = [(i, i + by) for i in range(size) if 0 <= i + by < size]
    return lax.ppermute(x, axis, pairs)


def request_lists(pattern_table, owners, blocks_own, slot_total):
    dest_entries = pattern_table.reshape(owners, -1)
    block_total = owners * blocks_own
    catalog = jnp.arange(block_total, dtype=jnp.int32)
    wanted = jnp.any(dest_entries[:, :, None] == catalog[None, None, :], axis=1)
    wanted = wanted.reshape(owners, owners, blocks_own)
    block_ranks = jnp.cumsum(wanted.astype(jnp.int32), axis=2) - 1
    slot_ids = jnp.arange(slot_total, dtype=jnp.int32)
    chosen = wanted[:, :, None, :] & (block_ranks[:, :, None, :] == slot_ids[None, None, :, None])
    local_ids = jnp.arange(blocks_own, dtype=jnp.int32)
    positions = jnp.sum(chosen.astype(jnp.int32) * local_ids[None, None, None, :], axis=3)
    present = jnp.any(chosen, axis=3)
    return (positions, present)


def body(features, weights, sources, bias, batch_rows):
    sections = lax.axis_size("section")
    owners = lax.axis_size("col")
    section_idx = lax.axis_index("section")
    col_idx = lax.axis_index("col")
    local_w = weights[0]
    blocks_own = local_w.shape[0]
    nonzero_count = local_w.shape[1]
    block_size = local_w.shape[2]
    local_src = sources[0].reshape(blocks_own * nonzero_count)
    local_bias = bias[0].reshape(blocks_own, 1, block_size)
    pattern_table = lax.all_gather(sources[0], "col", axis=0, tiled=True)
    positions, present = request_lists(pattern_table, owners, blocks_own, CAP)
    outgoing = lax.dynamic_index_in_dim(positions, col_idx, 1, keepdims=False).reshape(owners * CAP)
    incoming = lax.dynamic_index_in_dim(positions, col_idx, 0, keepdims=False)
    incoming_ok = lax.dynamic_index_in_dim(present, col_idx, 0, keepdims=False)
    global_ids = incoming + blocks_own * jnp.arange(owners, dtype=jnp.int32)[:, None]
    matches = (local_src[:, None] == global_ids.reshape(-1)[None, :]) & incoming_ok.reshape(-1)[
        None, :
    ]
    slot_of = jnp.sum(
        matches.astype(jnp.int32) * jnp.arange(owners * CAP, dtype=jnp.int32)[None, :], axis=1
    )
    all_inputs = lax.all_gather(features, "section", axis=1, tiled=True)
    batches = all_inputs.shape[0]
    row_total = all_inputs.shape[1]
    pieces = 1
    part_rows = row_total // pieces
    piece_total = batches * pieces
    tick_total = piece_total + sections - 1
    blocks_in = all_inputs.reshape(batches, pieces, part_rows, blocks_own, block_size)
    blocks_in = blocks_in.transpose(0, 1, 3, 2, 4).reshape(
        piece_total, blocks_own, part_rows, block_size
    )

    def combine(received):
        rows_here = received.shape[2]
        flat_recv = received.reshape(owners * CAP, rows_here, block_size)
        picked = jnp.take(flat_recv, slot_of, axis=0).reshape(
            blocks_own, nonzero_count, rows_here, block_size
        )
        preact = jnp.einsum("ckrb,ckbo->cro", picked, local_w, preferred_element_type=jnp.float32)
        return jnp.clip(preact + local_bias, 0.0, 32.0).astype(jnp.bfloat16)

    def apply_layer(carried):
        payload = jnp.take(carried, outgoing, axis=0).reshape(
            owners, CAP, carried.shape[1], block_size
        )
        return combine(lax.all_to_all(payload, "col", split_axis=0, concat_axis=0, tiled=True))

    def tick(tick_idx, carry):
        carried, finished = carry
        entering = lax.dynamic_index_in_dim(
            blocks_in, jnp.minimum(tick_idx, piece_total - 1), 0, keepdims=False
        )
        current = jnp.where(section_idx == 0, entering, carried)
        layer_out = apply_layer(current)
        slot_idx = jnp.clip(tick_idx - sections + 1, 0, piece_total - 1)
        storing = (section_idx == sections - 1) & (tick_idx >= sections - 1)
        existing = lax.dynamic_index_in_dim(finished, slot_idx, 0, keepdims=False)
        finished = lax.dynamic_update_index_in_dim(
            finished, jnp.where(storing, layer_out, existing), slot_idx, 0
        )
        passed = from_behind(layer_out, "section", 1)
        return (passed, finished)

    initial = (
        jnp.zeros((blocks_own, part_rows, block_size), jnp.bfloat16),
        jnp.zeros((piece_total, blocks_own, part_rows, block_size), jnp.bfloat16),
    )
    carried, finished = lax.fori_loop(0, tick_total, tick, initial)
    completed = finished.reshape(batches, pieces, blocks_own, part_rows, block_size)
    completed = completed.transpose(0, 1, 3, 2, 4).reshape(
        batches, row_total, blocks_own * block_size
    )
    own_rows = row_total // sections
    outgoing_rows = completed.reshape(batches, sections, own_rows, blocks_own * block_size)
    gathered = lax.all_to_all(outgoing_rows, "section", split_axis=1, concat_axis=1, tiled=True)
    own_result = gathered[:, sections - 1]
    row_ids = section_idx * own_rows + jnp.arange(own_rows, dtype=jnp.int32)
    row_mask = row_ids[None, :] < batch_rows[:, None]
    return jnp.where(row_mask[:, :, None], own_result, jnp.zeros_like(own_result))


def solution(mesh):
    in_specs = (
        P(None, "section", "col"),
        P("section", "col", None, None, None),
        P("section", "col", None),
        P("section", "col"),
        P(),
    )
    out_specs = P(None, "section", "col")
    return jax.shard_map(body, mesh=mesh, in_specs=in_specs, out_specs=out_specs, check_vma=False)
```

profile of v0, /device:TPU:28, one launch (start us, length us, event | category | flops | bytes accessed | tf_op | source)
XLA Modules:
  0.0 742.7 jit_solution(5742801372019623297)
XLA Ops:
  9.9 20.7 %all-gather = s32[1,512,4]{2,0,1:T(1,128)S(1)} all-gather(s32[1,32,4]{2,0,1:T(1,128)S(1)} %copy.19), channel_id=2, replica_groups=mesh['section'=16,'col'=16] {'col'}, dimensions={1}, use_global_device_ids=true | all-gather | bytes 8704 | tf_op jit(solution)/shard_map/all_gather | solution.py:41
  38.9 19.3 %all-gather.3.cloned.1.call-done = bf16[4,32,4096]{2,0,1:T(4,128)(2,1)} async-done(((bf16[4,2,4096]{2,0,1:T(4,128)(2,1)}), bf16[4,32,4096]{2,0,1:T(4,128)(2,1)}) %all-gather.3.cloned.1.call-update) | async-done | bytes 1048592 | tf_op jit(solution)/shard_map/all_gather | solution.py:53
  61.4 648.7 %while.19 = (s32[]{:T(128)}, bf16[32,32,128]{2,1,0:T(8,128)(2,1)S(1)}, bf16[4,32,32,128]{3,2,1,0:T(8,128)(2,1)S(1)}, s32[128]{0:T(128)S(1)}, s32[32]{0:T(128)S(1...) while((s32[]{:T(128)}, ...), condition=%wide.region_6.7_spmd, body=%wide.region_5.6_spmd.sunk | while | flops 135531952 | bytes 12878729 | solution.py:100
  64.1 7.1 all-to-all-start
  71.4 11.0 %all-to-all-done = bf16[16,2,32,128]{3,2,1,0:T(8,128)(2,1)S(1)} async-done(((bf16[16,2,32,128]{3,2,1,0:T(8,128)(2,1)}), bf16[16,2,32,128]{3,2,1,0:T(8,128)(2,1)S(1)}, u32[]{:S(2)}, u32[]{:S(2)}) %all-to-all-start) | async-done | bytes 262176 | tf_op jit(solution)/shard_map/while/body/eval_jaxpr/all_to_all | solution.py:78
  90.8 6.7 collective-permute-done
  103.9 10.8 %all-to-all-done = bf16[16,2,32,128]{3,2,1,0:T(8,128)(2,1)S(1)} async-done(((bf16[16,2,32,128]{3,2,1,0:T(8,128)(2,1)}), bf16[16,2,32,128]{3,2,1,0:T(8,128)(2,1)S(1)}, u32[]{:S(2)}, u32[]{:S(2)}) %all-to-all-start) | async-done | bytes 262176 | tf_op jit(solution)/shard_map/while/body/eval_jaxpr/all_to_all | solution.py:78
  137.9 10.8 %all-to-all-done = bf16[16,2,32,128]{3,2,1,0:T(8,128)(2,1)S(1)} async-done(((bf16[16,2,32,128]{3,2,1,0:T(8,128)(2,1)}), bf16[16,2,32,128]{3,2,1,0:T(8,128)(2,1)S(1)}, u32[]{:S(2)}, u32[]{:S(2)}) %all-to-all-start) | async-done | bytes 262176 | tf_op jit(solution)/shard_map/while/body/eval_jaxpr/all_to_all | solution.py:78
  152.5 6.5 collective-permute-start
  159.0 6.5 collective-permute-done
  171.9 10.8 %all-to-all-done = bf16[16,2,32,128]{3,2,1,0:T(8,128)(2,1)S(1)} async-done(((bf16[16,2,32,128]{3,2,1,0:T(8,128)(2,1)}), bf16[16,2,32,128]{3,2,1,0:T(8,128)(2,1)S(1)}, u32[]{:S(2)}, u32[]{:S(2)}) %all-to-all-start) | async-done | bytes 262176 | tf_op jit(solution)/shard_map/while/body/eval_jaxpr/all_to_all | solution.py:78
  186.6 6.5 collective-permute-start
  205.9 10.8 %all-to-all-done = bf16[16,2,32,128]{3,2,1,0:T(8,128)(2,1)S(1)} async-done(((bf16[16,2,32,128]{3,2,1,0:T(8,128)(2,1)}), bf16[16,2,32,128]{3,2,1,0:T(8,128)(2,1)S(1)}, u32[]{:S(2)}, u32[]{:S(2)}) %all-to-all-start) | async-done | bytes 262176 | tf_op jit(solution)/shard_map/while/body/eval_jaxpr/all_to_all | solution.py:78
  220.6 6.5 collective-permute-start
  227.1 6.5 collective-permute-done
  240.0 10.8 %all-to-all-done = bf16[16,2,32,128]{3,2,1,0:T(8,128)(2,1)S(1)} async-done(((bf16[16,2,32,128]{3,2,1,0:T(8,128)(2,1)}), bf16[16,2,32,128]{3,2,1,0:T(8,128)(2,1)S(1)}, u32[]{:S(2)}, u32[]{:S(2)}) %all-to-all-start) | async-done | bytes 262176 | tf_op jit(solution)/shard_map/while/body/eval_jaxpr/all_to_all | solution.py:78
  254.6 6.5 collective-permute-start
  261.2 6.5 collective-permute-done
  274.0 10.8 %all-to-all-done = bf16[16,2,32,128]{3,2,1,0:T(8,128)(2,1)S(1)} async-done(((bf16[16,2,32,128]{3,2,1,0:T(8,128)(2,1)}), bf16[16,2,32,128]{3,2,1,0:T(8,128)(2,1)S(1)}, u32[]{:S(2)}, u32[]{:S(2)}) %all-to-all-start) | async-done | bytes 262176 | tf_op jit(solution)/shard_map/while/body/eval_jaxpr/all_to_all | solution.py:78
  288.7 6.5 collective-permute-start
  308.1 10.8 %all-to-all-done = bf16[16,2,32,128]{3,2,1,0:T(8,128)(2,1)S(1)} async-done(((bf16[16,2,32,128]{3,2,1,0:T(8,128)(2,1)}), bf16[16,2,32,128]{3,2,1,0:T(8,128)(2,1)S(1)}, u32[]{:S(2)}, u32[]{:S(2)}) %all-to-all-start) | async-done | bytes 262176 | tf_op jit(solution)/shard_map/while/body/eval_jaxpr/all_to_all | solution.py:78
  322.7 6.5 collective-permute-start
  342.1 10.8 %all-to-all-done = bf16[16,2,32,128]{3,2,1,0:T(8,128)(2,1)S(1)} async-done(((bf16[16,2,32,128]{3,2,1,0:T(8,128)(2,1)}), bf16[16,2,32,128]{3,2,1,0:T(8,128)(2,1)S(1)}, u32[]{:S(2)}, u32[]{:S(2)}) %all-to-all-start) | async-done | bytes 262176 | tf_op jit(solution)/shard_map/while/body/eval_jaxpr/all_to_all | solution.py:78
  356.8 6.5 collective-permute-start
  363.3 6.5 collective-permute-done
  376.1 10.8 %all-to-all-done = bf16[16,2,32,128]{3,2,1,0:T(8,128)(2,1)S(1)} async-done(((bf16[16,2,32,128]{3,2,1,0:T(8,128)(2,1)}), bf16[16,2,32,128]{3,2,1,0:T(8,128)(2,1)S(1)}, u32[]{:S(2)}, u32[]{:S(2)}) %all-to-all-start) | async-done | bytes 262176 | tf_op jit(solution)/shard_map/while/body/eval_jaxpr/all_to_all | solution.py:78
  390.8 6.5 collective-permute-start
  397.3 6.5 collective-permute-done
  410.2 10.8 %all-to-all-done = bf16[16,2,32,128]{3,2,1,0:T(8,128)(2,1)S(1)} async-done(((bf16[16,2,32,128]{3,2,1,0:T(8,128)(2,1)}), bf16[16,2,32,128]{3,2,1,0:T(8,128)(2,1)S(1)}, u32[]{:S(2)}, u32[]{:S(2)}) %all-to-all-start) | async-done | bytes 262176 | tf_op jit(solution)/shard_map/while/body/eval_jaxpr/all_to_all | solution.py:78
  424.8 6.5 collective-permute-start
  444.2 10.8 %all-to-all-done = bf16[16,2,32,128]{3,2,1,0:T(8,128)(2,1)S(1)} async-done(((bf16[16,2,32,128]{3,2,1,0:T(8,128)(2,1)}), bf16[16,2,32,128]{3,2,1,0:T(8,128)(2,1)S(1)}, u32[]{:S(2)}, u32[]{:S(2)}) %all-to-all-start) | async-done | bytes 262176 | tf_op jit(solution)/shard_map/while/body/eval_jaxpr/all_to_all | solution.py:78
  458.9 6.5 collective-permute-start
  478.2 10.8 %all-to-all-done = bf16[16,2,32,128]{3,2,1,0:T(8,128)(2,1)S(1)} async-done(((bf16[16,2,32,128]{3,2,1,0:T(8,128)(2,1)}), bf16[16,2,32,128]{3,2,1,0:T(8,128)(2,1)S(1)}, u32[]{:S(2)}, u32[]{:S(2)}) %all-to-all-start) | async-done | bytes 262176 | tf_op jit(solution)/shard_map/while/body/eval_jaxpr/all_to_all | solution.py:78
  492.9 6.5 collective-permute-start
  512.3 10.8 %all-to-all-done = bf16[16,2,32,128]{3,2,1,0:T(8,128)(2,1)S(1)} async-done(((bf16[16,2,32,128]{3,2,1,0:T(8,128)(2,1)}), bf16[16,2,32,128]{3,2,1,0:T(8,128)(2,1)S(1)}, u32[]{:S(2)}, u32[]{:S(2)}) %all-to-all-start) | async-done | bytes 262176 | tf_op jit(solution)/shard_map/while/body/eval_jaxpr/all_to_all | solution.py:78
  526.9 6.5 collective-permute-start
  546.3 10.8 %all-to-all-done = bf16[16,2,32,128]{3,2,1,0:T(8,128)(2,1)S(1)} async-done(((bf16[16,2,32,128]{3,2,1,0:T(8,128)(2,1)}), bf16[16,2,32,128]{3,2,1,0:T(8,128)(2,1)S(1)}, u32[]{:S(2)}, u32[]{:S(2)}) %all-to-all-start) | async-done | bytes 262176 | tf_op jit(solution)/shard_map/while/body/eval_jaxpr/all_to_all | solution.py:78
  561.0 6.5 collective-permute-start
  580.4 10.8 %all-to-all-done = bf16[16,2,32,128]{3,2,1,0:T(8,128)(2,1)S(1)} async-done(((bf16[16,2,32,128]{3,2,1,0:T(8,128)(2,1)}), bf16[16,2,32,128]{3,2,1,0:T(8,128)(2,1)S(1)}, u32[]{:S(2)}, u32[]{:S(2)}) %all-to-all-start) | async-done | bytes 262176 | tf_op jit(solution)/shard_map/while/body/eval_jaxpr/all_to_all | solution.py:78
  595.0 6.5 collective-permute-start
  614.4 10.8 %all-to-all-done = bf16[16,2,32,128]{3,2,1,0:T(8,128)(2,1)S(1)} async-done(((bf16[16,2,32,128]{3,2,1,0:T(8,128)(2,1)}), bf16[16,2,32,128]{3,2,1,0:T(8,128)(2,1)S(1)}, u32[]{:S(2)}, u32[]{:S(2)}) %all-to-all-start) | async-done | bytes 262176 | tf_op jit(solution)/shard_map/while/body/eval_jaxpr/all_to_all | solution.py:78
  629.1 6.5 collective-permute-start
  648.4 10.8 %all-to-all-done = bf16[16,2,32,128]{3,2,1,0:T(8,128)(2,1)S(1)} async-done(((bf16[16,2,32,128]{3,2,1,0:T(8,128)(2,1)}), bf16[16,2,32,128]{3,2,1,0:T(8,128)(2,1)S(1)}, u32[]{:S(2)}, u32[]{:S(2)}) %all-to-all-start) | async-done | bytes 262176 | tf_op jit(solution)/shard_map/while/body/eval_jaxpr/all_to_all | solution.py:78
  663.1 6.5 collective-permute-start
  682.5 10.8 %all-to-all-done = bf16[16,2,32,128]{3,2,1,0:T(8,128)(2,1)S(1)} async-done(((bf16[16,2,32,128]{3,2,1,0:T(8,128)(2,1)}), bf16[16,2,32,128]{3,2,1,0:T(8,128)(2,1)S(1)}, u32[]{:S(2)}, u32[]{:S(2)}) %all-to-all-start) | async-done | bytes 262176 | tf_op jit(solution)/shard_map/while/body/eval_jaxpr/all_to_all | solution.py:78
  697.1 6.5 collective-permute-start
  713.0 8.1 %all-to-all-start.1 = ((bf16[4,16,2,4096]{3,2,0,1:T(2,128)(2,1)}), bf16[4,16,2,4096]{3,2,0,1:T(2,128)(2,1)S(1)}, u32[]{:S(2)}, u32[]{:S(2)}) async-start(bf16[4,16,2,4096]{3,2,0,1:T(2,128)(2,1)} %copy.26), calls=%async_computation.1 | async-start | bytes 2097152 | tf_op jit(solution)/shard_map/all_to_all | solution.py:107
  721.2 13.9 %all-to-all-done.1 = bf16[4,16,2,4096]{3,2,0,1:T(2,128)(2,1)S(1)} async-done(((bf16[4,16,2,4096]{3,2,0,1:T(2,128)(2,1)}), bf16[4,16,2,4096]{3,2,0,1:T(2,128)(2,1)S(1)}, u32[]{:S(2)}, u32[]{:S(2)}) %all-to-all-start.1) | async-done | bytes 1048608 | tf_op jit(solution)/shard_map/all_to_all | solution.py:107
  (360 shorter events, 302.8 us)
Async XLA Ops:
  6.5 54.9 %copy-start = (f32[1,4096]{1,0:T(1,128)S(1)}, f32[1,4096]{1,0:T(1,128)}, u32[]{:S(2)}) copy-start(f32[1,4096]{1,0:T(1,128)} %param.10) | copy-start | bytes 49156
  6.5 51.7 %all-gather.3.cloned.1.call-start = ((), (), s32[]{:S(2)}) async-start(), calls=%async_computation.2 | async-start | bytes 1114112 | tf_op jit(solution)/shard_map/all_gather | solution.py:53
  64.1 18.3 %all-to-all-start = ((bf16[16,2,32,128]{3,2,1,0:T(8,128)(2,1)}), bf16[16,2,32,128]{3,2,1,0:T(8,128)(2,1)S(1)}, u32[]{:S(2)}, u32[]{:S(2)}) async-start(bf16[16,2,32,128]{3,2,1,0:T(8,128)(2,1)} %broadcast_select_fusion.3), calls=%async_computation | async-start | bytes 524288 | tf_op jit(solution)/shard_map/while/body/eval_jaxpr/all_to_all | solution.py:78
  86.2 11.2 %collective-permute-start = (bf16[32,32,128]{2,1,0:T(8,128)(2,1)S(1)}, bf16[32,32,128]{2,1,0:T(8,128)(2,1)S(1)}, u32[]{:S(2)}, u32[]{:S(2)}) collective-permute-start(bf16[32,32,128]{2,1,0:T(8,128)(2,1)S(1)} %get-tuple-element.421), channel_id=1, source_target_pairs={{0,16},{16,32},{32,48},{48,64},{64,80},{80,96},{96,112},{112,128},... | collective-permute-start | bytes 786440 | tf_op jit(solution)/shard_map/while/body/eval_jaxpr/ppermute | solution.py:12
  100.1 14.5 %all-to-all-start = ((bf16[16,2,32,128]{3,2,1,0:T(8,128)(2,1)}), bf16[16,2,32,128]{3,2,1,0:T(8,128)(2,1)S(1)}, u32[]{:S(2)}, u32[]{:S(2)}) async-start(bf16[16,2,32,128]{3,2,1,0:T(8,128)(2,1)} %broadcast_select_fusion.3), calls=%async_computation | async-start | bytes 524288 | tf_op jit(solution)/shard_map/while/body/eval_jaxpr/all_to_all | solution.py:78
  118.5 13.0 %collective-permute-start = (bf16[32,32,128]{2,1,0:T(8,128)(2,1)S(1)}, bf16[32,32,128]{2,1,0:T(8,128)(2,1)S(1)}, u32[]{:S(2)}, u32[]{:S(2)}) collective-permute-start(bf16[32,32,128]{2,1,0:T(8,128)(2,1)S(1)} %get-tuple-element.421), channel_id=1, source_target_pairs={{0,16},{16,32},{32,48},{48,64},{64,80},{80,96},{96,112},{112,128},... | collective-permute-start | bytes 786440 | tf_op jit(solution)/shard_map/while/body/eval_jaxpr/ppermute | solution.py:12
  134.1 14.5 %all-to-all-start = ((bf16[16,2,32,128]{3,2,1,0:T(8,128)(2,1)}), bf16[16,2,32,128]{3,2,1,0:T(8,128)(2,1)S(1)}, u32[]{:S(2)}, u32[]{:S(2)}) async-start(bf16[16,2,32,128]{3,2,1,0:T(8,128)(2,1)} %broadcast_select_fusion.3), calls=%async_computation | async-start | bytes 524288 | tf_op jit(solution)/shard_map/while/body/eval_jaxpr/all_to_all | solution.py:78
  152.5 13.0 %collective-permute-start = (bf16[32,32,128]{2,1,0:T(8,128)(2,1)S(1)}, bf16[32,32,128]{2,1,0:T(8,128)(2,1)S(1)}, u32[]{:S(2)}, u32[]{:S(2)}) collective-permute-start(bf16[32,32,128]{2,1,0:T(8,128)(2,1)S(1)} %get-tuple-element.421), channel_id=1, source_target_pairs={{0,16},{16,32},{32,48},{48,64},{64,80},{80,96},{96,112},{112,128},... | collective-permute-start | bytes 786440 | tf_op jit(solution)/shard_map/while/body/eval_jaxpr/ppermute | solution.py:12
  168.2 14.5 %all-to-all-start = ((bf16[16,2,32,128]{3,2,1,0:T(8,128)(2,1)}), bf16[16,2,32,128]{3,2,1,0:T(8,128)(2,1)S(1)}, u32[]{:S(2)}, u32[]{:S(2)}) async-start(bf16[16,2,32,128]{3,2,1,0:T(8,128)(2,1)} %broadcast_select_fusion.3), calls=%async_computation | async-start | bytes 524288 | tf_op jit(solution)/shard_map/while/body/eval_jaxpr/all_to_all | solution.py:78
  186.6 13.0 %collective-permute-start = (bf16[32,32,128]{2,1,0:T(8,128)(2,1)S(1)}, bf16[32,32,128]{2,1,0:T(8,128)(2,1)S(1)}, u32[]{:S(2)}, u32[]{:S(2)}) collective-permute-start(bf16[32,32,128]{2,1,0:T(8,128)(2,1)S(1)} %get-tuple-element.421), channel_id=1, source_target_pairs={{0,16},{16,32},{32,48},{48,64},{64,80},{80,96},{96,112},{112,128},... | collective-permute-start | bytes 786440 | tf_op jit(solution)/shard_map/while/body/eval_jaxpr/ppermute | solution.py:12
  202.2 14.5 %all-to-all-start = ((bf16[16,2,32,128]{3,2,1,0:T(8,128)(2,1)}), bf16[16,2,32,128]{3,2,1,0:T(8,128)(2,1)S(1)}, u32[]{:S(2)}, u32[]{:S(2)}) async-start(bf16[16,2,32,128]{3,2,1,0:T(8,128)(2,1)} %broadcast_select_fusion.3), calls=%async_computation | async-start | bytes 524288 | tf_op jit(solution)/shard_map/while/body/eval_jaxpr/all_to_all | solution.py:78
  220.6 13.0 %collective-permute-start = (bf16[32,32,128]{2,1,0:T(8,128)(2,1)S(1)}, bf16[32,32,128]{2,1,0:T(8,128)(2,1)S(1)}, u32[]{:S(2)}, u32[]{:S(2)}) collective-permute-start(bf16[32,32,128]{2,1,0:T(8,128)(2,1)S(1)} %get-tuple-element.421), channel_id=1, source_target_pairs={{0,16},{16,32},{32,48},{48,64},{64,80},{80,96},{96,112},{112,128},... | collective-permute-start | bytes 786440 | tf_op jit(solution)/shard_map/while/body/eval_jaxpr/ppermute | solution.py:12
  236.3 14.5 %all-to-all-start = ((bf16[16,2,32,128]{3,2,1,0:T(8,128)(2,1)}), bf16[16,2,32,128]{3,2,1,0:T(8,128)(2,1)S(1)}, u32[]{:S(2)}, u32[]{:S(2)}) async-start(bf16[16,2,32,128]{3,2,1,0:T(8,128)(2,1)} %broadcast_select_fusion.3), calls=%async_computation | async-start | bytes 524288 | tf_op jit(solution)/shard_map/while/body/eval_jaxpr/all_to_all | solution.py:78
  254.6 13.0 %collective-permute-start = (bf16[32,32,128]{2,1,0:T(8,128)(2,1)S(1)}, bf16[32,32,128]{2,1,0:T(8,128)(2,1)S(1)}, u32[]{:S(2)}, u32[]{:S(2)}) collective-permute-start(bf16[32,32,128]{2,1,0:T(8,128)(2,1)S(1)} %get-tuple-element.421), channel_id=1, source_target_pairs={{0,16},{16,32},{32,48},{48,64},{64,80},{80,96},{96,112},{112,128},... | collective-permute-start | bytes 786440 | tf_op jit(solution)/shard_map/while/body/eval_jaxpr/ppermute | solution.py:12
  270.3 14.5 %all-to-all-start = ((bf16[16,2,32,128]{3,2,1,0:T(8,128)(2,1)}), bf16[16,2,32,128]{3,2,1,0:T(8,128)(2,1)S(1)}, u32[]{:S(2)}, u32[]{:S(2)}) async-start(bf16[16,2,32,128]{3,2,1,0:T(8,128)(2,1)} %broadcast_select_fusion.3), calls=%async_computation | async-start | bytes 524288 | tf_op jit(solution)/shard_map/while/body/eval_jaxpr/all_to_all | solution.py:78
  288.7 13.0 %collective-permute-start = (bf16[32,32,128]{2,1,0:T(8,128)(2,1)S(1)}, bf16[32,32,128]{2,1,0:T(8,128)(2,1)S(1)}, u32[]{:S(2)}, u32[]{:S(2)}) collective-permute-start(bf16[32,32,128]{2,1,0:T(8,128)(2,1)S(1)} %get-tuple-element.421), channel_id=1, source_target_pairs={{0,16},{16,32},{32,48},{48,64},{64,80},{80,96},{96,112},{112,128},... | collective-permute-start | bytes 786440 | tf_op jit(solution)/shard_map/while/body/eval_jaxpr/ppermute | solution.py:12
  304.3 14.5 %all-to-all-start = ((bf16[16,2,32,128]{3,2,1,0:T(8,128)(2,1)}), bf16[16,2,32,128]{3,2,1,0:T(8,128)(2,1)S(1)}, u32[]{:S(2)}, u32[]{:S(2)}) async-start(bf16[16,2,32,128]{3,2,1,0:T(8,128)(2,1)} %broadcast_select_fusion.3), calls=%async_computation | async-start | bytes 524288 | tf_op jit(solution)/shard_map/while/body/eval_jaxpr/all_to_all | solution.py:78
  322.7 13.0 %collective-permute-start = (bf16[32,32,128]{2,1,0:T(8,128)(2,1)S(1)}, bf16[32,32,128]{2,1,0:T(8,128)(2,1)S(1)}, u32[]{:S(2)}, u32[]{:S(2)}) collective-permute-start(bf16[32,32,128]{2,1,0:T(8,128)(2,1)S(1)} %get-tuple-element.421), channel_id=1, source_target_pairs={{0,16},{16,32},{32,48},{48,64},{64,80},{80,96},{96,112},{112,128},... | collective-permute-start | bytes 786440 | tf_op jit(solution)/shard_map/while/body/eval_jaxpr/ppermute | solution.py:12
  338.4 14.5 %all-to-all-start = ((bf16[16,2,32,128]{3,2,1,0:T(8,128)(2,1)}), bf16[16,2,32,128]{3,2,1,0:T(8,128)(2,1)S(1)}, u32[]{:S(2)}, u32[]{:S(2)}) async-start(bf16[16,2,32,128]{3,2,1,0:T(8,128)(2,1)} %broadcast_select_fusion.3), calls=%async_computation | async-start | bytes 524288 | tf_op jit(solution)/shard_map/while/body/eval_jaxpr/all_to_all | solution.py:78
  356.8 13.0 %collective-permute-start = (bf16[32,32,128]{2,1,0:T(8,128)(2,1)S(1)}, bf16[32,32,128]{2,1,0:T(8,128)(2,1)S(1)}, u32[]{:S(2)}, u32[]{:S(2)}) collective-permute-start(bf16[32,32,128]{2,1,0:T(8,128)(2,1)S(1)} %get-tuple-element.421), channel_id=1, source_target_pairs={{0,16},{16,32},{32,48},{48,64},{64,80},{80,96},{96,112},{112,128},... | collective-permute-start | bytes 786440 | tf_op jit(solution)/shard_map/while/body/eval_jaxpr/ppermute | solution.py:12
  372.4 14.5 %all-to-all-start = ((bf16[16,2,32,128]{3,2,1,0:T(8,128)(2,1)}), bf16[16,2,32,128]{3,2,1,0:T(8,128)(2,1)S(1)}, u32[]{:S(2)}, u32[]{:S(2)}) async-start(bf16[16,2,32,128]{3,2,1,0:T(8,128)(2,1)} %broadcast_select_fusion.3), calls=%async_computation | async-start | bytes 524288 | tf_op jit(solution)/shard_map/while/body/eval_jaxpr/all_to_all | solution.py:78
  390.8 13.0 %collective-permute-start = (bf16[32,32,128]{2,1,0:T(8,128)(2,1)S(1)}, bf16[32,32,128]{2,1,0:T(8,128)(2,1)S(1)}, u32[]{:S(2)}, u32[]{:S(2)}) collective-permute-start(bf16[32,32,128]{2,1,0:T(8,128)(2,1)S(1)} %get-tuple-element.421), channel_id=1, source_target_pairs={{0,16},{16,32},{32,48},{48,64},{64,80},{80,96},{96,112},{112,128},... | collective-permute-start | bytes 786440 | tf_op jit(solution)/shard_map/while/body/eval_jaxpr/ppermute | solution.py:12
  406.4 14.5 %all-to-all-start = ((bf16[16,2,32,128]{3,2,1,0:T(8,128)(2,1)}), bf16[16,2,32,128]{3,2,1,0:T(8,128)(2,1)S(1)}, u32[]{:S(2)}, u32[]{:S(2)}) async-start(bf16[16,2,32,128]{3,2,1,0:T(8,128)(2,1)} %broadcast_select_fusion.3), calls=%async_computation | async-start | bytes 524288 | tf_op jit(solution)/shard_map/while/body/eval_jaxpr/all_to_all | solution.py:78
  424.8 13.0 %collective-permute-start = (bf16[32,32,128]{2,1,0:T(8,128)(2,1)S(1)}, bf16[32,32,128]{2,1,0:T(8,128)(2,1)S(1)}, u32[]{:S(2)}, u32[]{:S(2)}) collective-permute-start(bf16[32,32,128]{2,1,0:T(8,128)(2,1)S(1)} %get-tuple-element.421), channel_id=1, source_target_pairs={{0,16},{16,32},{32,48},{48,64},{64,80},{80,96},{96,112},{112,128},... | collective-permute-start | bytes 786440 | tf_op jit(solution)/shard_map/while/body/eval_jaxpr/ppermute | solution.py:12
  440.5 14.5 %all-to-all-start = ((bf16[16,2,32,128]{3,2,1,0:T(8,128)(2,1)}), bf16[16,2,32,128]{3,2,1,0:T(8,128)(2,1)S(1)}, u32[]{:S(2)}, u32[]{:S(2)}) async-start(bf16[16,2,32,128]{3,2,1,0:T(8,128)(2,1)} %broadcast_select_fusion.3), calls=%async_computation | async-start | bytes 524288 | tf_op jit(solution)/shard_map/while/body/eval_jaxpr/all_to_all | solution.py:78
  458.9 13.0 %collective-permute-start = (bf16[32,32,128]{2,1,0:T(8,128)(2,1)S(1)}, bf16[32,32,128]{2,1,0:T(8,128)(2,1)S(1)}, u32[]{:S(2)}, u32[]{:S(2)}) collective-permute-start(bf16[32,32,128]{2,1,0:T(8,128)(2,1)S(1)} %get-tuple-element.421), channel_id=1, source_target_pairs={{0,16},{16,32},{32,48},{48,64},{64,80},{80,96},{96,112},{112,128},... | collective-permute-start | bytes 786440 | tf_op jit(solution)/shard_map/while/body/eval_jaxpr/ppermute | solution.py:12
  474.5 14.5 %all-to-all-start = ((bf16[16,2,32,128]{3,2,1,0:T(8,128)(2,1)}), bf16[16,2,32,128]{3,2,1,0:T(8,128)(2,1)S(1)}, u32[]{:S(2)}, u32[]{:S(2)}) async-start(bf16[16,2,32,128]{3,2,1,0:T(8,128)(2,1)} %broadcast_select_fusion.3), calls=%async_computation | async-start | bytes 524288 | tf_op jit(solution)/shard_map/while/body/eval_jaxpr/all_to_all | solution.py:78
  492.9 13.0 %collective-permute-start = (bf16[32,32,128]{2,1,0:T(8,128)(2,1)S(1)}, bf16[32,32,128]{2,1,0:T(8,128)(2,1)S(1)}, u32[]{:S(2)}, u32[]{:S(2)}) collective-permute-start(bf16[32,32,128]{2,1,0:T(8,128)(2,1)S(1)} %get-tuple-element.421), channel_id=1, source_target_pairs={{0,16},{16,32},{32,48},{48,64},{64,80},{80,96},{96,112},{112,128},... | collective-permute-start | bytes 786440 | tf_op jit(solution)/shard_map/while/body/eval_jaxpr/ppermute | solution.py:12
  508.6 14.5 %all-to-all-start = ((bf16[16,2,32,128]{3,2,1,0:T(8,128)(2,1)}), bf16[16,2,32,128]{3,2,1,0:T(8,128)(2,1)S(1)}, u32[]{:S(2)}, u32[]{:S(2)}) async-start(bf16[16,2,32,128]{3,2,1,0:T(8,128)(2,1)} %broadcast_select_fusion.3), calls=%async_computation | async-start | bytes 524288 | tf_op jit(solution)/shard_map/while/body/eval_jaxpr/all_to_all | solution.py:78
  526.9 13.0 %collective-permute-start = (bf16[32,32,128]{2,1,0:T(8,128)(2,1)S(1)}, bf16[32,32,128]{2,1,0:T(8,128)(2,1)S(1)}, u32[]{:S(2)}, u32[]{:S(2)}) collective-permute-start(bf16[32,32,128]{2,1,0:T(8,128)(2,1)S(1)} %get-tuple-element.421), channel_id=1, source_target_pairs={{0,16},{16,32},{32,48},{48,64},{64,80},{80,96},{96,112},{112,128},... | collective-permute-start | bytes 786440 | tf_op jit(solution)/shard_map/while/body/eval_jaxpr/ppermute | solution.py:12
  542.6 14.5 %all-to-all-start = ((bf16[16,2,32,128]{3,2,1,0:T(8,128)(2,1)}), bf16[16,2,32,128]{3,2,1,0:T(8,128)(2,1)S(1)}, u32[]{:S(2)}, u32[]{:S(2)}) async-start(bf16[16,2,32,128]{3,2,1,0:T(8,128)(2,1)} %broadcast_select_fusion.3), calls=%async_computation | async-start | bytes 524288 | tf_op jit(solution)/shard_map/while/body/eval_jaxpr/all_to_all | solution.py:78
  561.0 13.0 %collective-permute-start = (bf16[32,32,128]{2,1,0:T(8,128)(2,1)S(1)}, bf16[32,32,128]{2,1,0:T(8,128)(2,1)S(1)}, u32[]{:S(2)}, u32[]{:S(2)}) collective-permute-start(bf16[32,32,128]{2,1,0:T(8,128)(2,1)S(1)} %get-tuple-element.421), channel_id=1, source_target_pairs={{0,16},{16,32},{32,48},{48,64},{64,80},{80,96},{96,112},{112,128},... | collective-permute-start | bytes 786440 | tf_op jit(solution)/shard_map/while/body/eval_jaxpr/ppermute | solution.py:12
  576.6 14.5 %all-to-all-start = ((bf16[16,2,32,128]{3,2,1,0:T(8,128)(2,1)}), bf16[16,2,32,128]{3,2,1,0:T(8,128)(2,1)S(1)}, u32[]{:S(2)}, u32[]{:S(2)}) async-start(bf16[16,2,32,128]{3,2,1,0:T(8,128)(2,1)} %broadcast_select_fusion.3), calls=%async_computation | async-start | bytes 524288 | tf_op jit(solution)/shard_map/while/body/eval_jaxpr/all_to_all | solution.py:78
  595.0 13.0 %collective-permute-start = (bf16[32,32,128]{2,1,0:T(8,128)(2,1)S(1)}, bf16[32,32,128]{2,1,0:T(8,128)(2,1)S(1)}, u32[]{:S(2)}, u32[]{:S(2)}) collective-permute-start(bf16[32,32,128]{2,1,0:T(8,128)(2,1)S(1)} %get-tuple-element.421), channel_id=1, source_target_pairs={{0,16},{16,32},{32,48},{48,64},{64,80},{80,96},{96,112},{112,128},... | collective-permute-start | bytes 786440 | tf_op jit(solution)/shard_map/while/body/eval_jaxpr/ppermute | solution.py:12
  610.7 14.5 %all-to-all-start = ((bf16[16,2,32,128]{3,2,1,0:T(8,128)(2,1)}), bf16[16,2,32,128]{3,2,1,0:T(8,128)(2,1)S(1)}, u32[]{:S(2)}, u32[]{:S(2)}) async-start(bf16[16,2,32,128]{3,2,1,0:T(8,128)(2,1)} %broadcast_select_fusion.3), calls=%async_computation | async-start | bytes 524288 | tf_op jit(solution)/shard_map/while/body/eval_jaxpr/all_to_all | solution.py:78
  629.1 13.0 %collective-permute-start = (bf16[32,32,128]{2,1,0:T(8,128)(2,1)S(1)}, bf16[32,32,128]{2,1,0:T(8,128)(2,1)S(1)}, u32[]{:S(2)}, u32[]{:S(2)}) collective-permute-start(bf16[32,32,128]{2,1,0:T(8,128)(2,1)S(1)} %get-tuple-element.421), channel_id=1, source_target_pairs={{0,16},{16,32},{32,48},{48,64},{64,80},{80,96},{96,112},{112,128},... | collective-permute-start | bytes 786440 | tf_op jit(solution)/shard_map/while/body/eval_jaxpr/ppermute | solution.py:12
  644.7 14.5 %all-to-all-start = ((bf16[16,2,32,128]{3,2,1,0:T(8,128)(2,1)}), bf16[16,2,32,128]{3,2,1,0:T(8,128)(2,1)S(1)}, u32[]{:S(2)}, u32[]{:S(2)}) async-start(bf16[16,2,32,128]{3,2,1,0:T(8,128)(2,1)} %broadcast_select_fusion.3), calls=%async_computation | async-start | bytes 524288 | tf_op jit(solution)/shard_map/while/body/eval_jaxpr/all_to_all | solution.py:78
  663.1 13.0 %collective-permute-start = (bf16[32,32,128]{2,1,0:T(8,128)(2,1)S(1)}, bf16[32,32,128]{2,1,0:T(8,128)(2,1)S(1)}, u32[]{:S(2)}, u32[]{:S(2)}) collective-permute-start(bf16[32,32,128]{2,1,0:T(8,128)(2,1)S(1)} %get-tuple-element.421), channel_id=1, source_target_pairs={{0,16},{16,32},{32,48},{48,64},{64,80},{80,96},{96,112},{112,128},... | collective-permute-start | bytes 786440 | tf_op jit(solution)/shard_map/while/body/eval_jaxpr/ppermute | solution.py:12
  678.7 14.5 %all-to-all-start = ((bf16[16,2,32,128]{3,2,1,0:T(8,128)(2,1)}), bf16[16,2,32,128]{3,2,1,0:T(8,128)(2,1)S(1)}, u32[]{:S(2)}, u32[]{:S(2)}) async-start(bf16[16,2,32,128]{3,2,1,0:T(8,128)(2,1)} %broadcast_select_fusion.3), calls=%async_computation | async-start | bytes 524288 | tf_op jit(solution)/shard_map/while/body/eval_jaxpr/all_to_all | solution.py:78
  697.1 13.0 %collective-permute-start = (bf16[32,32,128]{2,1,0:T(8,128)(2,1)S(1)}, bf16[32,32,128]{2,1,0:T(8,128)(2,1)S(1)}, u32[]{:S(2)}, u32[]{:S(2)}) collective-permute-start(bf16[32,32,128]{2,1,0:T(8,128)(2,1)S(1)} %get-tuple-element.421), channel_id=1, source_target_pairs={{0,16},{16,32},{32,48},{48,64},{64,80},{80,96},{96,112},{112,128},... | collective-permute-start | bytes 786440 | tf_op jit(solution)/shard_map/while/body/eval_jaxpr/ppermute | solution.py:12
  710.1 11.0 %copy-start.1 = (s32[4]{0:T(128)S(1)}, s32[4]{0:T(128)}, u32[]{:S(2)}) copy-start(s32[4]{0:T(128)} %param.11) | copy-start | bytes 52
  713.0 22.1 %all-to-all-start.1 = ((bf16[4,16,2,4096]{3,2,0,1:T(2,128)(2,1)}), bf16[4,16,2,4096]{3,2,0,1:T(2,128)(2,1)S(1)}, u32[]{:S(2)}, u32[]{:S(2)}) async-start(bf16[4,16,2,4096]{3,2,0,1:T(2,128)(2,1)} %copy.26), calls=%async_computation.1 | async-start | bytes 2097152 | tf_op jit(solution)/shard_map/all_to_all | solution.py:107
Sparse Core Ops, SparseCore 0:
  9.8 48.4 all-gather.2
where the time goes:
time: 750 us; the launch traced here: 743 us
  waiting for transfers between devices  362 us (48%)
  starting transfers between devices  200 us (27%)
  local copies, waits for them, and re-layouts  59.3 us (8%)
  matrix products  58.6 us (8%)
  other arithmetic  25.8 us (3%)
  blocking collectives  20.7 us (3%)
  between operations  13.5 us (2%)
    all_to_all x19, waiting for transfers between devices, apply_layer(): lax.all_to_all(payload, 'col', split_axis=0, concat_axis=0, tiled=True)  206 us
    ppermute x19, waiting for transfers between devices, from_behind(): return lax.ppermute(x, axis, pairs)  124 us
    ppermute x19, starting transfers between devices, from_behind(): return lax.ppermute(x, axis, pairs)  122 us
    all_to_all x19, starting transfers between devices, apply_layer(): lax.all_to_all(payload, 'col', split_axis=0, concat_axis=0, tiled=True)  70.7 us
    dot_general x19, matrix products, combine(): jnp.einsum('ckrb,ckbo->cro', picked, local_w, preferred_element_type=jnp....  58.6 us
    all_gather x1, blocking collectives, body(): pattern_table = lax.all_gather(sources[0], 'col', axis=0, tiled=True)  20.7 us
    all_gather x1, waiting for transfers between devices, body(): all_inputs = lax.all_gather(features, 'section', axis=1, tiled=True)  19.3 us
    dynamic_slice x19, local copies, waits for them, and re-layouts, tick(): lax.dynamic_index_in_dim(blocks_in, jnp.minimum(tick_idx, piece_total - 1...  18.6 us
  transfers between devices with their start and end apart: 40, of which 40 were waited for; matrix products, arithmetic and copies ran while one was open for 2% of the time, Pallas kernels for 0%

commit v1 on v0

--- a/solution.py
+++ b/solution.py
@@ -1,9 +1,14 @@
+import functools
+
 import jax
 import jax.numpy as jnp
 from jax import lax
+from jax.experimental import pallas as pl
+from jax.experimental.pallas import tpu as pltpu
 from jax.sharding import PartitionSpec as P
 
 CAP = 2
+MESH_ID = pl.DeviceIdType.MESH
 
 
 def from_behind(x, axis, by):
@@ -27,6 +32,54 @@
     return (positions, present)
 
 
+def exchange_kernel(sections, owners, send_ref, recv_ref, send_sem, recv_sem):
+    me_s = lax.axis_index("section")
+    me_c = lax.axis_index("col")
+    nxt = lax.rem(me_s + 1, sections)
+    prv = lax.rem(me_s + sections - 1, sections)
+    barrier = pltpu.get_barrier_semaphore()
+    for d in range(owners):
+        pl.semaphore_signal(barrier, inc=1, device_id=(prv, d), device_id_type=MESH_ID)
+    pl.semaphore_wait(barrier, owners)
+    copies = []
+    for d in range(owners):
+        copy = pltpu.make_async_remote_copy(
+            src_ref=send_ref.at[d],
+            dst_ref=recv_ref.at[me_c],
+            send_sem=send_sem.at[d],
+            recv_sem=recv_sem.at[me_c],
+            device_id=(nxt, d),
+            device_id_type=MESH_ID,
+        )
+        copy.start()
+        copies.append(copy)
+    for d in range(owners):
+        copies[d].wait_send()
+    for e in range(owners):
+        pltpu.make_async_remote_copy(
+            src_ref=send_ref.at[e],
+            dst_ref=recv_ref.at[e],
+            send_sem=send_sem.at[e],
+            recv_sem=recv_sem.at[e],
+            device_id=(prv, e),
+            device_id_type=MESH_ID,
+        ).wait_recv()
+
+
+def exchange(send_buf, sections, owners):
+    return pl.pallas_call(
+        functools.partial(exchange_kernel, sections, owners),
+        out_shape=jax.ShapeDtypeStruct(send_buf.shape, send_buf.dtype),
+        in_specs=[pl.BlockSpec(memory_space=pltpu.VMEM)],
+        out_specs=pl.BlockSpec(memory_space=pltpu.VMEM),
+        scratch_shapes=[
+            pltpu.SemaphoreType.DMA((owners,)),
+            pltpu.SemaphoreType.DMA((owners,)),
+        ],
+        compiler_params=pltpu.CompilerParams(collective_id=0, has_side_effects=True),
+    )(send_buf)
+
+
 def body(features, weights, sources, bias, batch_rows):
     sections = lax.axis_size("section")
     owners = lax.axis_size("col")
@@ -40,7 +93,9 @@
     local_bias = bias[0].reshape(blocks_own, 1, block_size)
     pattern_table = lax.all_gather(sources[0], "col", axis=0, tiled=True)
     positions, present = request_lists(pattern_table, owners, blocks_own, CAP)
-    outgoing = lax.dynamic_index_in_dim(positions, col_idx, 1, keepdims=False).reshape(owners * CAP)
+    outgoing = lax.dynamic_index_in_dim(positions, col_idx, 1, keepdims=False)
+    outgoing_next = from_behind(outgoing, "section", -1).reshape(owners * CAP)
+    outgoing = outgoing.reshape(owners * CAP)
     incoming = lax.dynamic_index_in_dim(positions, col_idx, 0, keepdims=False)
     incoming_ok = lax.dynamic_index_in_dim(present, col_idx, 0, keepdims=False)
     global_ids = incoming + blocks_own * jnp.arange(owners, dtype=jnp.int32)[:, None]
@@ -53,53 +108,48 @@
     all_inputs = lax.all_gather(features, "section", axis=1, tiled=True)
     batches = all_inputs.shape[0]
     row_total = all_inputs.shape[1]
-    pieces = 1
-    part_rows = row_total // pieces
-    piece_total = batches * pieces
+    piece_total = batches
     tick_total = piece_total + sections - 1
-    blocks_in = all_inputs.reshape(batches, pieces, part_rows, blocks_own, block_size)
-    blocks_in = blocks_in.transpose(0, 1, 3, 2, 4).reshape(
-        piece_total, blocks_own, part_rows, block_size
+    blocks_in = all_inputs.reshape(batches, row_total, blocks_own, block_size)
+    blocks_in = blocks_in.transpose(0, 2, 1, 3)
+    first_payload = jnp.take(blocks_in, outgoing, axis=1).reshape(
+        batches, owners, CAP, row_total, block_size
     )
+    first_recv = lax.all_to_all(first_payload, "col", split_axis=1, concat_axis=1, tiled=True)
 
     def combine(received):
-        rows_here = received.shape[2]
-        flat_recv = received.reshape(owners * CAP, rows_here, block_size)
+        flat_recv = received.reshape(owners * CAP, row_total, block_size)
         picked = jnp.take(flat_recv, slot_of, axis=0).reshape(
-            blocks_own, nonzero_count, rows_here, block_size
+            blocks_own, nonzero_count, row_total, block_size
         )
         preact = jnp.einsum("ckrb,ckbo->cro", picked, local_w, preferred_element_type=jnp.float32)
         return jnp.clip(preact + local_bias, 0.0, 32.0).astype(jnp.bfloat16)
 
-    def apply_layer(carried):
-        payload = jnp.take(carried, outgoing, axis=0).reshape(
-            owners, CAP, carried.shape[1], block_size
-        )
-        return combine(lax.all_to_all(payload, "col", split_axis=0, concat_axis=0, tiled=True))
-
     def tick(tick_idx, carry):
         carried, finished = carry
         entering = lax.dynamic_index_in_dim(
-            blocks_in, jnp.minimum(tick_idx, piece_total - 1), 0, keepdims=False
+            first_recv, jnp.minimum(tick_idx, piece_total - 1), 0, keepdims=False
         )
         current = jnp.where(section_idx == 0, entering, carried)
-        layer_out = apply_layer(current)
+        layer_out = combine(current)
         slot_idx = jnp.clip(tick_idx - sections + 1, 0, piece_total - 1)
         storing = (section_idx == sections - 1) & (tick_idx >= sections - 1)
         existing = lax.dynamic_index_in_dim(finished, slot_idx, 0, keepdims=False)
         finished = lax.dynamic_update_index_in_dim(
             finished, jnp.where(storing, layer_out, existing), slot_idx, 0
         )
-        passed = from_behind(layer_out, "section", 1)
+        send_buf = jnp.take(layer_out, outgoing_next, axis=0).reshape(
+            owners, CAP, row_total, block_size
+        )
+        passed = exchange(send_buf, sections, owners)
         return (passed, finished)
 
     initial = (
-        jnp.zeros((blocks_own, part_rows, block_size), jnp.bfloat16),
-        jnp.zeros((piece_total, blocks_own, part_rows, block_size), jnp.bfloat16),
+        jnp.zeros((owners, CAP, row_total, block_size), jnp.bfloat16),
+        jnp.zeros((piece_total, blocks_own, row_total, block_size), jnp.bfloat16),
     )
     carried, finished = lax.fori_loop(0, tick_total, tick, initial)
-    completed = finished.reshape(batches, pieces, blocks_own, part_rows, block_size)
-    completed = completed.transpose(0, 1, 3, 2, 4).reshape(
+    completed = finished.transpose(0, 2, 1, 3).reshape(
         batches, row_total, blocks_own * block_size
     )
     own_rows = row_total // sections

time: 750 us -> 596 us (0.79)
  Pallas kernels: 0 us -> 312 us
  waiting for transfers between devices: 362 us -> 57.9 us
  starting transfers between devices: 200 us -> 40.5 us
  local copies, waits for them, and re-layouts: 59.3 us -> 41.1 us
  other arithmetic: 25.8 us -> 43.9 us
    pallas_call x0 -> x19, Pallas kernels: none -> 312 us  [exchange(): pl.pallas_call(functools.partial(exchange_kernel, sections, owners), out_...]
    all_to_all x19 -> x1, waiting for transfers between devices: 206 us -> 19 us  [body(): lax.all_to_all(first_payload, 'col', split_axis=1, concat_axis=1, tiled=T...]
    ppermute x19 -> x1, waiting for transfers between devices: 124 us -> 3.29 us  [from_behind(): return lax.ppermute(x, axis, pairs)]
    ppermute x19 -> x1, starting transfers between devices: 122 us -> 2.74 us  [from_behind(): return lax.ppermute(x, axis, pairs)]
    all_to_all x19 -> x1, starting transfers between devices: 70.7 us -> 7.17 us  [body(): lax.all_to_all(first_payload, 'col', split_axis=1, concat_axis=1, tiled=T...]
    all_to_all x1, starting transfers between devices: 8.1 us -> 30.6 us  [body(): lax.all_to_all(outgoing_rows, 'section', split_axis=1, concat_axis=1, til...]
    dynamic_slice x20 -> x2, local copies, waits for them, and re-layouts: 19 us -> 0.52 us  [body(): outgoing = lax.dynamic_index_in_dim(positions, col_idx, 1, keepdims=False)]
    select_n x19, other arithmetic: 2.04 us -> 18.8 us  [tick(): current = jnp.where(section_idx == 0, entering, carried)]
  transfers between devices with their start and end apart: 40 -> 4, of which waited for: 40 -> 4; matrix products, arithmetic and copies ran while one was open for 2% -> 2% of each run, Pallas kernels for 0% -> 0%
where the time goes in v1:
time: 596 us; the launch traced here: 590 us
  Pallas kernels  312 us (52%)
  matrix products  58.6 us (10%)
  waiting for transfers between devices  57.9 us (10%)
  other arithmetic  43.9 us (7%)
  local copies, waits for them, and re-layouts  41.1 us (7%)
  starting transfers between devices  40.5 us (7%)
  blocking collectives  20.7 us (3%)
  between operations  13.6 us (2%)
    pallas_call x19, Pallas kernels, exchange(): pl.pallas_call(functools.partial(exchange_kernel, sections, owners), out_...  312 us
    dot_general x19, matrix products, combine(): jnp.einsum('ckrb,ckbo->cro', picked, local_w, preferred_element_type=jnp....  58.6 us
    all_to_all x1, starting transfers between devices, body(): lax.all_to_all(outgoing_rows, 'section', split_axis=1, concat_axis=1, til...  30.6 us
    all_gather x1, waiting for transfers between devices, body(): all_inputs = lax.all_gather(features, 'section', axis=1, tiled=True)  21.4 us
    all_gather x1, blocking collectives, body(): pattern_table = lax.all_gather(sources[0], 'col', axis=0, tiled=True)  20.7 us
    all_to_all x1, waiting for transfers between devices, body(): lax.all_to_all(first_payload, 'col', split_axis=1, concat_axis=1, tiled=T...  19 us
    select_n x19, other arithmetic, tick(): current = jnp.where(section_idx == 0, entering, carried)  18.8 us
    select_n x38, other arithmetic, tick(): jnp.take(layer_out, outgoing_next, axis=0)  15.9 us
  transfers between devices with their start and end apart: 4, of which 4 were waited for; matrix products, arithmetic and copies ran while one was open for 2% of the time, Pallas kernels for 0%

profile of v1, /device:TPU:28, one launch (start us, length us, event | category | flops | bytes accessed | tf_op | source)
XLA Modules:
  0.0 590.1 jit_solution(4069360348568244830)
XLA Ops:
  8.9 20.7 %all-gather = s32[1,512,4]{2,0,1:T(1,128)S(1)} all-gather(s32[1,32,4]{2,0,1:T(1,128)S(1)} %copy.37), channel_id=2, replica_groups=mesh['section'=16,'col'=16] {'col'}, dimensions={1}, use_global_device_ids=true | all-gather | bytes 8704 | tf_op jit(solution)/shard_map/all_gather | solution.py:94
  32.5 3.0 reduce_window_sum.11
  36.9 21.4 %all-gather.3.cloned.1.call-done = bf16[4,32,4096]{2,0,1:T(4,128)(2,1)} async-done(((bf16[4,2,4096]{2,0,1:T(4,128)(2,1)}), bf16[4,32,4096]{2,0,1:T(4,128)(2,1)}) %all-gather.3.cloned.1.call-update) | async-done | bytes 1048592 | tf_op jit(solution)/shard_map/all_gather | solution.py:108
  63.1 7.2 %all-to-all-start = ((bf16[4,16,2,32,128]{4,3,2,0,1:T(8,128)(2,1)}), bf16[4,16,2,32,128]{4,3,2,0,1:T(8,128)(2,1)}, u32[]{:S(2)}, u32[]{:S(2)}) async-start(bf16[4,16,2,32,128]{4,3,2,0,1:T(8,128)(2,1)} %copy_select_fusion), calls=%async_computation | async-start | bytes 2097152 | tf_op jit(solution)/shard_map/all_to_all | solution.py:118
  70.3 2.7 collective-permute-start
  74.6 3.3 collective-permute-done
  78.0 19.0 %all-to-all-done = bf16[4,16,2,32,128]{4,3,2,0,1:T(8,128)(2,1)} async-done(((bf16[4,16,2,32,128]{4,3,2,0,1:T(8,128)(2,1)}), bf16[4,16,2,32,128]{4,3,2,0,1:T(8,128)(2,1)}, u32[]{:S(2)}, u32[]{:S(2)}) %all-to-all-start) | async-done | bytes 1048608 | tf_op jit(solution)/shard_map/all_to_all | solution.py:118
  97.2 437.5 %while.19 = (s32[]{:T(128)}, bf16[16,2,32,128]{3,2,1,0:T(8,128)(2,1)S(1)}, bf16[4,32,32,128]{3,2,1,0:T(8,128)(2,1)S(1)}, s32[32]{0:T(128)S(1)}, s32[128]{0:T(128...) while((s32[]{:T(128)}, ...), condition=%wide.region_6.7_spmd, body=%wide.region_5.6_spmd.sunk | while | flops 135531952 | bytes 10519361 | solution.py:151
  99.2 3.1 bitcast_dynamic-update-slice_fusion.2
  103.8 12.6 %eval_jaxpr.11 = bf16[16,2,32,128]{3,2,1,0:T(8,128)(2,1)S(1)} custom-call(bf16[16,2,32,128]{3,2,1,0:T(8,128)(2,1)} %broadcast_select_fusion.3.send_ref), custom_call_target="tpu_custom_call" | custom-call | tf_op jit(solution)/shard_map/while/body/eval_jaxpr/pallas_call | solution.py:70
  118.4 3.1 bitcast_dynamic-update-slice_fusion.2
  123.1 14.0 %eval_jaxpr.11 = bf16[16,2,32,128]{3,2,1,0:T(8,128)(2,1)S(1)} custom-call(bf16[16,2,32,128]{3,2,1,0:T(8,128)(2,1)} %broadcast_select_fusion.3.send_ref), custom_call_target="tpu_custom_call" | custom-call | tf_op jit(solution)/shard_map/while/body/eval_jaxpr/pallas_call | solution.py:70
  139.0 3.1 bitcast_dynamic-update-slice_fusion.2
  143.7 16.3 %eval_jaxpr.11 = bf16[16,2,32,128]{3,2,1,0:T(8,128)(2,1)S(1)} custom-call(bf16[16,2,32,128]{3,2,1,0:T(8,128)(2,1)} %broadcast_select_fusion.3.send_ref), custom_call_target="tpu_custom_call" | custom-call | tf_op jit(solution)/shard_map/while/body/eval_jaxpr/pallas_call | solution.py:70
  162.0 3.1 bitcast_dynamic-update-slice_fusion.2
  166.6 19.0 %eval_jaxpr.11 = bf16[16,2,32,128]{3,2,1,0:T(8,128)(2,1)S(1)} custom-call(bf16[16,2,32,128]{3,2,1,0:T(8,128)(2,1)} %broadcast_select_fusion.3.send_ref), custom_call_target="tpu_custom_call" | custom-call | tf_op jit(solution)/shard_map/while/body/eval_jaxpr/pallas_call | solution.py:70
  187.6 3.1 bitcast_dynamic-update-slice_fusion.2
  192.3 16.6 %eval_jaxpr.11 = bf16[16,2,32,128]{3,2,1,0:T(8,128)(2,1)S(1)} custom-call(bf16[16,2,32,128]{3,2,1,0:T(8,128)(2,1)} %broadcast_select_fusion.3.send_ref), custom_call_target="tpu_custom_call" | custom-call | tf_op jit(solution)/shard_map/while/body/eval_jaxpr/pallas_call | solution.py:70
  210.9 3.1 bitcast_dynamic-update-slice_fusion.2
  215.5 16.6 %eval_jaxpr.11 = bf16[16,2,32,128]{3,2,1,0:T(8,128)(2,1)S(1)} custom-call(bf16[16,2,32,128]{3,2,1,0:T(8,128)(2,1)} %broadcast_select_fusion.3.send_ref), custom_call_target="tpu_custom_call" | custom-call | tf_op jit(solution)/shard_map/while/body/eval_jaxpr/pallas_call | solution.py:70
  234.1 3.1 bitcast_dynamic-update-slice_fusion.2
  238.8 16.6 %eval_jaxpr.11 = bf16[16,2,32,128]{3,2,1,0:T(8,128)(2,1)S(1)} custom-call(bf16[16,2,32,128]{3,2,1,0:T(8,128)(2,1)} %broadcast_select_fusion.3.send_ref), custom_call_target="tpu_custom_call" | custom-call | tf_op jit(solution)/shard_map/while/body/eval_jaxpr/pallas_call | solution.py:70
  257.4 3.1 bitcast_dynamic-update-slice_fusion.2
  262.0 16.7 %eval_jaxpr.11 = bf16[16,2,32,128]{3,2,1,0:T(8,128)(2,1)S(1)} custom-call(bf16[16,2,32,128]{3,2,1,0:T(8,128)(2,1)} %broadcast_select_fusion.3.send_ref), custom_call_target="tpu_custom_call" | custom-call | tf_op jit(solution)/shard_map/while/body/eval_jaxpr/pallas_call | solution.py:70
  280.7 3.1 bitcast_dynamic-update-slice_fusion.2
  285.3 16.6 %eval_jaxpr.11 = bf16[16,2,32,128]{3,2,1,0:T(8,128)(2,1)S(1)} custom-call(bf16[16,2,32,128]{3,2,1,0:T(8,128)(2,1)} %broadcast_select_fusion.3.send_ref), custom_call_target="tpu_custom_call" | custom-call | tf_op jit(solution)/shard_map/while/body/eval_jaxpr/pallas_call | solution.py:70
  303.9 3.1 bitcast_dynamic-update-slice_fusion.2
  308.6 16.7 %eval_jaxpr.11 = bf16[16,2,32,128]{3,2,1,0:T(8,128)(2,1)S(1)} custom-call(bf16[16,2,32,128]{3,2,1,0:T(8,128)(2,1)} %broadcast_select_fusion.3.send_ref), custom_call_target="tpu_custom_call" | custom-call | tf_op jit(solution)/shard_map/while/body/eval_jaxpr/pallas_call | solution.py:70
  327.2 3.1 bitcast_dynamic-update-slice_fusion.2
  331.9 16.7 %eval_jaxpr.11 = bf16[16,2,32,128]{3,2,1,0:T(8,128)(2,1)S(1)} custom-call(bf16[16,2,32,128]{3,2,1,0:T(8,128)(2,1)} %broadcast_select_fusion.3.send_ref), custom_call_target="tpu_custom_call" | custom-call | tf_op jit(solution)/shard_map/while/body/eval_jaxpr/pallas_call | solution.py:70
  350.5 3.1 bitcast_dynamic-update-slice_fusion.2
  355.2 16.7 %eval_jaxpr.11 = bf16[16,2,32,128]{3,2,1,0:T(8,128)(2,1)S(1)} custom-call(bf16[16,2,32,128]{3,2,1,0:T(8,128)(2,1)} %broadcast_select_fusion.3.send_ref), custom_call_target="tpu_custom_call" | custom-call | tf_op jit(solution)/shard_map/while/body/eval_jaxpr/pallas_call | solution.py:70
  373.8 3.1 bitcast_dynamic-update-slice_fusion.2
  378.5 16.6 %eval_jaxpr.11 = bf16[16,2,32,128]{3,2,1,0:T(8,128)(2,1)S(1)} custom-call(bf16[16,2,32,128]{3,2,1,0:T(8,128)(2,1)} %broadcast_select_fusion.3.send_ref), custom_call_target="tpu_custom_call" | custom-call | tf_op jit(solution)/shard_map/while/body/eval_jaxpr/pallas_call | solution.py:70
  397.1 3.1 bitcast_dynamic-update-slice_fusion.2
  401.8 16.6 %eval_jaxpr.11 = bf16[16,2,32,128]{3,2,1,0:T(8,128)(2,1)S(1)} custom-call(bf16[16,2,32,128]{3,2,1,0:T(8,128)(2,1)} %broadcast_select_fusion.3.send_ref), custom_call_target="tpu_custom_call" | custom-call | tf_op jit(solution)/shard_map/while/body/eval_jaxpr/pallas_call | solution.py:70
  420.4 3.1 bitcast_dynamic-update-slice_fusion.2
  425.0 16.6 %eval_jaxpr.11 = bf16[16,2,32,128]{3,2,1,0:T(8,128)(2,1)S(1)} custom-call(bf16[16,2,32,128]{3,2,1,0:T(8,128)(2,1)} %broadcast_select_fusion.3.send_ref), custom_call_target="tpu_custom_call" | custom-call | tf_op jit(solution)/shard_map/while/body/eval_jaxpr/pallas_call | solution.py:70
  443.6 3.1 bitcast_dynamic-update-slice_fusion.2
  448.3 16.6 %eval_jaxpr.11 = bf16[16,2,32,128]{3,2,1,0:T(8,128)(2,1)S(1)} custom-call(bf16[16,2,32,128]{3,2,1,0:T(8,128)(2,1)} %broadcast_select_fusion.3.send_ref), custom_call_target="tpu_custom_call" | custom-call | tf_op jit(solution)/shard_map/while/body/eval_jaxpr/pallas_call | solution.py:70
  466.9 3.1 bitcast_dynamic-update-slice_fusion.2
  471.6 16.6 %eval_jaxpr.11 = bf16[16,2,32,128]{3,2,1,0:T(8,128)(2,1)S(1)} custom-call(bf16[16,2,32,128]{3,2,1,0:T(8,128)(2,1)} %broadcast_select_fusion.3.send_ref), custom_call_target="tpu_custom_call" | custom-call | tf_op jit(solution)/shard_map/while/body/eval_jaxpr/pallas_call | solution.py:70
  490.2 3.1 bitcast_dynamic-update-slice_fusion.2
  494.8 16.6 %eval_jaxpr.11 = bf16[16,2,32,128]{3,2,1,0:T(8,128)(2,1)S(1)} custom-call(bf16[16,2,32,128]{3,2,1,0:T(8,128)(2,1)} %broadcast_select_fusion.3.send_ref), custom_call_target="tpu_custom_call" | custom-call | tf_op jit(solution)/shard_map/while/body/eval_jaxpr/pallas_call | solution.py:70
  513.4 3.1 bitcast_dynamic-update-slice_fusion.2
  518.1 16.6 %eval_jaxpr.11 = bf16[16,2,32,128]{3,2,1,0:T(8,128)(2,1)S(1)} custom-call(bf16[16,2,32,128]{3,2,1,0:T(8,128)(2,1)} %broadcast_select_fusion.3.send_ref), custom_call_target="tpu_custom_call" | custom-call | tf_op jit(solution)/shard_map/while/body/eval_jaxpr/pallas_call | solution.py:70
  537.6 30.6 %all-to-all-start.1 = ((bf16[4,16,2,4096]{3,2,0,1:T(2,128)(2,1)}), bf16[4,16,2,4096]{3,2,0,1:T(2,128)(2,1)S(1)}, u32[]{:S(2)}, u32[]{:S(2)}) async-start(bf16[4,16,2,4096]{3,2,0,1:T(2,128)(2,1)} %copy.50), calls=%async_computation.1 | async-start | bytes 2097152 | tf_op jit(solution)/shard_map/all_to_all | solution.py:157
  568.3 14.3 %all-to-all-done.1 = bf16[4,16,2,4096]{3,2,0,1:T(2,128)(2,1)S(1)} async-done(((bf16[4,16,2,4096]{3,2,0,1:T(2,128)(2,1)}), bf16[4,16,2,4096]{3,2,0,1:T(2,128)(2,1)S(1)}, u32[]{:S(2)}, u32[]{:S(2)}) %all-to-all-start.1) | async-done | bytes 1048608 | tf_op jit(solution)/shard_map/all_to_all | solution.py:157
  (300 shorter events, 82.0 us)
Async XLA Ops:
  6.5 51.7 %all-gather.3.cloned.1.call-start = ((), (), s32[]{:S(2)}) async-start(), calls=%async_computation.2 | async-start | bytes 1114112 | tf_op jit(solution)/shard_map/all_gather | solution.py:108
  60.4 12.6 %copy-start.1 = (s32[1,32,4]{1,2,0:T(4,128)S(1)}, s32[1,32,4]{1,2,0:T(4,128)}, u32[]{:S(2)}) copy-start(s32[1,32,4]{1,2,0:T(4,128)} %param.9) | copy-start | bytes 1540
  61.1 36.1 %copy-start = (f32[1,4096]{1,0:T(1,128)S(1)}, f32[1,4096]{1,0:T(1,128)}, u32[]{:S(2)}) copy-start(f32[1,4096]{1,0:T(1,128)} %param.10) | copy-start | bytes 49156
  63.1 33.9 %all-to-all-start = ((bf16[4,16,2,32,128]{4,3,2,0,1:T(8,128)(2,1)}), bf16[4,16,2,32,128]{4,3,2,0,1:T(8,128)(2,1)}, u32[]{:S(2)}, u32[]{:S(2)}) async-start(bf16[4,16,2,32,128]{4,3,2,0,1:T(8,128)(2,1)} %copy_select_fusion), calls=%async_computation | async-start | bytes 2097152 | tf_op jit(solution)/shard_map/all_to_all | solution.py:118
  70.3 7.6 %collective-permute-start = (s32[16,2]{0,1:T(2,128)S(1)}, s32[16,2]{0,1:T(2,128)S(1)}, u32[]{:S(2)}, u32[]{:S(2)}) collective-permute-start(s32[16,2]{0,1:T(2,128)S(1)} %bitcast.87), channel_id=1, source_target_pairs={{16,0},{32,16},{48,32},{64,48},{80,64},{96,80},{112,96},{128,112},... | collective-permute-start | bytes 392 | tf_op jit(solution)/shard_map/ppermute | solution.py:17
  534.7 33.5 %copy-start.2 = (s32[4]{0:T(128)S(1)}, s32[4]{0:T(128)}, u32[]{:S(2)}) copy-start(s32[4]{0:T(128)} %param.11) | copy-start | bytes 52
  537.6 44.9 %all-to-all-start.1 = ((bf16[4,16,2,4096]{3,2,0,1:T(2,128)(2,1)}), bf16[4,16,2,4096]{3,2,0,1:T(2,128)(2,1)S(1)}, u32[]{:S(2)}, u32[]{:S(2)}) async-start(bf16[4,16,2,4096]{3,2,0,1:T(2,128)(2,1)} %copy.50), calls=%async_computation.1 | async-start | bytes 2097152 | tf_op jit(solution)/shard_map/all_to_all | solution.py:157
Sparse Core Ops, SparseCore 0:
  9.8 48.4 all-gather.2

commit v2 on v0

v2 whole, which is shorter than its diff:
```python
import functools

import jax
import jax.numpy as jnp
from jax import lax
from jax.experimental import pallas as pl
from jax.experimental.pallas import tpu as pltpu
from jax.sharding import PartitionSpec as P

CAP = 2
MESH_ID = pl.DeviceIdType.MESH


def from_behind(x, axis, by):
    size = lax.axis_size(axis)
    pairs = [(i, i + by) for i in range(size) if 0 <= i + by < size]
    return lax.ppermute(x, axis, pairs)


def request_lists(pattern_table, owners, blocks_own, slot_total):
    dest_entries = pattern_table.reshape(owners, -1)
    block_total = owners * blocks_own
    catalog = jnp.arange(block_total, dtype=jnp.int32)
    wanted = jnp.any(dest_entries[:, :, None] == catalog[None, None, :], axis=1)
    wanted = wanted.reshape(owners, owners, blocks_own)
    block_ranks = jnp.cumsum(wanted.astype(jnp.int32), axis=2) - 1
    slot_ids = jnp.arange(slot_total, dtype=jnp.int32)
    chosen = wanted[:, :, None, :] & (block_ranks[:, :, None, :] == slot_ids[None, None, :, None])
    local_ids = jnp.arange(blocks_own, dtype=jnp.int32)
    positions = jnp.sum(chosen.astype(jnp.int32) * local_ids[None, None, None, :], axis=3)
    present = jnp.any(chosen, axis=3)
    return (positions, present)


def pipeline_kernel(
    sections, owners, batches, first_ref, w_ref, b_ref, slot_ref, next_ref,
    out_ref, *scratch,
):
    recv = scratch[:batches]
    send = scratch[batches:2 * batches]
    send_sem, recv_sem, local_sem = scratch[2 * batches:]
    me_s = lax.axis_index("section")
    me_c = lax.axis_index("col")
    blocks_own = w_ref.shape[0]
    nonzero_count = w_ref.shape[1]
    barrier = pltpu.get_barrier_semaphore()

    @pl.when(me_s > 0)
    def _():
        for d in range(owners):
            pl.semaphore_signal(barrier, inc=1, device_id=(me_s - 1, d), device_id_type=MESH_ID)

    @pl.when(me_s < sections - 1)
    def _():
        for d in range(owners):
            pl.semaphore_signal(barrier, inc=1, device_id=(me_s + 1, d), device_id_type=MESH_ID)

    peers = owners * (
        (me_s > 0).astype(jnp.int32) + (me_s < sections - 1).astype(jnp.int32)
    )
    pl.semaphore_wait(barrier, peers)

    @pl.when(me_s == 0)
    def _():
        for m in range(batches):
            first = pltpu.make_async_copy(first_ref.at[m], recv[m], local_sem)
            first.start()
            first.wait()

    def outgoing_copy(m, d):
        return pltpu.make_async_remote_copy(
            src_ref=send[m].at[pl.ds(d * CAP, CAP)],
            dst_ref=recv[m].at[pl.ds(me_c * CAP, CAP)],
            send_sem=send_sem.at[m, d],
            recv_sem=recv_sem.at[m, me_c],
            device_id=(me_s + 1, d),
            device_id_type=MESH_ID,
        )

    for m in range(batches):

        @pl.when(me_s > 0)
        def _():
            for e in range(owners):
                pltpu.make_async_remote_copy(
                    src_ref=send[m].at[pl.ds(e * CAP, CAP)],
                    dst_ref=recv[m].at[pl.ds(e * CAP, CAP)],
                    send_sem=send_sem.at[m, e],
                    recv_sem=recv_sem.at[m, e],
                    device_id=(me_s - 1, e),
                    device_id_type=MESH_ID,
                ).wait_recv()

        def block_step(j, carry):
            acc = None
            for k in range(nonzero_count):
                picked = recv[m][slot_ref[j * nonzero_count + k]]
                term = jnp.dot(picked, w_ref[j, k], preferred_element_type=jnp.float32)
                acc = term if acc is None else acc + term
            out_ref[m, j] = jnp.clip(acc + b_ref[j], 0.0, 32.0).astype(out_ref.dtype)
            return carry

        lax.fori_loop(0, blocks_own, block_step, 0)

        @pl.when(me_s < sections - 1)
        def _():
            def stage(i, carry):
                send[m][i] = out_ref[m, next_ref[i]]
                return carry

            lax.fori_loop(0, owners * CAP, stage, 0)
            for d in range(owners):
                outgoing_copy(m, d).start()

    @pl.when(me_s < sections - 1)
    def _():
        for m in range(batches):
            for d in range(owners):
                outgoing_copy(m, d).wait_send()


def run_pipeline(first_recv, local_w, local_bias, slot_of, outgoing_next, sections, owners):
    batches = first_recv.shape[0]
    blocks_own = local_w.shape[0]
    rows = first_recv.shape[2]
    block_size = local_w.shape[-1]
    vmem = pl.BlockSpec(memory_space=pltpu.VMEM)
    smem = pl.BlockSpec(memory_space=pltpu.SMEM)
    return pl.pallas_call(
        functools.partial(pipeline_kernel, sections, owners, batches),
        out_shape=jax.ShapeDtypeStruct((batches, blocks_own, rows, block_size), jnp.bfloat16),
        in_specs=[vmem, vmem, vmem, smem, smem],
        out_specs=vmem,
        scratch_shapes=[
            *[pltpu.VMEM(first_recv.shape[1:], jnp.bfloat16) for _ in range(2 * batches)],
            pltpu.SemaphoreType.DMA((batches, owners)),
            pltpu.SemaphoreType.DMA((batches, owners)),
            pltpu.SemaphoreType.DMA(()),
        ],
        compiler_params=pltpu.CompilerParams(collective_id=0, has_side_effects=True),
    )(first_recv, local_w, local_bias, slot_of, outgoing_next)


def body(features, weights, sources, bias, batch_rows):
    sections = lax.axis_size("section")
    owners = lax.axis_size("col")
    section_idx = lax.axis_index("section")
    col_idx = lax.axis_index("col")
    local_w = weights[0]
    blocks_own = local_w.shape[0]
    nonzero_count = local_w.shape[1]
    block_size = local_w.shape[2]
    local_src = sources[0].reshape(blocks_own * nonzero_count)
    pattern_table = lax.all_gather(sources[0], "col", axis=0, tiled=True)
    positions, present = request_lists(pattern_table, owners, blocks_own, CAP)
    outgoing = lax.dynamic_index_in_dim(positions, col_idx, 1, keepdims=False)
    outgoing_next = from_behind(outgoing, "section", -1).reshape(owners * CAP)
    outgoing = outgoing.reshape(owners * CAP)
    incoming = lax.dynamic_index_in_dim(positions, col_idx, 0, keepdims=False)
    incoming_ok = lax.dynamic_index_in_dim(present, col_idx, 0, keepdims=False)
    global_ids = incoming + blocks_own * jnp.arange(owners, dtype=jnp.int32)[:, None]
    matches = (local_src[:, None] == global_ids.reshape(-1)[None, :]) & incoming_ok.reshape(-1)[
        None, :
    ]
    slot_of = jnp.sum(
        matches.astype(jnp.int32) * jnp.arange(owners * CAP, dtype=jnp.int32)[None, :], axis=1
    )
    all_inputs = lax.all_gather(features, "section", axis=1, tiled=True)
    batches = all_inputs.shape[0]
    row_total = all_inputs.shape[1]
    blocks_in = all_inputs.reshape(batches, row_total, blocks_own, block_size)
    blocks_in = blocks_in.transpose(0, 2, 1, 3)
    first_payload = jnp.take(blocks_in, outgoing, axis=1).reshape(
        batches, owners, CAP, row_total, block_size
    )
    first_recv = lax.all_to_all(first_payload, "col", split_axis=1, concat_axis=1, tiled=True)

    first_recv = first_recv.reshape(batches, owners * CAP, row_total, block_size)
    finished = run_pipeline(
        first_recv, local_w, bias[0].reshape(blocks_own, 1, block_size), slot_of,
        outgoing_next, sections, owners,
    )
    completed = finished.transpose(0, 2, 1, 3).reshape(
        batches, row_total, blocks_own * block_size
    )
    own_rows = row_total // sections
    outgoing_rows = completed.reshape(batches, sections, own_rows, blocks_own * block_size)
    gathered = lax.all_to_all(outgoing_rows, "section", split_axis=1, concat_axis=1, tiled=True)
    own_result = gathered[:, sections - 1]
    row_ids = section_idx * own_rows + jnp.arange(own_rows, dtype=jnp.int32)
    row_mask = row_ids[None, :] < batch_rows[:, None]
    return jnp.where(row_mask[:, :, None], own_result, jnp.zeros_like(own_result))


def solution(mesh):
    in_specs = (
        P(None, "section", "col"),
        P("section", "col", None, None, None),
        P("section", "col", None),
        P("section", "col"),
        P(),
    )
    out_specs = P(None, "section", "col")
    return jax.shard_map(body, mesh=mesh, in_specs=in_specs, out_specs=out_specs, check_vma=False)
```

time: 750 us -> 391 us (0.52)
  waiting for transfers between devices: 362 us -> 57.5 us
  Pallas kernels: 0 us -> 202 us
  starting transfers between devices: 200 us -> 69.4 us
  matrix products: 58.6 us -> 0 us
  local copies, waits for them, and re-layouts: 59.3 us -> 14 us
  other arithmetic: 25.8 us -> 9.02 us
    pallas_call x0 -> x1, Pallas kernels: none -> 202 us  [run_pipeline(): pl.pallas_call(functools.partial(pipeline_kernel, sections, owners, batch...]
    all_to_all x19 -> x1, waiting for transfers between devices: 206 us -> 18.4 us  [body(): lax.all_to_all(first_payload, 'col', split_axis=1, concat_axis=1, tiled=T...]
    ppermute x19 -> x1, waiting for transfers between devices: 124 us -> 2.78 us  [from_behind(): return lax.ppermute(x, axis, pairs)]
    ppermute x19 -> x1, starting transfers between devices: 122 us -> 2.74 us  [from_behind(): return lax.ppermute(x, axis, pairs)]
    all_to_all x19 -> x1, starting transfers between devices: 70.7 us -> 7.12 us  [body(): lax.all_to_all(first_payload, 'col', split_axis=1, concat_axis=1, tiled=T...]
    dot_general x19 -> x0, matrix products: 58.6 us -> none  [combine(): jnp.einsum('ckrb,ckbo->cro', picked, local_w, preferred_element_type=jnp....]
    all_to_all x1, starting transfers between devices: 8.1 us -> 59.5 us  [body(): lax.all_to_all(outgoing_rows, 'section', split_axis=1, concat_axis=1, til...]
    gather x38 -> x1, local copies, waits for them, and re-layouts: 25.8 us -> 0.75 us  [body(): jnp.take(blocks_in, outgoing, axis=1)]
  transfers between devices with their start and end apart: 40 -> 4, of which waited for: 40 -> 4; matrix products, arithmetic and copies ran while one was open for 2% -> 3% of each run, Pallas kernels for 0% -> 0%
where the time goes in v2:
time: 391 us; the launch traced here: 386 us
  Pallas kernels  202 us (52%)
  starting transfers between devices  69.4 us (18%)
  waiting for transfers between devices  57.5 us (15%)
  blocking collectives  20.7 us (5%)
  local copies, waits for them, and re-layouts  14 us (4%)
  between operations  13.6 us (3%)
  other arithmetic  9.02 us (2%)
    pallas_call x1, Pallas kernels, run_pipeline(): pl.pallas_call(functools.partial(pipeline_kernel, sections, owners, batch...  202 us
    all_to_all x1, starting transfers between devices, body(): lax.all_to_all(outgoing_rows, 'section', split_axis=1, concat_axis=1, til...  59.5 us
    all_gather x1, waiting for transfers between devices, body(): all_inputs = lax.all_gather(features, 'section', axis=1, tiled=True)  21.4 us
    all_gather x1, blocking collectives, body(): pattern_table = lax.all_gather(sources[0], 'col', axis=0, tiled=True)  20.7 us
    all_to_all x1, waiting for transfers between devices, body(): lax.all_to_all(first_payload, 'col', split_axis=1, concat_axis=1, tiled=T...  18.4 us
    all_to_all x1, waiting for transfers between devices, body(): lax.all_to_all(outgoing_rows, 'section', split_axis=1, concat_axis=1, til...  15 us
  transfers between devices with their start and end apart: 4, of which 4 were waited for; matrix products, arithmetic and copies ran while one was open for 3% of the time, Pallas kernels for 0%

profile of v2, /device:TPU:28, one launch (start us, length us, event | category | flops | bytes accessed | tf_op | source)
XLA Modules:
  0.0 386.3 jit_solution(13668521883560830991)
XLA Ops:
  6.5 0.0 all-gather.3.cloned.1.call-start
  6.5 1.5 copy.41
  8.1 0.0 all-gather.3.cloned.1.call-update
  8.1 0.8 copy.38
  8.9 20.7 %all-gather = s32[1,512,4]{2,0,1:T(1,128)S(1)} all-gather(s32[1,32,4]{2,0,1:T(1,128)S(1)} %copy.38), channel_id=2, replica_groups=mesh['section'=16,'col'=16] {'col'}, dimensions={1}, use_global_device_ids=true | all-gather | bytes 8704 | tf_op jit(solution)/shard_map/all_gather | solution.py:154
  29.5 0.6 broadcast.92
  30.1 1.3 reduce.4
  31.4 0.2 eq.43
  31.6 0.8 fusion
  32.4 0.1 and.30
  32.5 3.0 reduce_window_sum.11
  35.5 0.6 select_reduce_fusion
  36.2 0.4 fusion.4
  36.6 0.1 reshape.120
  36.7 0.1 copy.39
  36.8 0.1 copy.40
  36.9 21.4 %all-gather.3.cloned.1.call-done = bf16[4,32,4096]{2,0,1:T(4,128)(2,1)} async-done(((bf16[4,2,4096]{2,0,1:T(4,128)(2,1)}), bf16[4,32,4096]{2,0,1:T(4,128)(2,1)}) %all-gather.3.cloned.1.call-update) | async-done | bytes 1048592 | tf_op jit(solution)/shard_map/all_gather | solution.py:168
  58.3 2.1 reshape.133
  60.4 0.0 copy-start
  60.4 0.7 copy.56
  61.1 0.7 gather_fusion
  61.9 1.2 copy_select_fusion
  63.0 7.1 %all-to-all-start = ((bf16[4,16,2,32,128]{4,3,2,0,1:T(8,128)(2,1)}), bf16[4,16,2,32,128]{4,3,2,0,1:T(8,128)(2,1)S(1)}, u32[]{:S(2)}, u32[]{:S(2)}) async-start(bf16[4,16,2,32,128]{4,3,2,0,1:T(8,128)(2,1)} %copy_select_fusion), calls=%async_computation | async-start | bytes 2097152 | tf_op jit(solution)/shard_map/all_to_all | solution.py:176
  70.2 2.7 collective-permute-start
  72.9 0.1 copy.46
  73.0 0.1 add.66
  73.1 0.1 add.67
  73.2 0.1 eq.50
  73.3 0.7 fusion.2
  74.0 0.1 copy.48
  74.1 0.1 and.34
  74.2 0.1 copy.47
  74.3 0.1 squeeze.19
  74.4 0.6 select_reduce_fusion.1.slot_ref
  75.0 2.8 collective-permute-done
  77.7 0.1 copy.49
  77.8 0.6 reshape.122.next_ref
  78.4 18.4 %all-to-all-done = bf16[4,16,2,32,128]{4,3,2,0,1:T(8,128)(2,1)S(1)} async-done(((bf16[4,16,2,32,128]{4,3,2,0,1:T(8,128)(2,1)}), bf16[4,16,2,32,128]{4,3,2,0,1:T(8,128)(2,1)S(1)}, u32[]{:S(2)}, u32[]{:S(2)}) %all-to-all-start) | async-done | bytes 1048608 | tf_op jit(solution)/shard_map/all_to_all | solution.py:176
  96.8 1.1 copy.45
  97.9 202.1 %shard_map.55 = bf16[4,32,32,128]{3,2,1,0:T(8,128)(2,1)} custom-call(bf16[4,32,32,128]{3,2,1,0:T(8,128)(2,1)} %bitcast.26, bf16[32,4,128,128]{3,2,1,0:T(8,128)(2,1)} %bitcast.25, f32[32,1,128]{2,1,0:T(1,128)} %bitcast.28, s32[128]{0:T(128)} %select_reduce_fusion.1.slot_ref, s32[32]{0:T(128)} %reshape.122.next_ref), custom_call_target="tpu_custom_call" | custom-call | tf_op jit(solution)/shard_map/pallas_call | solution.py:129
  300.0 0.0 copy-start.1
  300.0 1.6 copy.50
  301.6 0.3 reshape_reshape.3
  301.9 2.2 copy.51
  304.1 59.5 %all-to-all-start.1 = ((bf16[4,16,2,4096]{3,2,0,1:T(2,128)(2,1)}), bf16[4,16,2,4096]{3,2,0,1:T(2,128)(2,1)S(1)}, u32[]{:S(2)}, u32[]{:S(2)}) async-start(bf16[4,16,2,4096]{3,2,0,1:T(2,128)(2,1)} %copy.51), calls=%async_computation.1 | async-start | bytes 2097152 | tf_op jit(solution)/shard_map/all_to_all | solution.py:188
  363.6 0.1 broadcast_compare_fusion
  363.7 15.0 %all-to-all-done.1 = bf16[4,16,2,4096]{3,2,0,1:T(2,128)(2,1)S(1)} async-done(((bf16[4,16,2,4096]{3,2,0,1:T(2,128)(2,1)}), bf16[4,16,2,4096]{3,2,0,1:T(2,128)(2,1)S(1)}, u32[]{:S(2)}, u32[]{:S(2)}) %all-to-all-start.1) | async-done | bytes 1048608 | tf_op jit(solution)/shard_map/all_to_all | solution.py:188
  378.7 0.8 broadcast_select_fusion
  (12 shorter events, 0.1 us)
Async XLA Ops:
  6.5 51.7 %all-gather.3.cloned.1.call-start = ((), (), s32[]{:S(2)}) async-start(), calls=%async_computation.2 | async-start | bytes 1114112 | tf_op jit(solution)/shard_map/all_gather | solution.py:168
  60.4 12.5 %copy-start = (s32[1,32,4]{1,2,0:T(4,128)S(1)}, s32[1,32,4]{1,2,0:T(4,128)}, u32[]{:S(2)}) copy-start(s32[1,32,4]{1,2,0:T(4,128)} %param.7) | copy-start | bytes 1540
  63.0 33.8 %all-to-all-start = ((bf16[4,16,2,32,128]{4,3,2,0,1:T(8,128)(2,1)}), bf16[4,16,2,32,128]{4,3,2,0,1:T(8,128)(2,1)S(1)}, u32[]{:S(2)}, u32[]{:S(2)}) async-start(bf16[4,16,2,32,128]{4,3,2,0,1:T(8,128)(2,1)} %copy_select_fusion), calls=%async_computation | async-start | bytes 2097152 | tf_op jit(solution)/shard_map/all_to_all | solution.py:176
  70.2 7.6 %collective-permute-start = (s32[16,2]{0,1:T(2,128)S(1)}, s32[16,2]{0,1:T(2,128)S(1)}, u32[]{:S(2)}, u32[]{:S(2)}) collective-permute-start(s32[16,2]{0,1:T(2,128)S(1)} %bitcast.29), channel_id=1, source_target_pairs={{16,0},{32,16},{48,32},{64,48},{80,64},{96,80},{112,96},{128,112},... | collective-permute-start | bytes 392 | tf_op jit(solution)/shard_map/ppermute | solution.py:17
  300.0 63.6 %copy-start.1 = (s32[4]{0:T(128)S(1)}, s32[4]{0:T(128)}, u32[]{:S(2)}) copy-start(s32[4]{0:T(128)} %param.9) | copy-start | bytes 52
  304.1 74.6 %all-to-all-start.1 = ((bf16[4,16,2,4096]{3,2,0,1:T(2,128)(2,1)}), bf16[4,16,2,4096]{3,2,0,1:T(2,128)(2,1)S(1)}, u32[]{:S(2)}, u32[]{:S(2)}) async-start(bf16[4,16,2,4096]{3,2,0,1:T(2,128)(2,1)} %copy.51), calls=%async_computation.1 | async-start | bytes 2097152 | tf_op jit(solution)/shard_map/all_to_all | solution.py:188
Sparse Core Ops, SparseCore 0:
  9.8 48.4 all-gather.2

commit v3 on v2

--- a/solution.py
+++ b/solution.py
@@ -42,7 +42,7 @@
     me_s = lax.axis_index("section")
     me_c = lax.axis_index("col")
     blocks_own = w_ref.shape[0]
-    nonzero_count = w_ref.shape[1]
+    nonzero_count = slot_ref.shape[0] // blocks_own
     barrier = pltpu.get_barrier_semaphore()
 
     @pl.when(me_s > 0)
@@ -92,15 +92,14 @@
                 ).wait_recv()
 
         def block_step(j, carry):
-            acc = None
-            for k in range(nonzero_count):
-                picked = recv[m][slot_ref[j * nonzero_count + k]]
-                term = jnp.dot(picked, w_ref[j, k], preferred_element_type=jnp.float32)
-                acc = term if acc is None else acc + term
+            picked = jnp.concatenate(
+                [recv[m][slot_ref[j * nonzero_count + k]] for k in range(nonzero_count)], axis=-1
+            )
+            acc = jnp.dot(picked, w_ref[j], preferred_element_type=jnp.float32)
             out_ref[m, j] = jnp.clip(acc + b_ref[j], 0.0, 32.0).astype(out_ref.dtype)
             return carry
 
-        lax.fori_loop(0, blocks_own, block_step, 0)
+        lax.fori_loop(0, blocks_own, block_step, 0, unroll=True)
 
         @pl.when(me_s < sections - 1)
         def _():
@@ -108,7 +107,7 @@
                 send[m][i] = out_ref[m, next_ref[i]]
                 return carry
 
-            lax.fori_loop(0, owners * CAP, stage, 0)
+            lax.fori_loop(0, owners * CAP, stage, 0, unroll=True)
             for d in range(owners):
                 outgoing_copy(m, d).start()
 
@@ -177,7 +176,7 @@
 
     first_recv = first_recv.reshape(batches, owners * CAP, row_total, block_size)
     finished = run_pipeline(
-        first_recv, local_w, bias[0].reshape(blocks_own, 1, block_size), slot_of,
+        first_recv, local_w.reshape(blocks_own, nonzero_count * block_size, block_size), bias[0].reshape(blocks_own, 1, block_size), slot_of,
         outgoing_next, sections, owners,
     )
     completed = finished.transpose(0, 2, 1, 3).reshape(

time: 391 us -> 325 us (0.83)
  Pallas kernels: 202 us -> 151 us
  starting transfers between devices: 69.4 us -> 54.1 us
    pallas_call x1, Pallas kernels: 202 us -> 151 us  [run_pipeline(): pl.pallas_call(functools.partial(pipeline_kernel, sections, owners, batch...]
    all_to_all x1, starting transfers between devices: 59.5 us -> 44.3 us  [body(): lax.all_to_all(outgoing_rows, 'section', split_axis=1, concat_axis=1, til...]
where the time goes in v3:
time: 325 us; the launch traced here: 319 us
  Pallas kernels  151 us (46%)
  waiting for transfers between devices  56.6 us (17%)
  starting transfers between devices  54.1 us (17%)
  blocking collectives  20.7 us (6%)
  local copies, waits for them, and re-layouts  14 us (4%)
  between operations  13.6 us (4%)
  other arithmetic  9.02 us (3%)
    pallas_call x1, Pallas kernels, run_pipeline(): pl.pallas_call(functools.partial(pipeline_kernel, sections, owners, batch...  151 us
    all_to_all x1, starting transfers between devices, body(): lax.all_to_all(outgoing_rows, 'section', split_axis=1, concat_axis=1, til...  44.3 us
    all_gather x1, waiting for transfers between devices, body(): all_inputs = lax.all_gather(features, 'section', axis=1, tiled=True)  21.4 us
    all_gather x1, blocking collectives, body(): pattern_table = lax.all_gather(sources[0], 'col', axis=0, tiled=True)  20.7 us
    all_to_all x1, waiting for transfers between devices, body(): lax.all_to_all(first_payload, 'col', split_axis=1, concat_axis=1, tiled=T...  18.4 us
    all_to_all x1, waiting for transfers between devices, body(): lax.all_to_all(outgoing_rows, 'section', split_axis=1, concat_axis=1, til...  14 us
    all_to_all x1, starting transfers between devices, body(): lax.all_to_all(first_payload, 'col', split_axis=1, concat_axis=1, tiled=T...  7.12 us
  transfers between devices with their start and end apart: 4, of which 4 were waited for; matrix products, arithmetic and copies ran while one was open for 3% of the time, Pallas kernels for 0%

profile of v3, /device:TPU:28, one launch (start us, length us, event | category | flops | bytes accessed | tf_op | source)
XLA Modules:
  0.0 318.8 jit_solution(2270747280414520760)
XLA Ops:
  6.5 1.5 copy.41
  8.1 0.0 all-gather.3.cloned.1.call-update
  8.1 0.8 copy.38
  8.9 20.7 %all-gather = s32[1,512,4]{2,0,1:T(1,128)S(1)} all-gather(s32[1,32,4]{2,0,1:T(1,128)S(1)} %copy.38), channel_id=2, replica_groups=mesh['section'=16,'col'=16] {'col'}, dimensions={1}, use_global_device_ids=true | all-gather | bytes 8704 | tf_op jit(solution)/shard_map/all_gather | solution.py:153
  29.5 0.6 broadcast.92
  30.1 1.3 reduce.4
  31.4 0.2 eq.43
  31.6 0.8 fusion
  32.4 0.1 and.30
  32.5 3.0 reduce_window_sum.11
  35.5 0.6 select_reduce_fusion
  36.2 0.4 fusion.4
  36.6 0.1 reshape.120
  36.7 0.1 copy.39
  36.8 0.1 copy.40
  36.9 21.4 %all-gather.3.cloned.1.call-done = bf16[4,32,4096]{2,0,1:T(4,128)(2,1)} async-done(((bf16[4,2,4096]{2,0,1:T(4,128)(2,1)}), bf16[4,32,4096]{2,0,1:T(4,128)(2,1)}) %all-gather.3.cloned.1.call-update) | async-done | bytes 1048592 | tf_op jit(solution)/shard_map/all_gather | solution.py:167
  58.3 2.1 reshape.133
  60.4 0.0 copy-start
  60.4 0.7 copy.56
  61.1 0.7 gather_fusion
  61.9 1.2 copy_select_fusion
  63.0 7.1 %all-to-all-start = ((bf16[4,16,2,32,128]{4,3,2,0,1:T(8,128)(2,1)}), bf16[4,16,2,32,128]{4,3,2,0,1:T(8,128)(2,1)S(1)}, u32[]{:S(2)}, u32[]{:S(2)}) async-start(bf16[4,16,2,32,128]{4,3,2,0,1:T(8,128)(2,1)} %copy_select_fusion), calls=%async_computation | async-start | bytes 2097152 | tf_op jit(solution)/shard_map/all_to_all | solution.py:175
  70.2 2.7 collective-permute-start
  72.9 0.1 copy.46
  73.0 0.1 add.66
  73.1 0.1 add.67
  73.2 0.1 eq.50
  73.3 0.7 fusion.2
  74.0 0.1 copy.48
  74.1 0.1 and.34
  74.2 0.1 copy.47
  74.3 0.1 squeeze.15
  74.4 0.6 select_reduce_fusion.1.slot_ref
  75.0 2.8 collective-permute-done
  77.7 0.1 copy.49
  77.8 0.6 reshape.122.next_ref
  78.4 18.4 %all-to-all-done = bf16[4,16,2,32,128]{4,3,2,0,1:T(8,128)(2,1)S(1)} async-done(((bf16[4,16,2,32,128]{4,3,2,0,1:T(8,128)(2,1)}), bf16[4,16,2,32,128]{4,3,2,0,1:T(8,128)(2,1)S(1)}, u32[]{:S(2)}, u32[]{:S(2)}) %all-to-all-start) | async-done | bytes 1048608 | tf_op jit(solution)/shard_map/all_to_all | solution.py:175
  96.8 1.1 copy.45
  97.9 150.8 %shard_map.55 = bf16[4,32,32,128]{3,2,1,0:T(8,128)(2,1)} custom-call(bf16[4,32,32,128]{3,2,1,0:T(8,128)(2,1)} %bitcast.26, bf16[32,512,128]{2,1,0:T(8,128)(2,1)} %bitcast.25, f32[32,1,128]{2,1,0:T(1,128)} %bitcast.28, s32[128]{0:T(128)} %select_reduce_fusion.1.slot_ref, s32[32]{0:T(128)} %reshape.122.next_ref), custom_call_target="tpu_custom_call" | custom-call | tf_op jit(solution)/shard_map/pallas_call | solution.py:128
  248.7 0.0 copy-start.1
  248.7 1.6 copy.50
  250.4 0.3 reshape_reshape.3
  250.6 2.2 copy.51
  252.8 44.3 %all-to-all-start.1 = ((bf16[4,16,2,4096]{3,2,0,1:T(2,128)(2,1)}), bf16[4,16,2,4096]{3,2,0,1:T(2,128)(2,1)S(1)}, u32[]{:S(2)}, u32[]{:S(2)}) async-start(bf16[4,16,2,4096]{3,2,0,1:T(2,128)(2,1)} %copy.51), calls=%async_computation.1 | async-start | bytes 2097152 | tf_op jit(solution)/shard_map/all_to_all | solution.py:187
  297.1 0.0 copy-done.1
  297.1 0.1 broadcast_compare_fusion
  297.2 14.0 %all-to-all-done.1 = bf16[4,16,2,4096]{3,2,0,1:T(2,128)(2,1)S(1)} async-done(((bf16[4,16,2,4096]{3,2,0,1:T(2,128)(2,1)}), bf16[4,16,2,4096]{3,2,0,1:T(2,128)(2,1)S(1)}, u32[]{:S(2)}, u32[]{:S(2)}) %all-to-all-start.1) | async-done | bytes 1048608 | tf_op jit(solution)/shard_map/all_to_all | solution.py:187
  311.2 0.8 broadcast_select_fusion
  (12 shorter events, 0.1 us)
Async XLA Ops:
  6.5 51.7 %all-gather.3.cloned.1.call-start = ((), (), s32[]{:S(2)}) async-start(), calls=%async_computation.2 | async-start | bytes 1114112 | tf_op jit(solution)/shard_map/all_gather | solution.py:167
  60.4 12.5 %copy-start = (s32[1,32,4]{1,2,0:T(4,128)S(1)}, s32[1,32,4]{1,2,0:T(4,128)}, u32[]{:S(2)}) copy-start(s32[1,32,4]{1,2,0:T(4,128)} %param.7) | copy-start | bytes 1540
  63.0 33.8 %all-to-all-start = ((bf16[4,16,2,32,128]{4,3,2,0,1:T(8,128)(2,1)}), bf16[4,16,2,32,128]{4,3,2,0,1:T(8,128)(2,1)S(1)}, u32[]{:S(2)}, u32[]{:S(2)}) async-start(bf16[4,16,2,32,128]{4,3,2,0,1:T(8,128)(2,1)} %copy_select_fusion), calls=%async_computation | async-start | bytes 2097152 | tf_op jit(solution)/shard_map/all_to_all | solution.py:175
  70.2 7.6 %collective-permute-start = (s32[16,2]{0,1:T(2,128)S(1)}, s32[16,2]{0,1:T(2,128)S(1)}, u32[]{:S(2)}, u32[]{:S(2)}) collective-permute-start(s32[16,2]{0,1:T(2,128)S(1)} %bitcast.29), channel_id=1, source_target_pairs={{16,0},{32,16},{48,32},{64,48},{80,64},{96,80},{112,96},{128,112},... | collective-permute-start | bytes 392 | tf_op jit(solution)/shard_map/ppermute | solution.py:17
  248.7 48.4 %copy-start.1 = (s32[4]{0:T(128)S(1)}, s32[4]{0:T(128)}, u32[]{:S(2)}) copy-start(s32[4]{0:T(128)} %param.9) | copy-start | bytes 52
  252.8 58.4 %all-to-all-start.1 = ((bf16[4,16,2,4096]{3,2,0,1:T(2,128)(2,1)}), bf16[4,16,2,4096]{3,2,0,1:T(2,128)(2,1)S(1)}, u32[]{:S(2)}, u32[]{:S(2)}) async-start(bf16[4,16,2,4096]{3,2,0,1:T(2,128)(2,1)} %copy.51), calls=%async_computation.1 | async-start | bytes 2097152 | tf_op jit(solution)/shard_map/all_to_all | solution.py:187
Sparse Core Ops, SparseCore 0:
  9.8 48.4 all-gather.2

commit v4 on v3

--- a/solution.py
+++ b/solution.py
@@ -140,6 +140,102 @@
     )(first_recv, local_w, local_bias, slot_of, outgoing_next)
 
 
+def pattern_kernel(sections, owners, src_ref, own_ref, nxt_ref, *sems):
+    own_send, own_recv, nxt_send, nxt_recv, local_sem = sems
+    me_s = lax.axis_index("section")
+    me_c = lax.axis_index("col")
+    barrier = pltpu.get_barrier_semaphore()
+    for d in range(owners):
+
+        @pl.when(me_c != d)
+        def _():
+            pl.semaphore_signal(barrier, inc=1, device_id=(me_s, d), device_id_type=MESH_ID)
+
+    @pl.when(me_s > 0)
+    def _():
+        for d in range(owners):
+            pl.semaphore_signal(barrier, inc=1, device_id=(me_s - 1, d), device_id_type=MESH_ID)
+
+    @pl.when(me_s < sections - 1)
+    def _():
+        for d in range(owners):
+            pl.semaphore_signal(barrier, inc=1, device_id=(me_s + 1, d), device_id_type=MESH_ID)
+
+    peers = (owners - 1) + owners * (
+        (me_s > 0).astype(jnp.int32) + (me_s < sections - 1).astype(jnp.int32)
+    )
+    pl.semaphore_wait(barrier, peers)
+
+    def own_copy(d, e):
+        return pltpu.make_async_remote_copy(
+            src_ref=src_ref,
+            dst_ref=own_ref.at[e],
+            send_sem=own_send.at[d],
+            recv_sem=own_recv.at[e],
+            device_id=(me_s, d),
+            device_id_type=MESH_ID,
+        )
+
+    def nxt_copy(dev_s, d, e):
+        return pltpu.make_async_remote_copy(
+            src_ref=src_ref,
+            dst_ref=nxt_ref.at[e],
+            send_sem=nxt_send.at[d],
+            recv_sem=nxt_recv.at[e],
+            device_id=(dev_s, d),
+            device_id_type=MESH_ID,
+        )
+
+    for d in range(owners):
+
+        @pl.when(me_c != d)
+        def _():
+            own_copy(d, me_c).start()
+
+    @pl.when(me_s > 0)
+    def _():
+        for d in range(owners):
+            nxt_copy(me_s - 1, d, me_c).start()
+
+    mine = pltpu.make_async_copy(src_ref, own_ref.at[me_c], local_sem)
+    mine.start()
+    mine.wait()
+    for d in range(owners):
+
+        @pl.when(me_c != d)
+        def _():
+            own_copy(d, me_c).wait_send()
+            own_copy(d, d).wait_recv()
+
+    @pl.when(me_s > 0)
+    def _():
+        for d in range(owners):
+            nxt_copy(me_s - 1, d, me_c).wait_send()
+
+    @pl.when(me_s < sections - 1)
+    def _():
+        for e in range(owners):
+            nxt_copy(me_s + 1, e, e).wait_recv()
+
+    @pl.when(me_s == sections - 1)
+    def _():
+        nxt_ref[...] = jnp.zeros_like(nxt_ref)
+
+
+def exchange_patterns(local_sources, sections, owners):
+    table = jax.ShapeDtypeStruct((owners,) + local_sources.shape, local_sources.dtype)
+    vmem = pl.BlockSpec(memory_space=pltpu.VMEM)
+    return pl.pallas_call(
+        functools.partial(pattern_kernel, sections, owners),
+        out_shape=(table, table),
+        in_specs=[vmem],
+        out_specs=(vmem, vmem),
+        scratch_shapes=[pltpu.SemaphoreType.DMA((owners,)) for _ in range(4)]
+        + [pltpu.SemaphoreType.DMA(())],
+        compiler_params=pltpu.CompilerParams(collective_id=1, has_side_effects=True),
+    )(local_sources)
+
+
 def body(features, weights, sources, bias, batch_rows):
     sections = lax.axis_size("section")
     owners = lax.axis_size("col")
@@ -150,11 +246,15 @@
     nonzero_count = local_w.shape[1]
     block_size = local_w.shape[2]
     local_src = sources[0].reshape(blocks_own * nonzero_count)
-    pattern_table = lax.all_gather(sources[0], "col", axis=0, tiled=True)
-    positions, present = request_lists(pattern_table, owners, blocks_own, CAP)
+    own_table, next_table = exchange_patterns(sources[0], sections, owners)
+    both_positions, both_present = jax.vmap(
+        lambda table: request_lists(table, owners, blocks_own, CAP)
+    )(jnp.stack([own_table, next_table]))
+    positions, present = both_positions[0], both_present[0]
     outgoing = lax.dynamic_index_in_dim(positions, col_idx, 1, keepdims=False)
-    outgoing_next = from_behind(outgoing, "section", -1).reshape(owners * CAP)
     outgoing = outgoing.reshape(owners * CAP)
+    outgoing_next = lax.dynamic_index_in_dim(both_positions[1], col_idx, 1, keepdims=False)
+    outgoing_next = outgoing_next.reshape(owners * CAP)
     incoming = lax.dynamic_index_in_dim(positions, col_idx, 0, keepdims=False)
     incoming_ok = lax.dynamic_index_in_dim(present, col_idx, 0, keepdims=False)
     global_ids = incoming + blocks_own * jnp.arange(owners, dtype=jnp.int32)[:, None]

time: 325 us -> 323 us (level)
  Pallas kernels: 151 us -> 174 us
  blocking collectives: 20.7 us -> 0 us
  waiting for transfers between devices: 56.6 us -> 50.4 us
  starting transfers between devices: 54.1 us -> 48.9 us
  other arithmetic: 9.02 us -> 13.3 us
    pallas_call x0 -> x1, Pallas kernels: none -> 23.4 us  [exchange_patterns(): pl.pallas_call(functools.partial(pattern_kernel, sections, owners), out_s...]
    all_gather x1 -> x0, blocking collectives: 20.7 us -> none  [body(): pattern_table = lax.all_gather(sources[0], 'col', axis=0, tiled=True)]
    all_gather x1, waiting for transfers between devices: 21.4 us -> 13.1 us  [body(): all_inputs = lax.all_gather(features, 'section', axis=1, tiled=True)]
    all_to_all x1, waiting for transfers between devices: 18.4 us -> 23 us  [body(): lax.all_to_all(first_payload, 'col', split_axis=1, concat_axis=1, tiled=T...]
  transfers between devices with their start and end apart: 4 -> 3, of which waited for: 4 -> 3; matrix products, arithmetic and copies ran while one was open for 3% -> 6% of each run, Pallas kernels for 0% -> 7%
where the time goes in v4:
time: 323 us; the launch traced here: 317 us
  Pallas kernels  174 us (54%)
  waiting for transfers between devices  50.4 us (16%)
  starting transfers between devices  48.9 us (15%)
  local copies, waits for them, and re-layouts  16.9 us (5%)
  between operations  13.6 us (4%)
  other arithmetic  13.3 us (4%)
    pallas_call x1, Pallas kernels, run_pipeline(): pl.pallas_call(functools.partial(pipeline_kernel, sections, owners, batch...  151 us
    all_to_all x1, starting transfers between devices, body(): lax.all_to_all(outgoing_rows, 'section', split_axis=1, concat_axis=1, til...  41.8 us
    pallas_call x1, Pallas kernels, exchange_patterns(): pl.pallas_call(functools.partial(pattern_kernel, sections, owners), out_s...  23.4 us
    all_to_all x1, waiting for transfers between devices, body(): lax.all_to_all(first_payload, 'col', split_axis=1, concat_axis=1, tiled=T...  23 us
    all_to_all x1, waiting for transfers between devices, body(): lax.all_to_all(outgoing_rows, 'section', split_axis=1, concat_axis=1, til...  14.3 us
    all_gather x1, waiting for transfers between devices, body(): all_inputs = lax.all_gather(features, 'section', axis=1, tiled=True)  13.1 us
    all_to_all x1, starting transfers between devices, body(): lax.all_to_all(first_payload, 'col', split_axis=1, concat_axis=1, tiled=T...  7.12 us
  transfers between devices with their start and end apart: 3, of which 3 were waited for; matrix products, arithmetic and copies ran while one was open for 6% of the time, Pallas kernels for 7%

profile of v4, /device:TPU:28, one launch (start us, length us, event | category | flops | bytes accessed | tf_op | source)
XLA Modules:
  0.0 317.4 jit_solution(8252136975470554106)
XLA Ops:
  6.5 0.0 all-gather.2.cloned.1.call-start
  6.5 1.5 copy.52
  8.1 0.0 all-gather.2.cloned.1.call-update
  8.1 1.4 copy.45.src_ref
  9.4 23.4 %shard_map.55 = (s32[16,32,4]{2,1,0:T(8,128)}, s32[16,32,4]{2,1,0:T(8,128)}) custom-call(s32[32,4]{1,0:T(8,128)} %copy.45.src_ref), custom_call_target="tpu_custom_call" | custom-call | tf_op jit(solution)/shard_map/pallas_call | solution.py:228
  32.9 1.2 copy.46
  34.2 1.2 copy.47
  35.4 0.1 copy.49
  35.5 2.3 fusion
  37.8 0.2 and.30
  38.0 6.0 %reduce_window_sum.11 = s32[2,16,16,32]{3,2,1,0:T(8,128)S(1)} reduce-window(s32[2,16,16,32]{3,2,1,0:T(8,128)S(1)} %convert_element_type.9, s32[]{:T(128)} %constant.51.clone.1), window={size=1x1x1x32 pad=0_0x0_0x0_0x31_0}, to_apply=%region_1.0 | reduce-window | flops 507904 | bytes 131076 | tf_op jit(solution)/shard_map/vmap(jit(cumsum))/reduce_window_sum | solution.py:26
  44.0 1.2 select_reduce_fusion
  45.2 0.4 fusion.4
  45.6 0.1 reshape.134
  45.7 0.1 copy.50
  45.8 0.1 copy.51
  46.0 13.1 %all-gather.2.cloned.1.call-done = bf16[4,32,4096]{2,0,1:T(4,128)(2,1)} async-done(((bf16[4,2,4096]{2,0,1:T(4,128)(2,1)}), bf16[4,32,4096]{2,0,1:T(4,128)(2,1)}) %all-gather.2.cloned.1.call-update) | async-done | bytes 1048592 | tf_op jit(solution)/shard_map/all_gather | solution.py:267
  59.1 2.1 reshape.145
  61.2 0.0 copy-start
  61.2 0.7 copy.66
  61.9 0.7 gather_fusion
  62.7 1.2 copy_select_fusion
  63.8 7.1 %all-to-all-start = ((bf16[4,16,2,32,128]{4,3,2,0,1:T(8,128)(2,1)}), bf16[4,16,2,32,128]{4,3,2,0,1:T(8,128)(2,1)S(1)}, u32[]{:S(2)}, u32[]{:S(2)}) async-start(bf16[4,16,2,32,128]{4,3,2,0,1:T(8,128)(2,1)} %copy_select_fusion), calls=%async_computation | async-start | bytes 2097152 | tf_op jit(solution)/shard_map/all_to_all | solution.py:275
  70.9 0.0 copy-done
  71.0 0.1 copy.57
  71.0 0.1 add.67
  71.1 0.1 add.68
  71.2 0.1 eq.50
  71.3 1.2 fusion.2
  72.6 0.4 dynamic-slice_reduce_fusion
  73.0 0.6 reshape.136.next_ref
  73.6 0.1 copy.59
  73.7 0.1 and.34
  73.8 0.1 copy.58
  73.9 0.1 squeeze.19
  74.0 0.6 select_reduce_fusion.1.slot_ref
  74.6 23.0 %all-to-all-done = bf16[4,16,2,32,128]{4,3,2,0,1:T(8,128)(2,1)S(1)} async-done(((bf16[4,16,2,32,128]{4,3,2,0,1:T(8,128)(2,1)}), bf16[4,16,2,32,128]{4,3,2,0,1:T(8,128)(2,1)S(1)}, u32[]{:S(2)}, u32[]{:S(2)}) %all-to-all-start) | async-done | bytes 1048608 | tf_op jit(solution)/shard_map/all_to_all | solution.py:275
  97.6 1.1 copy.56
  98.7 150.9 %shard_map.56 = bf16[4,32,32,128]{3,2,1,0:T(8,128)(2,1)} custom-call(bf16[4,32,32,128]{3,2,1,0:T(8,128)(2,1)} %bitcast.34, bf16[32,512,128]{2,1,0:T(8,128)(2,1)} %bitcast.33, f32[32,1,128]{2,1,0:T(1,128)} %bitcast.38, s32[128]{0:T(128)} %select_reduce_fusion.1.slot_ref, s32[32]{0:T(128)} %reshape.136.next_ref), custom_call_target="tpu_custom_call" | custom-call | tf_op jit(solution)/shard_map/pallas_call | solution.py:128
  249.6 0.0 copy-start.1
  249.6 1.6 copy.60
  251.3 0.3 reshape_reshape.3
  251.5 2.2 copy.61
  253.7 41.8 %all-to-all-start.1 = ((bf16[4,16,2,4096]{3,2,0,1:T(2,128)(2,1)}), bf16[4,16,2,4096]{3,2,0,1:T(2,128)(2,1)S(1)}, u32[]{:S(2)}, u32[]{:S(2)}) async-start(bf16[4,16,2,4096]{3,2,0,1:T(2,128)(2,1)} %copy.61), calls=%async_computation.1 | async-start | bytes 2097152 | tf_op jit(solution)/shard_map/all_to_all | solution.py:287
  295.5 0.0 copy-done.1
  295.5 0.1 broadcast_compare_fusion
  295.6 14.3 %all-to-all-done.1 = bf16[4,16,2,4096]{3,2,0,1:T(2,128)(2,1)S(1)} async-done(((bf16[4,16,2,4096]{3,2,0,1:T(2,128)(2,1)}), bf16[4,16,2,4096]{3,2,0,1:T(2,128)(2,1)S(1)}, u32[]{:S(2)}, u32[]{:S(2)}) %all-to-all-start.1) | async-done | bytes 1048608 | tf_op jit(solution)/shard_map/all_to_all | solution.py:287
  309.9 0.8 broadcast_select_fusion
  (14 shorter events, 0.2 us)
Async XLA Ops:
  6.5 52.5 %all-gather.2.cloned.1.call-start = ((), (), s32[]{:S(2)}) async-start(), calls=%async_computation.2 | async-start | bytes 1114112 | tf_op jit(solution)/shard_map/all_gather | solution.py:267
  61.2 9.7 %copy-start = (s32[1,32,4]{1,2,0:T(4,128)S(1)}, s32[1,32,4]{1,2,0:T(4,128)}, u32[]{:S(2)}) copy-start(s32[1,32,4]{1,2,0:T(4,128)} %param.7) | copy-start | bytes 1540
  63.8 33.8 %all-to-all-start = ((bf16[4,16,2,32,128]{4,3,2,0,1:T(8,128)(2,1)}), bf16[4,16,2,32,128]{4,3,2,0,1:T(8,128)(2,1)S(1)}, u32[]{:S(2)}, u32[]{:S(2)}) async-start(bf16[4,16,2,32,128]{4,3,2,0,1:T(8,128)(2,1)} %copy_select_fusion), calls=%async_computation | async-start | bytes 2097152 | tf_op jit(solution)/shard_map/all_to_all | solution.py:275
  249.6 45.9 %copy-start.1 = (s32[4]{0:T(128)S(1)}, s32[4]{0:T(128)}, u32[]{:S(2)}) copy-start(s32[4]{0:T(128)} %param.9) | copy-start | bytes 52
  253.7 56.1 %all-to-all-start.1 = ((bf16[4,16,2,4096]{3,2,0,1:T(2,128)(2,1)}), bf16[4,16,2,4096]{3,2,0,1:T(2,128)(2,1)S(1)}, u32[]{:S(2)}, u32[]{:S(2)}) async-start(bf16[4,16,2,4096]{3,2,0,1:T(2,128)(2,1)} %copy.61), calls=%async_computation.1 | async-start | bytes 2097152 | tf_op jit(solution)/shard_map/all_to_all | solution.py:287
Sparse Core Ops, SparseCore 0:
  9.8 49.2 all-gather.1

commit v5 on v4

--- a/solution.py
+++ b/solution.py
@@ -140,8 +140,8 @@
     )(first_recv, local_w, local_bias, slot_of, outgoing_next)
 
 
-def pattern_kernel(sections, owners, src_ref, own_ref, nxt_ref, *sems):
-    own_send, own_recv, nxt_send, nxt_recv, local_sem = sems
+def pattern_kernel(sections, owners, src_ref, feat_ref, own_ref, nxt_ref, rows_ref, *sems):
+    own_send, own_recv, nxt_send, nxt_recv, local_sem, rows_send, rows_recv, rows_sem = sems
     me_s = lax.axis_index("section")
     me_c = lax.axis_index("col")
     barrier = pltpu.get_barrier_semaphore()
@@ -161,9 +161,19 @@
         for d in range(owners):
             pl.semaphore_signal(barrier, inc=1, device_id=(me_s + 1, d), device_id_type=MESH_ID)
 
+    @pl.when(me_s > 0)
+    def _():
+        pl.semaphore_signal(barrier, inc=1, device_id=(0, me_c), device_id_type=MESH_ID)
+
+    @pl.when(me_s == 0)
+    def _():
+        for r in range(1, sections):
+            pl.semaphore_signal(barrier, inc=1, device_id=(r, me_c), device_id_type=MESH_ID)
+
+    is_first = (me_s == 0).astype(jnp.int32)
     peers = (owners - 1) + owners * (
         (me_s > 0).astype(jnp.int32) + (me_s < sections - 1).astype(jnp.int32)
-    )
+    ) + is_first * (sections - 1) + (1 - is_first)
     pl.semaphore_wait(barrier, peers)
 
     def own_copy(d, e):
@@ -197,6 +207,26 @@
         for d in range(owners):
             nxt_copy(me_s - 1, d, me_c).start()
 
+    def rows_copy(r):
+        return pltpu.make_async_remote_copy(
+            src_ref=feat_ref,
+            dst_ref=rows_ref.at[r],
+            send_sem=rows_send,
+            recv_sem=rows_recv.at[r],
+            device_id=(0, me_c),
+            device_id_type=MESH_ID,
+        )
+
+    @pl.when(me_s > 0)
+    def _():
+        rows_copy(me_s).start()
+
+    @pl.when(me_s == 0)
+    def _():
+        own_rows = pltpu.make_async_copy(feat_ref, rows_ref.at[0], rows_sem)
+        own_rows.start()
+        own_rows.wait()
+
     mine = pltpu.make_async_copy(src_ref, own_ref.at[me_c], local_sem)
     mine.start()
     mine.wait()
@@ -221,19 +251,35 @@
     def _():
         nxt_ref[...] = jnp.zeros_like(nxt_ref)
 
-
-def exchange_patterns(local_sources, sections, owners):
+    @pl.when(me_s > 0)
+    def _():
+        rows_copy(me_s).wait_send()
+        rows_ref[...] = jnp.zeros_like(rows_ref)
+
+    @pl.when(me_s == 0)
+    def _():
+        for r in range(1, sections):
+            rows_copy(r).wait_recv()
+
+
+def exchange_patterns(local_sources, features, sections, owners):
     table = jax.ShapeDtypeStruct((owners,) + local_sources.shape, local_sources.dtype)
+    rows = jax.ShapeDtypeStruct((sections,) + features.shape, features.dtype)
     vmem = pl.BlockSpec(memory_space=pltpu.VMEM)
     return pl.pallas_call(
         functools.partial(pattern_kernel, sections, owners),
-        out_shape=(table, table),
-        in_specs=[vmem],
-        out_specs=(vmem, vmem),
+        out_shape=(table, table, rows),
+        in_specs=[vmem, vmem],
+        out_specs=(vmem, vmem, vmem),
         scratch_shapes=[pltpu.SemaphoreType.DMA((owners,)) for _ in range(4)]
-        + [pltpu.SemaphoreType.DMA(())],
+        + [
+            pltpu.SemaphoreType.DMA(()),
+            pltpu.SemaphoreType.DMA(()),
+            pltpu.SemaphoreType.DMA((sections,)),
+            pltpu.SemaphoreType.DMA(()),
+        ],
         compiler_params=pltpu.CompilerParams(collective_id=1, has_side_effects=True),
-    )(local_sources)
+    )(local_sources, features)
 
 
 def body(features, weights, sources, bias, batch_rows):
@@ -246,7 +292,7 @@
     nonzero_count = local_w.shape[1]
     block_size = local_w.shape[2]
     local_src = sources[0].reshape(blocks_own * nonzero_count)
-    own_table, next_table = exchange_patterns(sources[0], sections, owners)
+    own_table, next_table, row_parts = exchange_patterns(sources[0], features, sections, owners)
     both_positions, both_present = jax.vmap(
         lambda table: request_lists(table, owners, blocks_own, CAP)
     )(jnp.stack([own_table, next_table]))
@@ -264,9 +310,9 @@
     slot_of = jnp.sum(
         matches.astype(jnp.int32) * jnp.arange(owners * CAP, dtype=jnp.int32)[None, :], axis=1
     )
-    all_inputs = lax.all_gather(features, "section", axis=1, tiled=True)
-    batches = all_inputs.shape[0]
-    row_total = all_inputs.shape[1]
+    batches = features.shape[0]
+    row_total = features.shape[1] * sections
+    all_inputs = row_parts.transpose(1, 0, 2, 3).reshape(batches, row_total, -1)
     blocks_in = all_inputs.reshape(batches, row_total, blocks_own, block_size)
     blocks_in = blocks_in.transpose(0, 2, 1, 3)
     first_payload = jnp.take(blocks_in, outgoing, axis=1).reshape(

time: 323 us -> 294 us (0.910)
  between operations: 13.6 us -> 0.2 us
  waiting for transfers between devices: 50.4 us -> 37.1 us
    all_gather x1 -> x0, waiting for transfers between devices: 13.1 us -> none  [body(): all_inputs = lax.all_gather(features, 'section', axis=1, tiled=True)]
    pallas_call x1, Pallas kernels: 151 us -> 147 us  [run_pipeline(): pl.pallas_call(functools.partial(pipeline_kernel, sections, owners, batch...]
  transfers between devices with their start and end apart: 3 -> 2, of which waited for: 3 -> 2; matrix products, arithmetic and copies ran while one was open for 6% -> 1% of each run, Pallas kernels for 7% -> 0%
where the time goes in v5:
time: 294 us; the launch traced here: 289 us
  Pallas kernels  171 us (58%)
  starting transfers between devices  50.3 us (17%)
  waiting for transfers between devices  37.1 us (13%)
  local copies, waits for them, and re-layouts  16 us (5%)
  other arithmetic  13.4 us (5%)
    pallas_call x1, Pallas kernels, run_pipeline(): pl.pallas_call(functools.partial(pipeline_kernel, sections, owners, batch...  147 us
    all_to_all x1, starting transfers between devices, body(): lax.all_to_all(outgoing_rows, 'section', split_axis=1, concat_axis=1, til...  42.8 us
    pallas_call x1, Pallas kernels, exchange_patterns(): pl.pallas_call(functools.partial(pattern_kernel, sections, owners), out_s...  24.1 us
    all_to_all x1, waiting for transfers between devices, body(): lax.all_to_all(first_payload, 'col', split_axis=1, concat_axis=1, tiled=T...  23 us
    all_to_all x1, waiting for transfers between devices, body(): lax.all_to_all(outgoing_rows, 'section', split_axis=1, concat_axis=1, til...  14.1 us
    all_to_all x1, starting transfers between devices, body(): lax.all_to_all(first_payload, 'col', split_axis=1, concat_axis=1, tiled=T...  7.55 us
    another operation x1, other arithmetic, request_lists(): block_ranks = jnp.cumsum(wanted.astype(jnp.int32), axis=2) - 1  5.98 us
  transfers between devices with their start and end apart: 2, of which 2 were waited for; matrix products, arithmetic and copies ran while one was open for 1% of the time, Pallas kernels for 0%

profile of v5, /device:TPU:28, one launch (start us, length us, event | category | flops | bytes accessed | tf_op | source)
XLA Modules:
  0.0 288.5 jit_solution(3279533886311576435)
XLA Ops:
  0.0 1.4 copy.35.src_ref
  1.4 24.1 %shard_map.55 = (s32[16,32,4]{2,1,0:T(8,128)}, s32[16,32,4]{2,1,0:T(8,128)}, bf16[16,4,2,4096]{3,2,1,0:T(2,128)(2,1)}) custom-call(s32[32,4]{1,0:T(8,128)} %copy.35.src_ref, bf16[4,2,4096]{2,1,0:T(2,128)(2,1)} %feat_ref.1), custom_call_target="tpu_custom_call" | custom-call | tf_op jit(solution)/shard_map/pallas_call | solution.py:269
  25.5 1.2 copy.36
  26.8 1.2 copy.37
  28.1 2.3 fusion
  30.4 0.2 and.30
  30.6 6.0 %reduce_window_sum.11 = s32[2,16,16,32]{3,2,1,0:T(8,128)S(1)} reduce-window(s32[2,16,16,32]{3,2,1,0:T(8,128)S(1)} %convert_element_type.9, s32[]{:T(128)} %constant.51.clone.1), window={size=1x1x1x32 pad=0_0x0_0x0_0x31_0}, to_apply=%region_1.0 | reduce-window | flops 507904 | bytes 131076 | tf_op jit(solution)/shard_map/vmap(jit(cumsum))/reduce_window_sum | solution.py:26
  36.6 1.2 select_reduce_fusion
  37.8 0.4 fusion.4
  38.3 0.1 reshape.130
  38.4 0.1 copy.40
  38.5 0.1 copy.41
  38.6 2.3 copy.42
  40.9 0.8 reshape_reshape.6
  41.7 0.0 copy-start
  41.7 0.4 copy.53
  42.1 0.7 gather_fusion
  42.9 1.2 copy_select_fusion
  44.1 7.6 %all-to-all-start = ((bf16[4,16,2,32,128]{4,3,2,0,1:T(8,128)(2,1)}), bf16[4,16,2,32,128]{4,3,2,0,1:T(8,128)(2,1)S(1)}, u32[]{:S(2)}, u32[]{:S(2)}) async-start(bf16[4,16,2,32,128]{4,3,2,0,1:T(8,128)(2,1)} %copy_select_fusion), calls=%async_computation | async-start | bytes 2097152 | tf_op jit(solution)/shard_map/all_to_all | solution.py:321
  51.6 0.0 copy-done
  51.6 0.1 copy.46
  51.7 0.1 add.67
  51.8 0.1 add.68
  51.9 0.1 eq.50
  52.0 1.2 fusion.2
  53.2 0.4 dynamic-slice_reduce_fusion
  53.6 0.6 reshape.132.next_ref
  54.3 0.1 copy.48
  54.4 0.1 and.34
  54.5 0.1 copy.47
  54.6 0.1 squeeze.19
  54.7 0.6 select_reduce_fusion.1.slot_ref
  55.3 23.0 %all-to-all-done = bf16[4,16,2,32,128]{4,3,2,0,1:T(8,128)(2,1)S(1)} async-done(((bf16[4,16,2,32,128]{4,3,2,0,1:T(8,128)(2,1)}), bf16[4,16,2,32,128]{4,3,2,0,1:T(8,128)(2,1)S(1)}, u32[]{:S(2)}, u32[]{:S(2)}) %all-to-all-start) | async-done | bytes 1048608 | tf_op jit(solution)/shard_map/all_to_all | solution.py:321
  78.3 1.1 copy.45
  79.4 147.3 %shard_map.56 = bf16[4,32,32,128]{3,2,1,0:T(8,128)(2,1)} custom-call(bf16[4,32,32,128]{3,2,1,0:T(8,128)(2,1)} %bitcast.33, bf16[32,512,128]{2,1,0:T(8,128)(2,1)} %bitcast.32, f32[32,1,128]{2,1,0:T(1,128)} %bitcast.38, s32[128]{0:T(128)} %select_reduce_fusion.1.slot_ref, s32[32]{0:T(128)} %reshape.132.next_ref), custom_call_target="tpu_custom_call" | custom-call | tf_op jit(solution)/shard_map/pallas_call | solution.py:128
  226.7 0.0 copy-start.1
  226.7 1.6 copy.49
  228.3 0.3 reshape_reshape.7
  228.6 2.2 copy.50
  230.8 42.8 %all-to-all-start.1 = ((bf16[4,16,2,4096]{3,2,0,1:T(2,128)(2,1)}), bf16[4,16,2,4096]{3,2,0,1:T(2,128)(2,1)S(1)}, u32[]{:S(2)}, u32[]{:S(2)}) async-start(bf16[4,16,2,4096]{3,2,0,1:T(2,128)(2,1)} %copy.50), calls=%async_computation.1 | async-start | bytes 2097152 | tf_op jit(solution)/shard_map/all_to_all | solution.py:333
  273.6 0.0 copy-done.1
  273.6 0.1 broadcast_compare_fusion
  273.7 14.1 %all-to-all-done.1 = bf16[4,16,2,4096]{3,2,0,1:T(2,128)(2,1)S(1)} async-done(((bf16[4,16,2,4096]{3,2,0,1:T(2,128)(2,1)}), bf16[4,16,2,4096]{3,2,0,1:T(2,128)(2,1)S(1)}, u32[]{:S(2)}, u32[]{:S(2)}) %all-to-all-start.1) | async-done | bytes 1048608 | tf_op jit(solution)/shard_map/all_to_all | solution.py:333
  287.8 0.8 broadcast_select_fusion
  (15 shorter events, 0.2 us)
Async XLA Ops:
  41.7 9.9 %copy-start = (s32[1,32,4]{1,2,0:T(4,128)S(1)}, s32[1,32,4]{1,2,0:T(4,128)}, u32[]{:S(2)}) copy-start(s32[1,32,4]{1,2,0:T(4,128)} %param.7) | copy-start | bytes 1540
  44.1 34.2 %all-to-all-start = ((bf16[4,16,2,32,128]{4,3,2,0,1:T(8,128)(2,1)}), bf16[4,16,2,32,128]{4,3,2,0,1:T(8,128)(2,1)S(1)}, u32[]{:S(2)}, u32[]{:S(2)}) async-start(bf16[4,16,2,32,128]{4,3,2,0,1:T(8,128)(2,1)} %copy_select_fusion), calls=%async_computation | async-start | bytes 2097152 | tf_op jit(solution)/shard_map/all_to_all | solution.py:321
  226.7 46.9 %copy-start.1 = (s32[4]{0:T(128)S(1)}, s32[4]{0:T(128)}, u32[]{:S(2)}) copy-start(s32[4]{0:T(128)} %param.9) | copy-start | bytes 52
  230.8 57.0 %all-to-all-start.1 = ((bf16[4,16,2,4096]{3,2,0,1:T(2,128)(2,1)}), bf16[4,16,2,4096]{3,2,0,1:T(2,128)(2,1)S(1)}, u32[]{:S(2)}, u32[]{:S(2)}) async-start(bf16[4,16,2,4096]{3,2,0,1:T(2,128)(2,1)} %copy.50), calls=%async_computation.1 | async-start | bytes 2097152 | tf_op jit(solution)/shard_map/all_to_all | solution.py:333

commit v6 on v5

--- a/solution.py
+++ b/solution.py
@@ -320,12 +320,18 @@
     )
     first_recv = lax.all_to_all(first_payload, "col", split_axis=1, concat_axis=1, tiled=True)
 
-    first_recv = first_recv.reshape(batches, owners * CAP, row_total, block_size)
+    piece_rows = 16
+    splits = row_total // piece_rows
+    first_recv = first_recv.reshape(batches, owners * CAP, splits, piece_rows, block_size)
+    first_recv = first_recv.transpose(0, 2, 1, 3, 4).reshape(
+        batches * splits, owners * CAP, piece_rows, block_size
+    )
     finished = run_pipeline(
         first_recv, local_w.reshape(blocks_own, nonzero_count * block_size, block_size), bias[0].reshape(blocks_own, 1, block_size), slot_of,
         outgoing_next, sections, owners,
     )
-    completed = finished.transpose(0, 2, 1, 3).reshape(
+    finished = finished.reshape(batches, splits, blocks_own, piece_rows, block_size)
+    completed = finished.transpose(0, 1, 3, 2, 4).reshape(
         batches, row_total, blocks_own * block_size
     )
     own_rows = row_total // sections

time: 294 us -> 255 us (0.87)
  Pallas kernels: 171 us -> 142 us
  starting transfers between devices: 50.3 us -> 41.6 us
    pallas_call x1, Pallas kernels: 147 us -> 118 us  [run_pipeline(): pl.pallas_call(functools.partial(pipeline_kernel, sections, owners, batch...]
    all_to_all x1, starting transfers between devices: 42.8 us -> 34 us  [body(): lax.all_to_all(outgoing_rows, 'section', split_axis=1, concat_axis=1, til...]
where the time goes in v6:
time: 255 us; the launch traced here: 251 us
  Pallas kernels  142 us (56%)
  starting transfers between devices  41.6 us (16%)
  waiting for transfers between devices  37.6 us (15%)
  local copies, waits for them, and re-layouts  15.9 us (6%)
  other arithmetic  13.4 us (5%)
    pallas_call x1, Pallas kernels, run_pipeline(): pl.pallas_call(functools.partial(pipeline_kernel, sections, owners, batch...  118 us
    all_to_all x1, starting transfers between devices, body(): lax.all_to_all(outgoing_rows, 'section', split_axis=1, concat_axis=1, til...  34 us
    pallas_call x1, Pallas kernels, exchange_patterns(): pl.pallas_call(functools.partial(pattern_kernel, sections, owners), out_s...  24.1 us
    all_to_all x1, waiting for transfers between devices, body(): lax.all_to_all(first_payload, 'col', split_axis=1, concat_axis=1, tiled=T...  23.4 us
    all_to_all x1, waiting for transfers between devices, body(): lax.all_to_all(outgoing_rows, 'section', split_axis=1, concat_axis=1, til...  14.2 us
    all_to_all x1, starting transfers between devices, body(): lax.all_to_all(first_payload, 'col', split_axis=1, concat_axis=1, tiled=T...  7.55 us
    another operation x1, other arithmetic, request_lists(): block_ranks = jnp.cumsum(wanted.astype(jnp.int32), axis=2) - 1  5.98 us
  transfers between devices with their start and end apart: 2, of which 2 were waited for; matrix products, arithmetic and copies ran while one was open for 1% of the time, Pallas kernels for 0%

profile of v6, /device:TPU:28, one launch (start us, length us, event | category | flops | bytes accessed | tf_op | source)
XLA Modules:
  0.0 250.5 jit_solution(302074387073125946)
XLA Ops:
  0.0 1.4 copy.37.src_ref
  1.4 24.1 %shard_map.55 = (s32[16,32,4]{2,1,0:T(8,128)}, s32[16,32,4]{2,1,0:T(8,128)}, bf16[16,4,2,4096]{3,2,1,0:T(2,128)(2,1)}) custom-call(s32[32,4]{1,0:T(8,128)} %copy.37.src_ref, bf16[4,2,4096]{2,1,0:T(2,128)(2,1)} %feat_ref.1), custom_call_target="tpu_custom_call" | custom-call | tf_op jit(solution)/shard_map/pallas_call | solution.py:269
  25.5 1.2 copy.38
  26.8 1.2 copy.39
  28.1 2.3 fusion
  30.4 0.2 and.30
  30.6 6.0 %reduce_window_sum.11 = s32[2,16,16,32]{3,2,1,0:T(8,128)S(1)} reduce-window(s32[2,16,16,32]{3,2,1,0:T(8,128)S(1)} %convert_element_type.9, s32[]{:T(128)} %constant.51.clone.1), window={size=1x1x1x32 pad=0_0x0_0x0_0x31_0}, to_apply=%region_1.0 | reduce-window | flops 507904 | bytes 131076 | tf_op jit(solution)/shard_map/vmap(jit(cumsum))/reduce_window_sum | solution.py:26
  36.6 1.2 select_reduce_fusion
  37.8 0.7 fusion.4
  38.5 0.1 reshape.136
  38.6 0.1 copy.42
  38.7 0.1 copy.43
  38.8 2.3 copy.44
  41.1 0.8 reshape_reshape.6
  42.0 0.0 copy-start
  42.0 0.4 copy.58
  42.4 0.7 gather_fusion
  43.2 1.2 copy_select_fusion
  44.3 7.6 %all-to-all-start = ((bf16[4,16,2,32,128]{4,3,2,0,1:T(8,128)(2,1)}), bf16[4,16,2,32,128]{4,3,2,0,1:T(8,128)(2,1)S(1)}, u32[]{:S(2)}, u32[]{:S(2)}) async-start(bf16[4,16,2,32,128]{4,3,2,0,1:T(8,128)(2,1)} %copy_select_fusion), calls=%async_computation | async-start | bytes 2097152 | tf_op jit(solution)/shard_map/all_to_all | solution.py:321
  51.9 0.0 copy-done
  51.9 0.1 copy.49
  52.0 0.1 add.67
  52.1 0.1 add.68
  52.1 0.1 eq.50
  52.3 1.2 fusion.2
  53.5 0.6 reshape.139.next_ref
  54.1 0.1 copy.51
  54.2 0.1 and.34
  54.3 0.1 copy.50
  54.4 0.1 squeeze.19
  54.5 0.6 select_reduce_fusion.1.slot_ref
  55.1 23.4 %all-to-all-done = bf16[4,16,2,32,128]{4,3,2,0,1:T(8,128)(2,1)S(1)} async-done(((bf16[4,16,2,32,128]{4,3,2,0,1:T(8,128)(2,1)}), bf16[4,16,2,32,128]{4,3,2,0,1:T(8,128)(2,1)S(1)}, u32[]{:S(2)}, u32[]{:S(2)}) %all-to-all-start) | async-done | bytes 1048608 | tf_op jit(solution)/shard_map/all_to_all | solution.py:321
  78.5 0.1 copy.47
  78.6 1.2 copy.48
  79.8 117.6 %shard_map.56 = bf16[8,32,16,128]{3,2,1,0:T(8,128)(2,1)} custom-call(bf16[8,32,16,128]{3,2,1,0:T(8,128)(2,1)} %bitcast.41, bf16[32,512,128]{2,1,0:T(8,128)(2,1)} %bitcast.38, f32[32,1,128]{2,1,0:T(1,128)} %bitcast.46, s32[128]{0:T(128)} %select_reduce_fusion.1.slot_ref, s32[32]{0:T(128)} %reshape.139.next_ref), custom_call_target="tpu_custom_call" | custom-call | tf_op jit(solution)/shard_map/pallas_call | solution.py:128
  197.4 0.0 copy-start.1
  197.4 1.5 copy.57
  199.0 0.3 reshape_reshape.7
  199.2 2.2 copy.53
  201.4 34.0 %all-to-all-start.1 = ((bf16[4,16,2,4096]{3,2,0,1:T(2,128)(2,1)}), bf16[4,16,2,4096]{3,2,0,1:T(2,128)(2,1)S(1)}, u32[]{:S(2)}, u32[]{:S(2)}) async-start(bf16[4,16,2,4096]{3,2,0,1:T(2,128)(2,1)} %copy.53), calls=%async_computation.1 | async-start | bytes 2097152 | tf_op jit(solution)/shard_map/all_to_all | solution.py:339
  235.5 0.0 copy-done.1
  235.5 0.1 broadcast_compare_fusion
  235.5 14.2 %all-to-all-done.1 = bf16[4,16,2,4096]{3,2,0,1:T(2,128)(2,1)S(1)} async-done(((bf16[4,16,2,4096]{3,2,0,1:T(2,128)(2,1)}), bf16[4,16,2,4096]{3,2,0,1:T(2,128)(2,1)S(1)}, u32[]{:S(2)}, u32[]{:S(2)}) %all-to-all-start.1) | async-done | bytes 1048608 | tf_op jit(solution)/shard_map/all_to_all | solution.py:339
  249.8 0.8 broadcast_select_fusion
  (15 shorter events, 0.2 us)
Async XLA Ops:
  42.0 9.9 %copy-start = (s32[1,32,4]{1,2,0:T(4,128)S(1)}, s32[1,32,4]{1,2,0:T(4,128)}, u32[]{:S(2)}) copy-start(s32[1,32,4]{1,2,0:T(4,128)} %param.7) | copy-start | bytes 1540
  44.3 34.2 %all-to-all-start = ((bf16[4,16,2,32,128]{4,3,2,0,1:T(8,128)(2,1)}), bf16[4,16,2,32,128]{4,3,2,0,1:T(8,128)(2,1)S(1)}, u32[]{:S(2)}, u32[]{:S(2)}) async-start(bf16[4,16,2,32,128]{4,3,2,0,1:T(8,128)(2,1)} %copy_select_fusion), calls=%async_computation | async-start | bytes 2097152 | tf_op jit(solution)/shard_map/all_to_all | solution.py:321
  197.4 38.0 %copy-start.1 = (s32[4]{0:T(128)S(1)}, s32[4]{0:T(128)}, u32[]{:S(2)}) copy-start(s32[4]{0:T(128)} %param.9) | copy-start | bytes 52
  201.4 48.4 %all-to-all-start.1 = ((bf16[4,16,2,4096]{3,2,0,1:T(2,128)(2,1)}), bf16[4,16,2,4096]{3,2,0,1:T(2,128)(2,1)S(1)}, u32[]{:S(2)}, u32[]{:S(2)}) async-start(bf16[4,16,2,4096]{3,2,0,1:T(2,128)(2,1)} %copy.53), calls=%async_computation.1 | async-start | bytes 2097152 | tf_op jit(solution)/shard_map/all_to_all | solution.py:339

commit v7 on v6

--- a/solution.py
+++ b/solution.py
@@ -23,7 +23,11 @@
     catalog = jnp.arange(block_total, dtype=jnp.int32)
     wanted = jnp.any(dest_entries[:, :, None] == catalog[None, None, :], axis=1)
     wanted = wanted.reshape(owners, owners, blocks_own)
-    block_ranks = jnp.cumsum(wanted.astype(jnp.int32), axis=2) - 1
+    local_rows = jnp.arange(blocks_own, dtype=jnp.int32)
+    below = local_rows[:, None] <= local_rows[None, :]
+    block_ranks = jnp.einsum(
+        "abi,ij->abj", wanted.astype(jnp.float32), below.astype(jnp.float32)
+    ).astype(jnp.int32) - 1
     slot_ids = jnp.arange(slot_total, dtype=jnp.int32)
     chosen = wanted[:, :, None, :] & (block_ranks[:, :, None, :] == slot_ids[None, None, :, None])
     local_ids = jnp.arange(blocks_own, dtype=jnp.int32)
@@ -33,12 +37,13 @@
 
 
 def pipeline_kernel(
-    sections, owners, batches, first_ref, w_ref, b_ref, slot_ref, next_ref,
+    sections, owners, batches, first_ref, w_ref, b_ref, slot_ref, next_ref, first_list_ref,
     out_ref, *scratch,
 ):
     recv = scratch[:batches]
     send = scratch[batches:2 * batches]
-    send_sem, recv_sem, local_sem = scratch[2 * batches:]
+    send0 = scratch[2 * batches:3 * batches]
+    send_sem, recv_sem, local_sem, send0_sem = scratch[3 * batches:]
     me_s = lax.axis_index("section")
     me_c = lax.axis_index("col")
     blocks_own = w_ref.shape[0]
@@ -55,17 +60,53 @@
         for d in range(owners):
             pl.semaphore_signal(barrier, inc=1, device_id=(me_s + 1, d), device_id_type=MESH_ID)
 
+    @pl.when(me_s == 0)
+    def _():
+        for d in range(owners):
+
+            @pl.when(me_c != d)
+            def _():
+                pl.semaphore_signal(barrier, inc=1, device_id=(0, d), device_id_type=MESH_ID)
+
+    is_first = (me_s == 0).astype(jnp.int32)
     peers = owners * (
         (me_s > 0).astype(jnp.int32) + (me_s < sections - 1).astype(jnp.int32)
-    )
+    ) + is_first * (owners - 1)
     pl.semaphore_wait(barrier, peers)
 
+    def first_copy(m, d):
+        return pltpu.make_async_remote_copy(
+            src_ref=send0[m].at[pl.ds(d * CAP, CAP)],
+            dst_ref=recv[m].at[pl.ds(me_c * CAP, CAP)],
+            send_sem=send0_sem.at[m, d],
+            recv_sem=recv_sem.at[m, me_c],
+            device_id=(0, d),
+            device_id_type=MESH_ID,
+        )
+
+    def first_local(m):
+        return pltpu.make_async_copy(
+            send0[m].at[pl.ds(me_c * CAP, CAP)],
+            recv[m].at[pl.ds(me_c * CAP, CAP)],
+            local_sem.at[m],
+        )
+
     @pl.when(me_s == 0)
     def _():
         for m in range(batches):
-            first = pltpu.make_async_copy(first_ref.at[m], recv[m], local_sem)
-            first.start()
-            first.wait()
+
+            def stage_first(i, carry):
+                send0[m][i] = first_ref[m, first_list_ref[i]]
+                return carry
+
+            lax.fori_loop(0, owners * CAP, stage_first, 0, unroll=True)
+            for d in range(owners):
+
+                @pl.when(me_c != d)
+                def _():
+                    first_copy(m, d).start()
+
+            first_local(m).start()
 
     def outgoing_copy(m, d):
         return pltpu.make_async_remote_copy(
@@ -78,6 +119,22 @@
         )
 
     for m in range(batches):
+
+        @pl.when(me_s == 0)
+        def _():
+            first_local(m).wait()
+            for e in range(owners):
+
+                @pl.when(me_c != e)
+                def _():
+                    pltpu.make_async_remote_copy(
+                        src_ref=send0[m].at[pl.ds(e * CAP, CAP)],
+                        dst_ref=recv[m].at[pl.ds(e * CAP, CAP)],
+                        send_sem=send0_sem.at[m, e],
+                        recv_sem=recv_sem.at[m, e],
+                        device_id=(0, e),
+                        device_id_type=MESH_ID,
+                    ).wait_recv()
 
         @pl.when(me_s > 0)
         def _():
@@ -117,27 +174,40 @@
             for d in range(owners):
                 outgoing_copy(m, d).wait_send()
 
-
-def run_pipeline(first_recv, local_w, local_bias, slot_of, outgoing_next, sections, owners):
-    batches = first_recv.shape[0]
+    @pl.when(me_s == 0)
+    def _():
+        for m in range(batches):
+            for d in range(owners):
+
+                @pl.when(me_c != d)
+                def _():
+                    first_copy(m, d).wait_send()
+
+
+def run_pipeline(
+    first_blocks, local_w, local_bias, slot_of, outgoing_next, outgoing, sections, owners
+):
+    batches = first_blocks.shape[0]
     blocks_own = local_w.shape[0]
-    rows = first_recv.shape[2]
+    rows = first_blocks.shape[2]
+    slots_shape = (owners * CAP,) + first_blocks.shape[2:]
     block_size = local_w.shape[-1]
     vmem = pl.BlockSpec(memory_space=pltpu.VMEM)
     smem = pl.BlockSpec(memory_space=pltpu.SMEM)
     return pl.pallas_call(
         functools.partial(pipeline_kernel, sections, owners, batches),
         out_shape=jax.ShapeDtypeStruct((batches, blocks_own, rows, block_size), jnp.bfloat16),
-        in_specs=[vmem, vmem, vmem, smem, smem],
+        in_specs=[vmem, vmem, vmem, smem, smem, smem],
         out_specs=vmem,
         scratch_shapes=[
-            *[pltpu.VMEM(first_recv.shape[1:], jnp.bfloat16) for _ in range(2 * batches)],
+            *[pltpu.VMEM(slots_shape, jnp.bfloat16) for _ in range(3 * batches)],
             pltpu.SemaphoreType.DMA((batches, owners)),
             pltpu.SemaphoreType.DMA((batches, owners)),
-            pltpu.SemaphoreType.DMA(()),
+            pltpu.SemaphoreType.DMA((batches,)),
+            pltpu.SemaphoreType.DMA((batches, owners)),
         ],
         compiler_params=pltpu.CompilerParams(collective_id=0, has_side_effects=True),
-    )(first_recv, local_w, local_bias, slot_of, outgoing_next)
+    )(first_blocks, local_w, local_bias, slot_of, outgoing_next, outgoing)
 
 
 def pattern_kernel(sections, owners, src_ref, feat_ref, own_ref, nxt_ref, rows_ref, *sems):
@@ -313,22 +383,19 @@
     batches = features.shape[0]
     row_total = features.shape[1] * sections
     all_inputs = row_parts.transpose(1, 0, 2, 3).reshape(batches, row_total, -1)
-    blocks_in = all_inputs.reshape(batches, row_total, blocks_own, block_size)
-    blocks_in = blocks_in.transpose(0, 2, 1, 3)
-    first_payload = jnp.take(blocks_in, outgoing, axis=1).reshape(
-        batches, owners, CAP, row_total, block_size
-    )
-    first_recv = lax.all_to_all(first_payload, "col", split_axis=1, concat_axis=1, tiled=True)
-
     piece_rows = 16
     splits = row_total // piece_rows
-    first_recv = first_recv.reshape(batches, owners * CAP, splits, piece_rows, block_size)
-    first_recv = first_recv.transpose(0, 2, 1, 3, 4).reshape(
-        batches * splits, owners * CAP, piece_rows, block_size
-    )
+    first_blocks = all_inputs.reshape(batches * splits, piece_rows, blocks_own, block_size)
+    first_blocks = first_blocks.transpose(0, 2, 1, 3)
     finished = run_pipeline(
-        first_recv, local_w.reshape(blocks_own, nonzero_count * block_size, block_size), bias[0].reshape(blocks_own, 1, block_size), slot_of,
-        outgoing_next, sections, owners,
+        first_blocks,
+        local_w.reshape(blocks_own, nonzero_count * block_size, block_size),
+        bias[0].reshape(blocks_own, 1, block_size),
+        slot_of,
+        outgoing_next,
+        outgoing,
+        sections,
+        owners,
     )
     finished = finished.reshape(batches, splits, blocks_own, piece_rows, block_size)
     completed = finished.transpose(0, 1, 3, 2, 4).reshape(

time: 255 us -> 245 us (0.961)
  Pallas kernels: 142 us -> 168 us
  waiting for transfers between devices: 37.6 us -> 13.9 us
  other arithmetic: 13.4 us -> 6.16 us
  starting transfers between devices: 41.6 us -> 37.2 us
    pallas_call x1, Pallas kernels: 118 us -> 144 us  [run_pipeline(): pl.pallas_call(functools.partial(pipeline_kernel, sections, owners, batch...]
    all_to_all x1 -> x0, waiting for transfers between devices: 23.4 us -> none  [body(): lax.all_to_all(first_payload, 'col', split_axis=1, concat_axis=1, tiled=T...]
    all_to_all x1 -> x0, starting transfers between devices: 7.55 us -> none  [body(): lax.all_to_all(first_payload, 'col', split_axis=1, concat_axis=1, tiled=T...]
    another operation x1 -> x0, other arithmetic: 5.98 us -> none  [request_lists(): block_ranks = jnp.cumsum(wanted.astype(jnp.int32), axis=2) - 1]
    all_to_all x1, starting transfers between devices: 34 us -> 37.2 us  [body(): lax.all_to_all(outgoing_rows, 'section', split_axis=1, concat_axis=1, til...]
  transfers between devices with their start and end apart: 2 -> 1, of which waited for: 2 -> 1; matrix products, arithmetic and copies ran while one was open for 1% -> 0% of each run, Pallas kernels for 0% -> 0%
where the time goes in v7:
time: 245 us; the launch traced here: 241 us
  Pallas kernels  168 us (69%)
  starting transfers between devices  37.2 us (15%)
  local copies, waits for them, and re-layouts  15.9 us (6%)
  waiting for transfers between devices  13.9 us (6%)
  other arithmetic  6.16 us (3%)
    pallas_call x1, Pallas kernels, run_pipeline(): pl.pallas_call(functools.partial(pipeline_kernel, sections, owners, batch...  144 us
    all_to_all x1, starting transfers between devices, body(): lax.all_to_all(outgoing_rows, 'section', split_axis=1, concat_axis=1, til...  37.2 us
    pallas_call x1, Pallas kernels, exchange_patterns(): pl.pallas_call(functools.partial(pattern_kernel, sections, owners), out_s...  24.1 us
    all_to_all x1, waiting for transfers between devices, body(): lax.all_to_all(outgoing_rows, 'section', split_axis=1, concat_axis=1, til...  13.9 us
  transfers between devices with their start and end apart: 1, of which 1 were waited for; matrix products, arithmetic and copies ran while one was open for 0% of the time, Pallas kernels for 0%

profile of v7, /device:TPU:28, one launch (start us, length us, event | category | flops | bytes accessed | tf_op | source)
XLA Modules:
  0.0 241.2 jit_solution(1753736224840075680)
XLA Ops:
  0.0 1.4 copy.26.src_ref
  1.4 24.1 %shard_map.55 = (s32[16,32,4]{2,1,0:T(8,128)}, s32[16,32,4]{2,1,0:T(8,128)}, bf16[16,4,2,4096]{3,2,1,0:T(2,128)(2,1)}) custom-call(s32[32,4]{1,0:T(8,128)} %copy.26.src_ref, bf16[4,2,4096]{2,1,0:T(2,128)(2,1)} %feat_ref.1), custom_call_target="tpu_custom_call" | custom-call | tf_op jit(solution)/shard_map/pallas_call | solution.py:339
  25.5 1.2 copy.30
  26.8 1.2 copy.31
  28.1 2.3 fusion
  30.4 0.2 and.22
  30.6 0.2 fusion.1
  30.7 1.2 select_reduce_fusion
  32.0 1.2 fusion.3
  33.2 0.8 copy.29
  34.0 0.1 copy.34
  34.0 0.1 squeeze.19
  34.1 0.1 add.37
  34.2 0.1 add.38
  34.3 0.1 copy.35
  34.4 0.1 and.25
  34.5 0.1 eq.43
  34.6 0.7 dynamic-slice_reduce_fusion
  35.3 0.6 reshape.79.next_ref
  35.9 0.6 reshape.80.first_list_ref
  36.6 2.3 copy.27
  38.9 0.8 reshape_reshape.6
  39.7 1.4 copy.42
  41.1 0.6 select_reduce_fusion.1.slot_ref
  41.7 143.6 %shard_map.56 = bf16[8,32,16,128]{3,2,1,0:T(8,128)(2,1)} custom-call(bf16[8,32,16,128]{3,2,1,0:T(8,128)(2,1)} %bitcast.33, bf16[32,512,128]{2,1,0:T(8,128)(2,1)} %bitcast.31, f32[32,1,128]{2,1,0:T(1,128)} %bitcast.38, s32[128]{0:T(128)} %select_reduce_fusion.1.slot_ref, s32[32]{0:T(128)} %reshape.79.next_ref, s32[32]{0:T(128)} %reshape.80.first_list_ref), custom_call_target="tpu_custom_call" | custom-call | tf_op jit(solution)/shard_map/pallas_call | solution.py:197
  185.3 0.0 copy-start
  185.3 1.5 copy.41
  186.8 0.3 reshape_reshape.7
  187.1 2.2 copy.37
  189.3 37.2 %all-to-all-start = ((bf16[4,16,2,4096]{3,2,0,1:T(2,128)(2,1)}), bf16[4,16,2,4096]{3,2,0,1:T(2,128)(2,1)S(1)}, u32[]{:S(2)}, u32[]{:S(2)}) async-start(bf16[4,16,2,4096]{3,2,0,1:T(2,128)(2,1)} %copy.37), calls=%async_computation | async-start | bytes 2097152 | tf_op jit(solution)/shard_map/all_to_all | solution.py:406
  226.5 0.0 copy-done
  226.5 0.1 broadcast_compare_fusion
  226.5 13.9 %all-to-all-done = bf16[4,16,2,4096]{3,2,0,1:T(2,128)(2,1)S(1)} async-done(((bf16[4,16,2,4096]{3,2,0,1:T(2,128)(2,1)}), bf16[4,16,2,4096]{3,2,0,1:T(2,128)(2,1)S(1)}, u32[]{:S(2)}, u32[]{:S(2)}) %all-to-all-start) | async-done | bytes 1048608 | tf_op jit(solution)/shard_map/all_to_all | solution.py:406
  240.5 0.8 broadcast_select_fusion
  (10 shorter events, 0.1 us)
Async XLA Ops:
  185.3 41.2 %copy-start = (s32[4]{0:T(128)S(1)}, s32[4]{0:T(128)}, u32[]{:S(2)}) copy-start(s32[4]{0:T(128)} %param.9) | copy-start | bytes 52
  189.3 51.2 %all-to-all-start = ((bf16[4,16,2,4096]{3,2,0,1:T(2,128)(2,1)}), bf16[4,16,2,4096]{3,2,0,1:T(2,128)(2,1)S(1)}, u32[]{:S(2)}, u32[]{:S(2)}) async-start(bf16[4,16,2,4096]{3,2,0,1:T(2,128)(2,1)} %copy.37), calls=%async_computation | async-start | bytes 2097152 | tf_op jit(solution)/shard_map/all_to_all | solution.py:406

commit v8 on v7

--- a/solution.py
+++ b/solution.py
@@ -383,7 +383,7 @@
     batches = features.shape[0]
     row_total = features.shape[1] * sections
     all_inputs = row_parts.transpose(1, 0, 2, 3).reshape(batches, row_total, -1)
-    piece_rows = 16
+    piece_rows = 8
     splits = row_total // piece_rows
     first_blocks = all_inputs.reshape(batches * splits, piece_rows, blocks_own, block_size)
     first_blocks = first_blocks.transpose(0, 2, 1, 3)

time: 245 us -> 229 us (0.935)
  Pallas kernels: 168 us -> 157 us
  starting transfers between devices: 37.2 us -> 31.8 us
    pallas_call x1, Pallas kernels: 144 us -> 133 us  [run_pipeline(): pl.pallas_call(functools.partial(pipeline_kernel, sections, owners, batch...]
    all_to_all x1, starting transfers between devices: 37.2 us -> 31.8 us  [body(): lax.all_to_all(outgoing_rows, 'section', split_axis=1, concat_axis=1, til...]
where the time goes in v8:
time: 229 us; the launch traced here: 225 us
  Pallas kernels  157 us (69%)
  starting transfers between devices  31.8 us (14%)
  local copies, waits for them, and re-layouts  15.9 us (7%)
  waiting for transfers between devices  13.9 us (6%)
  other arithmetic  6.16 us (3%)
    pallas_call x1, Pallas kernels, run_pipeline(): pl.pallas_call(functools.partial(pipeline_kernel, sections, owners, batch...  133 us
    all_to_all x1, starting transfers between devices, body(): lax.all_to_all(outgoing_rows, 'section', split_axis=1, concat_axis=1, til...  31.8 us
    pallas_call x1, Pallas kernels, exchange_patterns(): pl.pallas_call(functools.partial(pattern_kernel, sections, owners), out_s...  24.1 us
    all_to_all x1, waiting for transfers between devices, body(): lax.all_to_all(outgoing_rows, 'section', split_axis=1, concat_axis=1, til...  13.9 us
  transfers between devices with their start and end apart: 1, of which 1 were waited for; matrix products, arithmetic and copies ran while one was open for 0% of the time, Pallas kernels for 0%

profile of v8, /device:TPU:28, one launch (start us, length us, event | category | flops | bytes accessed | tf_op | source)
XLA Modules:
  0.0 224.9 jit_solution(16358859338422609929)
XLA Ops:
  0.0 1.4 copy.26.src_ref
  1.4 24.1 %shard_map.55 = (s32[16,32,4]{2,1,0:T(8,128)}, s32[16,32,4]{2,1,0:T(8,128)}, bf16[16,4,2,4096]{3,2,1,0:T(2,128)(2,1)}) custom-call(s32[32,4]{1,0:T(8,128)} %copy.26.src_ref, bf16[4,2,4096]{2,1,0:T(2,128)(2,1)} %feat_ref.1), custom_call_target="tpu_custom_call" | custom-call | tf_op jit(solution)/shard_map/pallas_call | solution.py:339
  25.5 1.2 copy.30
  26.8 1.2 copy.31
  28.1 2.3 %fusion = pred[2,16,512]{2,1,0:T(8,128)(4,1)S(1)} fusion(s32[2,16,128]{2,1,0:T(8,128)S(1)} %add_bitcast_fusion), kind=kLoop, calls=%fused_computation.1 | loop fusion | flops 4177920 | bytes 32768 | tf_op jit(solution)/shard_map/vmap()/reduce_or | solution.py:24
  30.4 0.2 and.22
  30.6 0.2 fusion.1
  30.7 1.2 select_reduce_fusion
  32.0 1.2 fusion.3
  33.2 0.8 copy.29
  34.0 0.1 copy.34
  34.0 0.1 squeeze.19
  34.1 0.1 add.37
  34.2 0.1 add.38
  34.3 0.1 copy.35
  34.4 0.1 and.25
  34.5 0.1 eq.43
  34.6 0.7 dynamic-slice_reduce_fusion
  35.3 0.6 reshape.79.next_ref
  35.9 0.6 reshape.80.first_list_ref
  36.6 2.3 %copy.27 = bf16[4,16,2,4096]{3,2,1,0:T(2,128)(2,1)S(1)} copy(bf16[4,16,2,4096]{3,2,0,1:T(2,128)(2,1)} %bitcast.35) | data formatting | bytes 2097152 | tf_op jit(solution)/shard_map/transpose | solution.py:385
  38.9 0.8 reshape_reshape.6
  39.7 1.4 copy.42
  41.1 0.6 select_reduce_fusion.1.slot_ref
  41.8 132.7 %shard_map.56 = bf16[16,32,8,128]{3,2,1,0:T(8,128)(2,1)} custom-call(bf16[16,32,8,128]{3,2,1,0:T(8,128)(2,1)} %bitcast.33, bf16[32,512,128]{2,1,0:T(8,128)(2,1)} %bitcast.31, f32[32,1,128]{2,1,0:T(1,128)} %bitcast.38, s32[128]{0:T(128)} %select_reduce_fusion.1.slot_ref, s32[32]{0:T(128)} %reshape.79.next_ref, s32[32]{0:T(128)} %reshape.80.first_list_ref), custom_call_target="tpu_custom_call" | custom-call | tf_op jit(solution)/shard_map/pallas_call | solution.py:197
  174.4 0.0 copy-start
  174.4 1.4 copy.41
  175.9 0.3 reshape_reshape.7
  176.2 2.2 copy.37
  178.4 31.8 %all-to-all-start = ((bf16[4,16,2,4096]{3,2,0,1:T(2,128)(2,1)}), bf16[4,16,2,4096]{3,2,0,1:T(2,128)(2,1)S(1)}, u32[]{:S(2)}, u32[]{:S(2)}) async-start(bf16[4,16,2,4096]{3,2,0,1:T(2,128)(2,1)} %copy.37), calls=%async_computation | async-start | bytes 2097152 | tf_op jit(solution)/shard_map/all_to_all | solution.py:406
  210.2 0.0 copy-done
  210.2 0.1 broadcast_compare_fusion
  210.2 13.9 %all-to-all-done = bf16[4,16,2,4096]{3,2,0,1:T(2,128)(2,1)S(1)} async-done(((bf16[4,16,2,4096]{3,2,0,1:T(2,128)(2,1)}), bf16[4,16,2,4096]{3,2,0,1:T(2,128)(2,1)S(1)}, u32[]{:S(2)}, u32[]{:S(2)}) %all-to-all-start) | async-done | bytes 1048608 | tf_op jit(solution)/shard_map/all_to_all | solution.py:406
  224.1 0.8 broadcast_select_fusion
  (10 shorter events, 0.1 us)
Async XLA Ops:
  174.4 35.7 %copy-start = (s32[4]{0:T(128)S(1)}, s32[4]{0:T(128)}, u32[]{:S(2)}) copy-start(s32[4]{0:T(128)} %param.9) | copy-start | bytes 52
  178.4 45.8 %all-to-all-start = ((bf16[4,16,2,4096]{3,2,0,1:T(2,128)(2,1)}), bf16[4,16,2,4096]{3,2,0,1:T(2,128)(2,1)S(1)}, u32[]{:S(2)}, u32[]{:S(2)}) async-start(bf16[4,16,2,4096]{3,2,0,1:T(2,128)(2,1)} %copy.37), calls=%async_computation | async-start | bytes 2097152 | tf_op jit(solution)/shard_map/all_to_all | solution.py:406

commit v9 on v8

--- a/solution.py
+++ b/solution.py
@@ -91,10 +91,9 @@
             local_sem.at[m],
         )
 
-    @pl.when(me_s == 0)
-    def _():
-        for m in range(batches):
-
+    def first_send(m):
+        @pl.when(me_s == 0)
+        def _():
             def stage_first(i, carry):
                 send0[m][i] = first_ref[m, first_list_ref[i]]
                 return carry
@@ -107,6 +106,10 @@
                     first_copy(m, d).start()
 
             first_local(m).start()
+
+    ahead = 2
+    for m in range(min(ahead, batches)):
+        first_send(m)
 
     def outgoing_copy(m, d):
         return pltpu.make_async_remote_copy(
@@ -167,6 +170,9 @@
             lax.fori_loop(0, owners * CAP, stage, 0, unroll=True)
             for d in range(owners):
                 outgoing_copy(m, d).start()
+
+        if m + ahead < batches:
+            first_send(m + ahead)
 
     @pl.when(me_s < sections - 1)
     def _():

time: 229 us -> 246 us (1.074)
  Pallas kernels: 157 us -> 175 us
    pallas_call x1, Pallas kernels: 133 us -> 151 us  [run_pipeline(): pl.pallas_call(functools.partial(pipeline_kernel, sections, owners, batch...]
where the time goes in v9:
time: 246 us; the launch traced here: 242 us
  Pallas kernels  175 us (71%)
  starting transfers between devices  30.9 us (13%)
  local copies, waits for them, and re-layouts  15.9 us (6%)
  waiting for transfers between devices  13.9 us (6%)
  other arithmetic  6.16 us (3%)
    pallas_call x1, Pallas kernels, run_pipeline(): pl.pallas_call(functools.partial(pipeline_kernel, sections, owners, batch...  151 us
    all_to_all x1, starting transfers between devices, body(): lax.all_to_all(outgoing_rows, 'section', split_axis=1, concat_axis=1, til...  30.9 us
    pallas_call x1, Pallas kernels, exchange_patterns(): pl.pallas_call(functools.partial(pattern_kernel, sections, owners), out_s...  24.1 us
    all_to_all x1, waiting for transfers between devices, body(): lax.all_to_all(outgoing_rows, 'section', split_axis=1, concat_axis=1, til...  13.9 us
  transfers between devices with their start and end apart: 1, of which 1 were waited for; matrix products, arithmetic and copies ran while one was open for 0% of the time, Pallas kernels for 0%

profile of v9, /device:TPU:28, one launch (start us, length us, event | category | flops | bytes accessed | tf_op | source)
XLA Modules:
  0.0 242.1 jit_solution(14829559866238069007)
XLA Ops:
  0.0 1.4 copy.26.src_ref
  1.4 24.1 %shard_map.55 = (s32[16,32,4]{2,1,0:T(8,128)}, s32[16,32,4]{2,1,0:T(8,128)}, bf16[16,4,2,4096]{3,2,1,0:T(2,128)(2,1)}) custom-call(s32[32,4]{1,0:T(8,128)} %copy.26.src_ref, bf16[4,2,4096]{2,1,0:T(2,128)(2,1)} %feat_ref.1), custom_call_target="tpu_custom_call" | custom-call | tf_op jit(solution)/shard_map/pallas_call | solution.py:345
  25.5 1.2 copy.30
  26.8 1.2 copy.31
  28.1 2.3 fusion
  30.4 0.2 and.22
  30.6 0.2 fusion.1
  30.7 1.2 select_reduce_fusion
  32.0 1.2 fusion.3
  33.2 0.8 copy.29
  34.0 0.1 copy.34
  34.0 0.1 squeeze.19
  34.1 0.1 add.37
  34.2 0.1 add.38
  34.3 0.1 copy.35
  34.4 0.1 and.25
  34.5 0.1 eq.43
  34.6 0.7 dynamic-slice_reduce_fusion
  35.3 0.6 reshape.79.next_ref
  35.9 0.6 reshape.80.first_list_ref
  36.6 2.3 copy.27
  38.9 0.8 reshape_reshape.6
  39.7 1.4 copy.42
  41.1 0.6 select_reduce_fusion.1.slot_ref
  41.8 150.7 %shard_map.56 = bf16[16,32,8,128]{3,2,1,0:T(8,128)(2,1)} custom-call(bf16[16,32,8,128]{3,2,1,0:T(8,128)(2,1)} %bitcast.33, bf16[32,512,128]{2,1,0:T(8,128)(2,1)} %bitcast.31, f32[32,1,128]{2,1,0:T(1,128)} %bitcast.38, s32[128]{0:T(128)} %select_reduce_fusion.1.slot_ref, s32[32]{0:T(128)} %reshape.79.next_ref, s32[32]{0:T(128)} %reshape.80.first_list_ref), custom_call_target="tpu_custom_call" | custom-call | tf_op jit(solution)/shard_map/pallas_call | solution.py:203
  192.5 0.0 copy-start
  192.5 1.4 copy.41
  194.0 0.3 reshape_reshape.7
  194.3 2.2 copy.37
  196.4 30.9 %all-to-all-start = ((bf16[4,16,2,4096]{3,2,0,1:T(2,128)(2,1)}), bf16[4,16,2,4096]{3,2,0,1:T(2,128)(2,1)S(1)}, u32[]{:S(2)}, u32[]{:S(2)}) async-start(bf16[4,16,2,4096]{3,2,0,1:T(2,128)(2,1)} %copy.37), calls=%async_computation | async-start | bytes 2097152 | tf_op jit(solution)/shard_map/all_to_all | solution.py:412
  227.4 0.0 copy-done
  227.4 0.1 broadcast_compare_fusion
  227.5 13.9 %all-to-all-done = bf16[4,16,2,4096]{3,2,0,1:T(2,128)(2,1)S(1)} async-done(((bf16[4,16,2,4096]{3,2,0,1:T(2,128)(2,1)}), bf16[4,16,2,4096]{3,2,0,1:T(2,128)(2,1)S(1)}, u32[]{:S(2)}, u32[]{:S(2)}) %all-to-all-start) | async-done | bytes 1048608 | tf_op jit(solution)/shard_map/all_to_all | solution.py:412
  241.4 0.8 broadcast_select_fusion
  (10 shorter events, 0.1 us)
Async XLA Ops:
  192.5 34.9 %copy-start = (s32[4]{0:T(128)S(1)}, s32[4]{0:T(128)}, u32[]{:S(2)}) copy-start(s32[4]{0:T(128)} %param.9) | copy-start | bytes 52
  196.4 44.9 %all-to-all-start = ((bf16[4,16,2,4096]{3,2,0,1:T(2,128)(2,1)}), bf16[4,16,2,4096]{3,2,0,1:T(2,128)(2,1)S(1)}, u32[]{:S(2)}, u32[]{:S(2)}) async-start(bf16[4,16,2,4096]{3,2,0,1:T(2,128)(2,1)} %copy.37), calls=%async_computation | async-start | bytes 2097152 | tf_op jit(solution)/shard_map/all_to_all | solution.py:412

commit v10 on v8

--- a/solution.py
+++ b/solution.py
@@ -41,9 +41,8 @@
     out_ref, *scratch,
 ):
     recv = scratch[:batches]
-    send = scratch[batches:2 * batches]
-    send0 = scratch[2 * batches:3 * batches]
-    send_sem, recv_sem, local_sem, send0_sem = scratch[3 * batches:]
+    send0 = scratch[batches:2 * batches]
+    send_sem, recv_sem, local_sem, send0_sem = scratch[2 * batches:]
     me_s = lax.axis_index("section")
     me_c = lax.axis_index("col")
     blocks_own = w_ref.shape[0]
@@ -110,7 +109,7 @@
 
     def outgoing_copy(m, d):
         return pltpu.make_async_remote_copy(
-            src_ref=send[m].at[pl.ds(d * CAP, CAP)],
+            src_ref=out_ref.at[m, pl.ds(d * CAP, CAP)],
             dst_ref=recv[m].at[pl.ds(me_c * CAP, CAP)],
             send_sem=send_sem.at[m, d],
             recv_sem=recv_sem.at[m, me_c],
@@ -140,7 +139,7 @@
         def _():
             for e in range(owners):
                 pltpu.make_async_remote_copy(
-                    src_ref=send[m].at[pl.ds(e * CAP, CAP)],
+                    src_ref=out_ref.at[m, pl.ds(e * CAP, CAP)],
                     dst_ref=recv[m].at[pl.ds(e * CAP, CAP)],
                     send_sem=send_sem.at[m, e],
                     recv_sem=recv_sem.at[m, e],
@@ -149,22 +148,19 @@
                 ).wait_recv()
 
         def block_step(j, carry):
+            block = next_ref[j]
             picked = jnp.concatenate(
-                [recv[m][slot_ref[j * nonzero_count + k]] for k in range(nonzero_count)], axis=-1
+                [recv[m][slot_ref[block * nonzero_count + k]] for k in range(nonzero_count)],
+                axis=-1,
             )
-            acc = jnp.dot(picked, w_ref[j], preferred_element_type=jnp.float32)
-            out_ref[m, j] = jnp.clip(acc + b_ref[j], 0.0, 32.0).astype(out_ref.dtype)
+            acc = jnp.dot(picked, w_ref[block], preferred_element_type=jnp.float32)
+            out_ref[m, j] = jnp.clip(acc + b_ref[block], 0.0, 32.0).astype(out_ref.dtype)
             return carry
 
         lax.fori_loop(0, blocks_own, block_step, 0, unroll=True)
 
         @pl.when(me_s < sections - 1)
         def _():
-            def stage(i, carry):
-                send[m][i] = out_ref[m, next_ref[i]]
-                return carry
-
-            lax.fori_loop(0, owners * CAP, stage, 0, unroll=True)
             for d in range(owners):
                 outgoing_copy(m, d).start()
 
@@ -200,7 +196,7 @@
         in_specs=[vmem, vmem, vmem, smem, smem, smem],
         out_specs=vmem,
         scratch_shapes=[
-            *[pltpu.VMEM(slots_shape, jnp.bfloat16) for _ in range(3 * batches)],
+            *[pltpu.VMEM(slots_shape, jnp.bfloat16) for _ in range(2 * batches)],
             pltpu.SemaphoreType.DMA((batches, owners)),
             pltpu.SemaphoreType.DMA((batches, owners)),
             pltpu.SemaphoreType.DMA((batches,)),
@@ -370,7 +366,11 @@
     outgoing = lax.dynamic_index_in_dim(positions, col_idx, 1, keepdims=False)
     outgoing = outgoing.reshape(owners * CAP)
     outgoing_next = lax.dynamic_index_in_dim(both_positions[1], col_idx, 1, keepdims=False)
-    outgoing_next = outgoing_next.reshape(owners * CAP)
+    outgoing_next = jnp.where(
+        section_idx == sections - 1,
+        jnp.arange(owners * CAP, dtype=jnp.int32),
+        outgoing_next.reshape(owners * CAP),
+    )
     incoming = lax.dynamic_index_in_dim(positions, col_idx, 0, keepdims=False)
     incoming_ok = lax.dynamic_index_in_dim(present, col_idx, 0, keepdims=False)
     global_ids = incoming + blocks_own * jnp.arange(owners, dtype=jnp.int32)[:, None]

time: 229 us -> 229 us (level)
  no operation moved by 1% of the time
where the time goes in v10:
time: 229 us; the launch traced here: 225 us
  Pallas kernels  157 us (69%)
  starting transfers between devices  31.3 us (14%)
  local copies, waits for them, and re-layouts  15.4 us (7%)
  waiting for transfers between devices  13.9 us (6%)
  other arithmetic  6.7 us (3%)
    pallas_call x1, Pallas kernels, run_pipeline(): pl.pallas_call(functools.partial(pipeline_kernel, sections, owners, batch...  133 us
    all_to_all x1, starting transfers between devices, body(): lax.all_to_all(outgoing_rows, 'section', split_axis=1, concat_axis=1, til...  31.3 us
    pallas_call x1, Pallas kernels, exchange_patterns(): pl.pallas_call(functools.partial(pattern_kernel, sections, owners), out_s...  24.1 us
    all_to_all x1, waiting for transfers between devices, body(): lax.all_to_all(outgoing_rows, 'section', split_axis=1, concat_axis=1, til...  13.9 us
  transfers between devices with their start and end apart: 1, of which 1 were waited for; matrix products, arithmetic and copies ran while one was open for 0% of the time, Pallas kernels for 0%

profile of v10, /device:TPU:28, one launch (start us, length us, event | category | flops | bytes accessed | tf_op | source)
XLA Modules:
  0.0 224.5 jit_solution(785534433102747601)
XLA Ops:
  0.0 1.4 copy.26.src_ref
  1.4 24.1 %shard_map.55 = (s32[16,32,4]{2,1,0:T(8,128)}, s32[16,32,4]{2,1,0:T(8,128)}, bf16[16,4,2,4096]{3,2,1,0:T(2,128)(2,1)}) custom-call(s32[32,4]{1,0:T(8,128)} %copy.26.src_ref, bf16[4,2,4096]{2,1,0:T(2,128)(2,1)} %feat_ref.1), custom_call_target="tpu_custom_call" | custom-call | tf_op jit(solution)/shard_map/pallas_call | solution.py:335
  25.5 1.2 copy.30
  26.8 1.2 copy.31
  28.1 2.3 %fusion = pred[2,16,512]{2,1,0:T(8,128)(4,1)S(1)} fusion(s32[2,16,128]{2,1,0:T(8,128)S(1)} %add_bitcast_fusion), kind=kLoop, calls=%fused_computation.1 | loop fusion | flops 4177920 | bytes 32768 | tf_op jit(solution)/shard_map/vmap()/reduce_or | solution.py:24
  30.4 0.2 and.22
  30.6 0.2 fusion.1
  30.7 1.2 select_reduce_fusion
  32.0 1.2 fusion.3
  33.2 0.8 copy.29
  34.0 0.1 copy.34
  34.0 0.1 squeeze.19
  34.1 0.1 add.37
  34.2 0.1 add.38
  34.3 0.1 copy.35
  34.4 0.1 and.25
  34.5 0.1 eq.46
  34.6 0.7 dynamic-slice_reduce_fusion
  35.3 0.1 reshape.79
  35.4 0.6 reshape.80.first_list_ref
  36.0 2.3 %copy.27 = bf16[4,16,2,4096]{3,2,1,0:T(2,128)(2,1)S(1)} copy(bf16[4,16,2,4096]{3,2,0,1:T(2,128)(2,1)} %bitcast.35) | data formatting | bytes 2097152 | tf_op jit(solution)/shard_map/transpose | solution.py:385
  38.3 0.8 reshape_reshape.6
  39.2 1.4 copy.42
  40.6 0.5 broadcast_select_fusion.1.next_ref
  41.2 0.6 select_reduce_fusion.1.slot_ref
  41.8 132.8 %shard_map.56 = bf16[16,32,8,128]{3,2,1,0:T(8,128)(2,1)} custom-call(bf16[16,32,8,128]{3,2,1,0:T(8,128)(2,1)} %bitcast.33, bf16[32,512,128]{2,1,0:T(8,128)(2,1)} %bitcast.31, f32[32,1,128]{2,1,0:T(1,128)} %bitcast.38, s32[128]{0:T(128)} %select_reduce_fusion.1.slot_ref, s32[32]{0:T(128)} %broadcast_select_fusion.1.next_ref, s32[32]{0:T(128)} %reshape.80.first_list_ref), custom_call_target="tpu_custom_call" | custom-call | tf_op jit(solution)/shard_map/pallas_call | solution.py:193
  174.6 0.0 copy-start
  174.6 1.4 copy.41
  176.0 0.3 reshape_reshape.7
  176.3 2.2 copy.37
  178.5 31.3 %all-to-all-start = ((bf16[4,16,2,4096]{3,2,0,1:T(2,128)(2,1)}), bf16[4,16,2,4096]{3,2,0,1:T(2,128)(2,1)S(1)}, u32[]{:S(2)}, u32[]{:S(2)}) async-start(bf16[4,16,2,4096]{3,2,0,1:T(2,128)(2,1)} %copy.37), calls=%async_computation | async-start | bytes 2097152 | tf_op jit(solution)/shard_map/all_to_all | solution.py:406
  209.8 0.0 copy-done
  209.8 0.1 broadcast_compare_fusion
  209.8 13.9 %all-to-all-done = bf16[4,16,2,4096]{3,2,0,1:T(2,128)(2,1)S(1)} async-done(((bf16[4,16,2,4096]{3,2,0,1:T(2,128)(2,1)}), bf16[4,16,2,4096]{3,2,0,1:T(2,128)(2,1)S(1)}, u32[]{:S(2)}, u32[]{:S(2)}) %all-to-all-start) | async-done | bytes 1048608 | tf_op jit(solution)/shard_map/all_to_all | solution.py:406
  223.8 0.8 broadcast_select_fusion
  (10 shorter events, 0.1 us)
Async XLA Ops:
  174.6 35.2 %copy-start = (s32[4]{0:T(128)S(1)}, s32[4]{0:T(128)}, u32[]{:S(2)}) copy-start(s32[4]{0:T(128)} %param.9) | copy-start | bytes 52
  178.5 45.3 %all-to-all-start = ((bf16[4,16,2,4096]{3,2,0,1:T(2,128)(2,1)}), bf16[4,16,2,4096]{3,2,0,1:T(2,128)(2,1)S(1)}, u32[]{:S(2)}, u32[]{:S(2)}) async-start(bf16[4,16,2,4096]{3,2,0,1:T(2,128)(2,1)} %copy.37), calls=%async_computation | async-start | bytes 2097152 | tf_op jit(solution)/shard_map/all_to_all | solution.py:406

commit v11 on v10

--- a/solution.py
+++ b/solution.py
@@ -346,6 +346,65 @@
         ],
         compiler_params=pltpu.CompilerParams(collective_id=1, has_side_effects=True),
     )(local_sources, features)
+
+
+def rows_kernel(sections, src_ref, out_ref, send_sem, recv_sem, local_sem):
+    me_s = lax.axis_index("section")
+    me_c = lax.axis_index("col")
+    last = sections - 1
+    barrier = pltpu.get_barrier_semaphore()
+
+    @pl.when(me_s == last)
+    def _():
+        for r in range(last):
+            pl.semaphore_signal(barrier, inc=1, device_id=(r, me_c), device_id_type=MESH_ID)
+
+    @pl.when(me_s != last)
+    def _():
+        pl.semaphore_signal(barrier, inc=1, device_id=(last, me_c), device_id_type=MESH_ID)
+
+    is_last = (me_s == last).astype(jnp.int32)
+    pl.semaphore_wait(barrier, is_last * last + (1 - is_last))
+
+    def row_copy(r):
+        return pltpu.make_async_remote_copy(
+            src_ref=src_ref.at[r],
+            dst_ref=out_ref,
+            send_sem=send_sem.at[r],
+            recv_sem=recv_sem,
+            device_id=(r, me_c),
+            device_id_type=MESH_ID,
+        )
+
+    @pl.when(me_s == last)
+    def _():
+        for r in range(last):
+            row_copy(r).start()
+        mine = pltpu.make_async_copy(src_ref.at[last], out_ref, local_sem)
+        mine.start()
+        mine.wait()
+        for r in range(last):
+            row_copy(r).wait_send()
+
+    @pl.when(me_s != last)
+    def _():
+        row_copy(0).wait_recv()
+
+
+def deliver_rows(row_parts, sections):
+    anywhere = pl.BlockSpec(memory_space=pl.ANY)
+    return pl.pallas_call(
+        functools.partial(rows_kernel, sections),
+        out_shape=jax.ShapeDtypeStruct(row_parts.shape[1:], row_parts.dtype),
+        in_specs=[anywhere],
+        out_specs=anywhere,
+        scratch_shapes=[
+            pltpu.SemaphoreType.DMA((sections,)),
+            pltpu.SemaphoreType.DMA(()),
+            pltpu.SemaphoreType.DMA(()),
+        ],
+        compiler_params=pltpu.CompilerParams(collective_id=2, has_side_effects=True),
+    )(row_parts)
 
 
 def body(features, weights, sources, bias, batch_rows):
@@ -403,8 +462,7 @@
     )
     own_rows = row_total // sections
     outgoing_rows = completed.reshape(batches, sections, own_rows, blocks_own * block_size)
-    gathered = lax.all_to_all(outgoing_rows, "section", split_axis=1, concat_axis=1, tiled=True)
-    own_result = gathered[:, sections - 1]
+    own_result = deliver_rows(outgoing_rows.transpose(1, 0, 2, 3), sections)
     row_ids = section_idx * own_rows + jnp.arange(own_rows, dtype=jnp.int32)
     row_mask = row_ids[None, :] < batch_rows[:, None]
     return jnp.where(row_mask[:, :, None], own_result, jnp.zeros_like(own_result))

time: 229 us -> 221 us (0.965); the launches traced: 225 us -> 221 us
  Pallas kernels: 157 us -> 197 us
  starting transfers between devices: 31.3 us -> 0 us
  waiting for transfers between devices: 13.9 us -> 0 us
    pallas_call x0 -> x1, Pallas kernels: none -> 40.7 us  [deliver_rows(): pl.pallas_call(functools.partial(rows_kernel, sections), out_shape=jax.Sh...]
    all_to_all x1 -> x0, starting transfers between devices: 31.3 us -> none  [body(): lax.all_to_all(outgoing_rows, 'section', split_axis=1, concat_axis=1, til...]
    all_to_all x1 -> x0, waiting for transfers between devices: 13.9 us -> none  [body(): lax.all_to_all(outgoing_rows, 'section', split_axis=1, concat_axis=1, til...]
  transfers between devices with their start and end apart: 1 -> 0, of which waited for: 1 -> 0; matrix products, arithmetic and copies ran while one was open for 0% -> 0% of each run, Pallas kernels for 0% -> 0%
where the time goes in v11:
time: 221 us
  Pallas kernels  197 us (89%)
  local copies, waits for them, and re-layouts  15.4 us (7%)
  other arithmetic  7.52 us (3%)
    pallas_call x1, Pallas kernels, run_pipeline(): pl.pallas_call(functools.partial(pipeline_kernel, sections, owners, batch...  133 us
    pallas_call x1, Pallas kernels, deliver_rows(): pl.pallas_call(functools.partial(rows_kernel, sections), out_shape=jax.Sh...  40.7 us
    pallas_call x1, Pallas kernels, exchange_patterns(): pl.pallas_call(functools.partial(pattern_kernel, sections, owners), out_s...  24.1 us

profile of v11, /device:TPU:28, one launch (start us, length us, event | category | flops | bytes accessed | tf_op | source)
XLA Modules:
  0.0 220.6 jit_solution(1097337589663916154)
XLA Ops:
  0.0 1.4 copy.27.src_ref
  1.4 24.1 %shard_map.55 = (s32[16,32,4]{2,1,0:T(8,128)}, s32[16,32,4]{2,1,0:T(8,128)}, bf16[16,4,2,4096]{3,2,1,0:T(2,128)(2,1)}) custom-call(s32[32,4]{1,0:T(8,128)} %copy.27.src_ref, bf16[4,2,4096]{2,1,0:T(2,128)(2,1)} %feat_ref.1), custom_call_target="tpu_custom_call" | custom-call | tf_op jit(solution)/shard_map/pallas_call | solution.py:335
  25.5 1.2 copy.31
  26.8 1.2 copy.32
  28.1 2.3 %fusion = pred[2,16,512]{2,1,0:T(8,128)(4,1)S(1)} fusion(s32[2,16,128]{2,1,0:T(8,128)S(1)} %add_bitcast_fusion), kind=kLoop, calls=%fused_computation.1 | loop fusion | flops 4177920 | bytes 32768 | tf_op jit(solution)/shard_map/vmap()/reduce_or | solution.py:24
  30.4 0.2 and.22
  30.6 0.2 fusion.1
  30.7 1.2 select_reduce_fusion
  32.0 0.1 copy.35
  32.1 0.1 squeeze.16
  32.2 0.1 add.37
  32.2 0.1 add.38
  32.3 1.2 fusion.3
  33.6 0.1 copy.36
  33.7 0.1 and.25
  33.8 0.8 copy.30
  34.6 0.1 eq.46
  34.7 0.6 select_reduce_fusion.1.slot_ref
  35.3 0.7 dynamic-slice_reduce_fusion
  36.0 0.1 reshape.79
  36.1 0.5 broadcast_select_fusion.1.next_ref
  36.6 0.6 reshape.80.first_list_ref
  37.2 2.3 %copy.28 = bf16[4,16,2,4096]{3,2,1,0:T(2,128)(2,1)S(1)} copy(bf16[4,16,2,4096]{3,2,0,1:T(2,128)(2,1)} %bitcast.35) | data formatting | bytes 2097152 | tf_op jit(solution)/shard_map/transpose | solution.py:444
  39.5 0.8 reshape_reshape.6
  40.4 1.4 copy.45
  41.8 132.5 %shard_map.56 = bf16[16,32,8,128]{3,2,1,0:T(8,128)(2,1)} custom-call(bf16[16,32,8,128]{3,2,1,0:T(8,128)(2,1)} %bitcast.33, bf16[32,512,128]{2,1,0:T(8,128)(2,1)} %bitcast.30, f32[32,1,128]{2,1,0:T(1,128)} %bitcast.38, s32[128]{0:T(128)} %select_reduce_fusion.1.slot_ref, s32[32]{0:T(128)} %broadcast_select_fusion.1.next_ref, s32[32]{0:T(128)} %reshape.80.first_list_ref), custom_call_target="tpu_custom_call" | custom-call | tf_op jit(solution)/shard_map/pallas_call | solution.py:193
  174.3 0.0 copy-start
  174.3 1.4 copy.44
  175.8 0.3 reshape_reshape.7
  176.1 2.2 copy.43
  178.2 40.7 %shard_map.57 = bf16[4,2,4096]{2,1,0:T(2,128)(2,1)} custom-call(bf16[16,4,2,4096]{3,2,1,0:T(2,128)(2,1)} %bitcast.32), custom_call_target="tpu_custom_call" | custom-call | tf_op jit(solution)/shard_map/pallas_call | solution.py:396
  218.9 0.0 copy-done
  219.0 0.1 broadcast_compare_fusion
  219.0 1.6 broadcast_select_fusion
  (10 shorter events, 0.2 us)
Async XLA Ops:
  174.3 44.7 %copy-start = (s32[4]{0:T(128)S(1)}, s32[4]{0:T(128)}, u32[]{:S(2)}) copy-start(s32[4]{0:T(128)} %param.9) | copy-start | bytes 52

commit v12 on v11

--- a/solution.py
+++ b/solution.py
@@ -9,31 +9,6 @@
 
 CAP = 2
 MESH_ID = pl.DeviceIdType.MESH
-
-
-def from_behind(x, axis, by):
-    size = lax.axis_size(axis)
-    pairs = [(i, i + by) for i in range(size) if 0 <= i + by < size]
-    return lax.ppermute(x, axis, pairs)
-
-
-def request_lists(pattern_table, owners, blocks_own, slot_total):
-    dest_entries = pattern_table.reshape(owners, -1)
-    block_total = owners * blocks_own
-    catalog = jnp.arange(block_total, dtype=jnp.int32)
-    wanted = jnp.any(dest_entries[:, :, None] == catalog[None, None, :], axis=1)
-    wanted = wanted.reshape(owners, owners, blocks_own)
-    local_rows = jnp.arange(blocks_own, dtype=jnp.int32)
-    below = local_rows[:, None] <= local_rows[None, :]
-    block_ranks = jnp.einsum(
-        "abi,ij->abj", wanted.astype(jnp.float32), below.astype(jnp.float32)
-    ).astype(jnp.int32) - 1
-    slot_ids = jnp.arange(slot_total, dtype=jnp.int32)
-    chosen = wanted[:, :, None, :] & (block_ranks[:, :, None, :] == slot_ids[None, None, :, None])
-    local_ids = jnp.arange(blocks_own, dtype=jnp.int32)
-    positions = jnp.sum(chosen.astype(jnp.int32) * local_ids[None, None, None, :], axis=3)
-    present = jnp.any(chosen, axis=3)
-    return (positions, present)
 
 
 def pipeline_kernel(
@@ -418,26 +393,33 @@
     block_size = local_w.shape[2]
     local_src = sources[0].reshape(blocks_own * nonzero_count)
     own_table, next_table, row_parts = exchange_patterns(sources[0], features, sections, owners)
-    both_positions, both_present = jax.vmap(
-        lambda table: request_lists(table, owners, blocks_own, CAP)
-    )(jnp.stack([own_table, next_table]))
-    positions, present = both_positions[0], both_present[0]
-    outgoing = lax.dynamic_index_in_dim(positions, col_idx, 1, keepdims=False)
-    outgoing = outgoing.reshape(owners * CAP)
-    outgoing_next = lax.dynamic_index_in_dim(both_positions[1], col_idx, 1, keepdims=False)
+    local_rows = jnp.arange(blocks_own, dtype=jnp.int32)
+    below = (local_rows[:, None] <= local_rows[None, :]).astype(jnp.float32)
+    slot_ids = jnp.arange(CAP, dtype=jnp.int32)
+
+    def ranks_of(wanted):
+        return jnp.einsum("...i,ij->...j", wanted.astype(jnp.float32), below).astype(jnp.int32) - 1
+
+    def sender_list(table):
+        flat = table.reshape(owners, blocks_own * nonzero_count)
+        mine = col_idx * blocks_own + local_rows
+        wanted = jnp.any(flat[:, :, None] == mine[None, None, :], axis=1)
+        chosen = wanted[:, None, :] & (ranks_of(wanted)[:, None, :] == slot_ids[None, :, None])
+        return jnp.sum(chosen.astype(jnp.int32) * local_rows[None, None, :], axis=2)
+
+    both_lists = jax.vmap(sender_list)(jnp.stack([own_table, next_table]))
+    outgoing = both_lists[0].reshape(owners * CAP)
     outgoing_next = jnp.where(
         section_idx == sections - 1,
         jnp.arange(owners * CAP, dtype=jnp.int32),
-        outgoing_next.reshape(owners * CAP),
+        both_lists[1].reshape(owners * CAP),
     )
-    incoming = lax.dynamic_index_in_dim(positions, col_idx, 0, keepdims=False)
-    incoming_ok = lax.dynamic_index_in_dim(present, col_idx, 0, keepdims=False)
-    global_ids = incoming + blocks_own * jnp.arange(owners, dtype=jnp.int32)[:, None]
-    matches = (local_src[:, None] == global_ids.reshape(-1)[None, :]) & incoming_ok.reshape(-1)[
-        None, :
-    ]
+    catalog = jnp.arange(owners * blocks_own, dtype=jnp.int32)
+    requested = jnp.any(local_src[:, None] == catalog[None, :], axis=0).reshape(owners, blocks_own)
+    slot_table = jnp.arange(owners, dtype=jnp.int32)[:, None] * CAP + ranks_of(requested)
     slot_of = jnp.sum(
-        matches.astype(jnp.int32) * jnp.arange(owners * CAP, dtype=jnp.int32)[None, :], axis=1
+        (local_src[:, None] == catalog[None, :]).astype(jnp.int32) * slot_table.reshape(-1)[None, :],
+        axis=1,
     )
     batches = features.shape[0]
     row_total = features.shape[1] * sections

time: 221 us -> 213 us (0.964)
  other arithmetic: 7.52 us -> 3.9 us
    reduce_or x2, other arithmetic: 3.5 us -> 0.84 us  [the longest x1 0.72 us: sender_list(): wanted = jnp.any(flat[:, :, None] == mine[None, None, :], axis=1)]
where the time goes in v12:
time: 213 us
  Pallas kernels  195 us (92%)
  local copies, waits for them, and re-layouts  13.8 us (6%)
  other arithmetic  3.9 us (2%)
    pallas_call x1, Pallas kernels, run_pipeline(): pl.pallas_call(functools.partial(pipeline_kernel, sections, owners, batch...  132 us
    pallas_call x1, Pallas kernels, deliver_rows(): pl.pallas_call(functools.partial(rows_kernel, sections), out_shape=jax.Sh...  38.7 us
    pallas_call x1, Pallas kernels, exchange_patterns(): pl.pallas_call(functools.partial(pattern_kernel, sections, owners), out_s...  24.1 us

profile of v12, /device:TPU:28, one launch (start us, length us, event | category | flops | bytes accessed | tf_op | source)
XLA Modules:
  0.0 212.6 jit_solution(11449303278479260970)
XLA Ops:
  0.0 0.0 copy-start
  0.0 1.4 copy.27.src_ref
  1.4 24.1 %shard_map.55 = (s32[16,32,4]{2,1,0:T(8,128)}, s32[16,32,4]{2,1,0:T(8,128)}, bf16[16,4,2,4096]{3,2,1,0:T(2,128)(2,1)}) custom-call(s32[32,4]{1,0:T(8,128)} %copy.27.src_ref, bf16[4,2,4096]{2,1,0:T(2,128)(2,1)} %feat_ref.1), custom_call_target="tpu_custom_call" | custom-call | tf_op jit(solution)/shard_map/pallas_call | solution.py:310
  25.6 1.2 copy.31
  26.9 1.2 copy.32
  28.2 0.7 compare_reduce_fusion
  28.9 0.1 fusion
  29.0 0.2 select_reduce_fusion.1
  29.2 0.1 copy.35
  29.3 0.1 reshape_squeeze.14
  29.4 0.5 broadcast_select_fusion.1.next_ref
  29.9 0.1 copy.36
  30.0 0.6 reshape_squeeze.15.first_list_ref
  30.6 2.3 %copy.28 = bf16[4,16,2,4096]{3,2,1,0:T(2,128)(2,1)S(1)} copy(bf16[4,16,2,4096]{3,2,0,1:T(2,128)(2,1)} %bitcast.30) | data formatting | bytes 2097152 | tf_op jit(solution)/shard_map/transpose | solution.py:426
  32.9 0.8 reshape_reshape.6
  33.8 1.4 copy.44
  35.2 0.0 copy-done
  35.2 0.1 copy.30
  35.3 0.1 eq.24
  35.4 0.1 fusion.3
  35.5 0.1 reshape.56
  35.6 0.1 fusion.2
  35.7 0.1 mul.34
  35.8 0.7 select_reduce_fusion.slot_ref
  36.5 131.7 %shard_map.56 = bf16[16,32,8,128]{3,2,1,0:T(8,128)(2,1)} custom-call(bf16[16,32,8,128]{3,2,1,0:T(8,128)(2,1)} %bitcast.28, bf16[32,512,128]{2,1,0:T(8,128)(2,1)} %bitcast.25, f32[32,1,128]{2,1,0:T(1,128)} %bitcast.33, s32[128]{0:T(128)} %select_reduce_fusion.slot_ref, s32[32]{0:T(128)} %broadcast_select_fusion.1.next_ref, s32[32]{0:T(128)} %reshape_squeeze.15.first_list_ref), custom_call_target="tpu_custom_call" | custom-call | tf_op jit(solution)/shard_map/pallas_call | solution.py:168
  168.2 0.0 copy-start.1
  168.3 1.4 copy.43
  169.7 0.3 reshape_reshape.7
  170.0 2.2 %copy.42 = bf16[4,16,2,4096]{3,2,0,1:T(2,128)(2,1)} copy(bf16[4,16,2,4096]{3,2,1,0:T(2,128)(2,1)S(1)} %reshape_reshape.7) | data formatting | bytes 2097152 | tf_op jit(solution)/shard_map/reshape;reshape | solution.py:446
  172.2 38.7 %shard_map.57 = bf16[4,2,4096]{2,1,0:T(2,128)(2,1)} custom-call(bf16[16,4,2,4096]{3,2,1,0:T(2,128)(2,1)} %bitcast.27), custom_call_target="tpu_custom_call" | custom-call | tf_op jit(solution)/shard_map/pallas_call | solution.py:371
  210.9 0.0 copy-done.1
  210.9 0.1 broadcast_compare_fusion
  211.0 1.6 broadcast_select_fusion
  (7 shorter events, 0.1 us)
Async XLA Ops:
  0.0 35.2 %copy-start = (s32[1,32,4]{1,2,0:T(4,128)S(1)}, s32[1,32,4]{1,2,0:T(4,128)}, u32[]{:S(2)}) copy-start(s32[1,32,4]{1,2,0:T(4,128)} %param.7) | copy-start | bytes 1540
  168.2 42.6 %copy-start.1 = (s32[4]{0:T(128)S(1)}, s32[4]{0:T(128)}, u32[]{:S(2)}) copy-start(s32[4]{0:T(128)} %param.9) | copy-start | bytes 52

commit v13 on v12

--- a/solution.py
+++ b/solution.py
@@ -288,14 +288,9 @@
         for e in range(owners):
             nxt_copy(me_s + 1, e, e).wait_recv()
 
-    @pl.when(me_s == sections - 1)
-    def _():
-        nxt_ref[...] = jnp.zeros_like(nxt_ref)
-
     @pl.when(me_s > 0)
     def _():
         rows_copy(me_s).wait_send()
-        rows_ref[...] = jnp.zeros_like(rows_ref)
 
     @pl.when(me_s == 0)
     def _():
@@ -306,12 +301,12 @@
 def exchange_patterns(local_sources, features, sections, owners):
     table = jax.ShapeDtypeStruct((owners,) + local_sources.shape, local_sources.dtype)
     rows = jax.ShapeDtypeStruct((sections,) + features.shape, features.dtype)
-    vmem = pl.BlockSpec(memory_space=pltpu.VMEM)
+    anywhere = pl.BlockSpec(memory_space=pl.ANY)
     return pl.pallas_call(
         functools.partial(pattern_kernel, sections, owners),
         out_shape=(table, table, rows),
-        in_specs=[vmem, vmem],
-        out_specs=(vmem, vmem, vmem),
+        in_specs=[anywhere, anywhere],
+        out_specs=(anywhere, anywhere, anywhere),
         scratch_shapes=[pltpu.SemaphoreType.DMA((owners,)) for _ in range(4)]
         + [
             pltpu.SemaphoreType.DMA(()),

time: 213 us -> 212 us (level)
  no operation moved by 1% of the time
where the time goes in v13:
time: 212 us; the launch traced here: 211 us
  Pallas kernels  193 us (91%)
  local copies, waits for them, and re-layouts  13.8 us (7%)
  other arithmetic  3.9 us (2%)
    pallas_call x1, Pallas kernels, run_pipeline(): pl.pallas_call(functools.partial(pipeline_kernel, sections, owners, batch...  133 us
    pallas_call x1, Pallas kernels, deliver_rows(): pl.pallas_call(functools.partial(rows_kernel, sections), out_shape=jax.Sh...  38.4 us
    pallas_call x1, Pallas kernels, exchange_patterns(): pl.pallas_call(functools.partial(pattern_kernel, sections, owners), out_s...  22.3 us

profile of v13, /device:TPU:28, one launch (start us, length us, event | category | flops | bytes accessed | tf_op | source)
XLA Modules:
  0.0 211.4 jit_solution(5693374409943021143)
XLA Ops:
  0.0 0.0 copy-start
  0.0 1.4 copy.27.src_ref
  1.4 22.3 %shard_map.55 = (s32[16,32,4]{2,1,0:T(8,128)}, s32[16,32,4]{2,1,0:T(8,128)}, bf16[16,4,2,4096]{3,2,1,0:T(2,128)(2,1)}) custom-call(s32[32,4]{1,0:T(8,128)} %copy.27.src_ref, bf16[4,2,4096]{2,1,0:T(2,128)(2,1)} %feat_ref.1), custom_call_target="tpu_custom_call" | custom-call | tf_op jit(solution)/shard_map/pallas_call | solution.py:305
  23.8 1.2 copy.31
  25.0 1.2 copy.32
  26.3 0.7 compare_reduce_fusion
  27.1 0.1 fusion
  27.2 0.2 select_reduce_fusion.1
  27.4 0.1 copy.35
  27.4 0.1 reshape_squeeze.14
  27.5 0.5 broadcast_select_fusion.1.next_ref
  28.1 0.1 copy.36
  28.1 0.6 reshape_squeeze.15.first_list_ref
  28.8 2.3 %copy.28 = bf16[4,16,2,4096]{3,2,1,0:T(2,128)(2,1)S(1)} copy(bf16[4,16,2,4096]{3,2,0,1:T(2,128)(2,1)} %bitcast.30) | data formatting | bytes 2097152 | tf_op jit(solution)/shard_map/transpose | solution.py:421
  31.1 0.8 reshape_reshape.6
  31.9 1.4 copy.44
  33.4 0.0 copy-done
  33.4 0.1 copy.30
  33.4 0.1 eq.24
  33.6 0.1 fusion.3
  33.7 0.1 reshape.56
  33.8 0.1 fusion.2
  33.8 0.1 mul.34
  34.0 0.7 select_reduce_fusion.slot_ref
  34.7 132.8 %shard_map.56 = bf16[16,32,8,128]{3,2,1,0:T(8,128)(2,1)} custom-call(bf16[16,32,8,128]{3,2,1,0:T(8,128)(2,1)} %bitcast.28, bf16[32,512,128]{2,1,0:T(8,128)(2,1)} %bitcast.25, f32[32,1,128]{2,1,0:T(1,128)} %bitcast.33, s32[128]{0:T(128)} %select_reduce_fusion.slot_ref, s32[32]{0:T(128)} %broadcast_select_fusion.1.next_ref, s32[32]{0:T(128)} %reshape_squeeze.15.first_list_ref), custom_call_target="tpu_custom_call" | custom-call | tf_op jit(solution)/shard_map/pallas_call | solution.py:168
  167.5 0.0 copy-start.1
  167.5 1.4 copy.43
  168.9 0.3 reshape_reshape.7
  169.2 2.2 %copy.42 = bf16[4,16,2,4096]{3,2,0,1:T(2,128)(2,1)} copy(bf16[4,16,2,4096]{3,2,1,0:T(2,128)(2,1)S(1)} %reshape_reshape.7) | data formatting | bytes 2097152 | tf_op jit(solution)/shard_map/reshape;reshape | solution.py:441
  171.4 38.4 %shard_map.57 = bf16[4,2,4096]{2,1,0:T(2,128)(2,1)} custom-call(bf16[16,4,2,4096]{3,2,1,0:T(2,128)(2,1)} %bitcast.27), custom_call_target="tpu_custom_call" | custom-call | tf_op jit(solution)/shard_map/pallas_call | solution.py:366
  209.8 0.0 copy-done.1
  209.8 0.1 broadcast_compare_fusion
  209.9 1.6 broadcast_select_fusion
  (7 shorter events, 0.1 us)
Async XLA Ops:
  0.0 33.4 %copy-start = (s32[1,32,4]{1,2,0:T(4,128)S(1)}, s32[1,32,4]{1,2,0:T(4,128)}, u32[]{:S(2)}) copy-start(s32[1,32,4]{1,2,0:T(4,128)} %param.7) | copy-start | bytes 1540
  167.5 42.3 %copy-start.1 = (s32[4]{0:T(128)S(1)}, s32[4]{0:T(128)}, u32[]{:S(2)}) copy-start(s32[4]{0:T(128)} %param.9) | copy-start | bytes 52

commit v14 on v13

--- a/solution.py
+++ b/solution.py
@@ -251,7 +251,7 @@
     def rows_copy(r):
         return pltpu.make_async_remote_copy(
             src_ref=feat_ref,
-            dst_ref=rows_ref.at[r],
+            dst_ref=rows_ref.at[:, r],
             send_sem=rows_send,
             recv_sem=rows_recv.at[r],
             device_id=(0, me_c),
@@ -264,7 +264,7 @@
 
     @pl.when(me_s == 0)
     def _():
-        own_rows = pltpu.make_async_copy(feat_ref, rows_ref.at[0], rows_sem)
+        own_rows = pltpu.make_async_copy(feat_ref, rows_ref.at[:, 0], rows_sem)
         own_rows.start()
         own_rows.wait()
 
@@ -300,7 +300,9 @@
 
 def exchange_patterns(local_sources, features, sections, owners):
     table = jax.ShapeDtypeStruct((owners,) + local_sources.shape, local_sources.dtype)
-    rows = jax.ShapeDtypeStruct((sections,) + features.shape, features.dtype)
+    rows = jax.ShapeDtypeStruct(
+        (features.shape[0], sections) + features.shape[1:], features.dtype
+    )
     anywhere = pl.BlockSpec(memory_space=pl.ANY)
     return pl.pallas_call(
         functools.partial(pattern_kernel, sections, owners),
@@ -418,7 +420,7 @@
     )
     batches = features.shape[0]
     row_total = features.shape[1] * sections
-    all_inputs = row_parts.transpose(1, 0, 2, 3).reshape(batches, row_total, -1)
+    all_inputs = row_parts.reshape(batches, row_total, -1)
     piece_rows = 8
     splits = row_total // piece_rows
     first_blocks = all_inputs.reshape(batches * splits, piece_rows, blocks_own, block_size)

time: 212 us -> 211 us (level)
    transpose x1 -> x0, local copies, waits for them, and re-layouts: 2.31 us -> none  [body(): all_inputs = row_parts.transpose(1, 0, 2, 3).reshape(batches, row_total, -1)]
where the time goes in v14:
time: 211 us
  Pallas kernels  194 us (92%)
  local copies, waits for them, and re-layouts  12.5 us (6%)
  other arithmetic  3.9 us (2%)
    pallas_call x1, Pallas kernels, run_pipeline(): pl.pallas_call(functools.partial(pipeline_kernel, sections, owners, batch...  133 us
    pallas_call x1, Pallas kernels, deliver_rows(): pl.pallas_call(functools.partial(rows_kernel, sections), out_shape=jax.Sh...  39.2 us
    pallas_call x1, Pallas kernels, exchange_patterns(): pl.pallas_call(functools.partial(pattern_kernel, sections, owners), out_s...  22.3 us

profile of v14, /device:TPU:28, one launch (start us, length us, event | category | flops | bytes accessed | tf_op | source)
XLA Modules:
  0.0 211.1 jit_solution(7522234676038934376)
XLA Ops:
  0.0 0.0 copy-start
  0.0 1.4 copy.25.src_ref
  1.4 22.3 %shard_map.55 = (s32[16,32,4]{2,1,0:T(8,128)}, s32[16,32,4]{2,1,0:T(8,128)}, bf16[4,16,2,4096]{3,2,1,0:T(2,128)(2,1)}) custom-call(s32[32,4]{1,0:T(8,128)} %copy.25.src_ref, bf16[4,2,4096]{2,1,0:T(2,128)(2,1)} %feat_ref.1), custom_call_target="tpu_custom_call" | custom-call | tf_op jit(solution)/shard_map/pallas_call | solution.py:307
  23.8 1.2 copy.28
  25.0 1.2 copy.29
  26.3 0.7 compare_reduce_fusion
  27.1 0.1 fusion
  27.2 0.2 select_reduce_fusion.1
  27.4 0.1 copy.32
  27.4 0.1 reshape_squeeze.14
  27.5 0.5 broadcast_select_fusion.1.next_ref
  28.1 0.1 copy.33
  28.1 0.6 reshape_squeeze.15.first_list_ref
  28.8 1.9 reshape_reshape.6
  30.6 1.4 copy.41
  32.1 0.0 copy-done
  32.1 0.1 copy.27
  32.2 0.1 eq.24
  32.3 0.1 fusion.3
  32.4 0.1 reshape.56
  32.5 0.1 fusion.2
  32.6 0.1 mul.34
  32.7 0.7 select_reduce_fusion.slot_ref
  33.4 132.9 %shard_map.56 = bf16[16,32,8,128]{3,2,1,0:T(8,128)(2,1)} custom-call(bf16[16,32,8,128]{3,2,1,0:T(8,128)(2,1)} %bitcast.27, bf16[32,512,128]{2,1,0:T(8,128)(2,1)} %bitcast.24, f32[32,1,128]{2,1,0:T(1,128)} %bitcast.31, s32[128]{0:T(128)} %select_reduce_fusion.slot_ref, s32[32]{0:T(128)} %broadcast_select_fusion.1.next_ref, s32[32]{0:T(128)} %reshape_squeeze.15.first_list_ref), custom_call_target="tpu_custom_call" | custom-call | tf_op jit(solution)/shard_map/pallas_call | solution.py:168
  166.3 0.0 copy-start.1
  166.3 1.4 copy.40
  167.7 0.3 reshape_reshape.7
  168.0 2.2 %copy.39 = bf16[4,16,2,4096]{3,2,0,1:T(2,128)(2,1)} copy(bf16[4,16,2,4096]{3,2,1,0:T(2,128)(2,1)S(1)} %reshape_reshape.7) | data formatting | bytes 2097152 | tf_op jit(solution)/shard_map/reshape;reshape | solution.py:443
  170.2 39.2 %shard_map.57 = bf16[4,2,4096]{2,1,0:T(2,128)(2,1)} custom-call(bf16[16,4,2,4096]{3,2,1,0:T(2,128)(2,1)} %bitcast.26), custom_call_target="tpu_custom_call" | custom-call | tf_op jit(solution)/shard_map/pallas_call | solution.py:368
  209.4 0.0 copy-done.1
  209.4 0.1 broadcast_compare_fusion
  209.5 1.6 broadcast_select_fusion
  (7 shorter events, 0.1 us)
Async XLA Ops:
  0.0 32.1 %copy-start = (s32[1,32,4]{1,2,0:T(4,128)S(1)}, s32[1,32,4]{1,2,0:T(4,128)}, u32[]{:S(2)}) copy-start(s32[1,32,4]{1,2,0:T(4,128)} %param.7) | copy-start | bytes 1540
  166.3 43.1 %copy-start.1 = (s32[4]{0:T(128)S(1)}, s32[4]{0:T(128)}, u32[]{:S(2)}) copy-start(s32[4]{0:T(128)} %param.9) | copy-start | bytes 52

commit v15 on v14

--- a/solution.py
+++ b/solution.py
@@ -136,8 +136,8 @@
 
         @pl.when(me_s < sections - 1)
         def _():
-            for d in range(owners):
-                outgoing_copy(m, d).start()
+            for k in range(owners):
+                outgoing_copy(m, lax.rem(me_c + k, owners)).start()
 
     @pl.when(me_s < sections - 1)
     def _():

time: 211 us -> 216 us (1.024)
  Pallas kernels: 194 us -> 199 us
    pallas_call x1, Pallas kernels: 133 us -> 136 us  [run_pipeline(): pl.pallas_call(functools.partial(pipeline_kernel, sections, owners, batch...]
where the time goes in v15:
time: 216 us
  Pallas kernels  199 us (92%)
  local copies, waits for them, and re-layouts  12.5 us (6%)
  other arithmetic  3.9 us (2%)
    pallas_call x1, Pallas kernels, run_pipeline(): pl.pallas_call(functools.partial(pipeline_kernel, sections, owners, batch...  136 us
    pallas_call x1, Pallas kernels, deliver_rows(): pl.pallas_call(functools.partial(rows_kernel, sections), out_shape=jax.Sh...  40.4 us
    pallas_call x1, Pallas kernels, exchange_patterns(): pl.pallas_call(functools.partial(pattern_kernel, sections, owners), out_s...  22.3 us

profile of v15, /device:TPU:28, one launch (start us, length us, event | category | flops | bytes accessed | tf_op | source)
XLA Modules:
  0.0 215.8 jit_solution(7971218300887450867)
XLA Ops:
  0.0 0.0 copy-start
  0.0 1.4 copy.25.src_ref
  1.4 22.3 %shard_map.55 = (s32[16,32,4]{2,1,0:T(8,128)}, s32[16,32,4]{2,1,0:T(8,128)}, bf16[4,16,2,4096]{3,2,1,0:T(2,128)(2,1)}) custom-call(s32[32,4]{1,0:T(8,128)} %copy.25.src_ref, bf16[4,2,4096]{2,1,0:T(2,128)(2,1)} %feat_ref.1), custom_call_target="tpu_custom_call" | custom-call | tf_op jit(solution)/shard_map/pallas_call | solution.py:307
  23.8 1.2 copy.28
  25.0 1.2 copy.29
  26.3 0.7 compare_reduce_fusion
  27.1 0.1 fusion
  27.2 0.2 select_reduce_fusion.1
  27.4 0.1 copy.32
  27.4 0.1 reshape_squeeze.14
  27.5 0.5 broadcast_select_fusion.1.next_ref
  28.1 0.1 copy.33
  28.1 0.6 reshape_squeeze.15.first_list_ref
  28.8 1.9 reshape_reshape.6
  30.6 1.4 copy.41
  32.1 0.0 copy-done
  32.1 0.1 copy.27
  32.2 0.1 eq.24
  32.3 0.1 fusion.3
  32.4 0.1 reshape.56
  32.5 0.1 fusion.2
  32.6 0.1 mul.34
  32.7 0.7 select_reduce_fusion.slot_ref
  33.4 136.4 %shard_map.56 = bf16[16,32,8,128]{3,2,1,0:T(8,128)(2,1)} custom-call(bf16[16,32,8,128]{3,2,1,0:T(8,128)(2,1)} %bitcast.27, bf16[32,512,128]{2,1,0:T(8,128)(2,1)} %bitcast.24, f32[32,1,128]{2,1,0:T(1,128)} %bitcast.31, s32[128]{0:T(128)} %select_reduce_fusion.slot_ref, s32[32]{0:T(128)} %broadcast_select_fusion.1.next_ref, s32[32]{0:T(128)} %reshape_squeeze.15.first_list_ref), custom_call_target="tpu_custom_call" | custom-call | tf_op jit(solution)/shard_map/pallas_call | solution.py:168
  169.8 0.0 copy-start.1
  169.8 1.4 copy.40
  171.3 0.3 reshape_reshape.7
  171.6 2.2 %copy.39 = bf16[4,16,2,4096]{3,2,0,1:T(2,128)(2,1)} copy(bf16[4,16,2,4096]{3,2,1,0:T(2,128)(2,1)S(1)} %reshape_reshape.7) | data formatting | bytes 2097152 | tf_op jit(solution)/shard_map/reshape;reshape | solution.py:443
  173.7 40.4 %shard_map.57 = bf16[4,2,4096]{2,1,0:T(2,128)(2,1)} custom-call(bf16[16,4,2,4096]{3,2,1,0:T(2,128)(2,1)} %bitcast.26), custom_call_target="tpu_custom_call" | custom-call | tf_op jit(solution)/shard_map/pallas_call | solution.py:368
  214.1 0.0 copy-done.1
  214.2 0.1 broadcast_compare_fusion
  214.2 1.6 broadcast_select_fusion
  (7 shorter events, 0.1 us)
Async XLA Ops:
  0.0 32.1 %copy-start = (s32[1,32,4]{1,2,0:T(4,128)S(1)}, s32[1,32,4]{1,2,0:T(4,128)}, u32[]{:S(2)}) copy-start(s32[1,32,4]{1,2,0:T(4,128)} %param.7) | copy-start | bytes 1540
  169.8 44.4 %copy-start.1 = (s32[4]{0:T(128)S(1)}, s32[4]{0:T(128)}, u32[]{:S(2)}) copy-start(s32[4]{0:T(128)} %param.9) | copy-start | bytes 52

commit v16 on v14

--- a/solution.py
+++ b/solution.py
@@ -338,9 +338,16 @@
     is_last = (me_s == last).astype(jnp.int32)
     pl.semaphore_wait(barrier, is_last * last + (1 - is_last))
 
+    own_rows = out_ref.shape[2]
+    piece_rows = src_ref.shape[3]
+
+    def part(r):
+        first = r * own_rows
+        return src_ref.at[:, first // piece_rows, :, pl.ds(first % piece_rows, own_rows), :]
+
     def row_copy(r):
         return pltpu.make_async_remote_copy(
-            src_ref=src_ref.at[r],
+            src_ref=part(r),
             dst_ref=out_ref,
             send_sem=send_sem.at[r],
             recv_sem=recv_sem,
@@ -352,7 +359,7 @@
     def _():
         for r in range(last):
             row_copy(r).start()
-        mine = pltpu.make_async_copy(src_ref.at[last], out_ref, local_sem)
+        mine = pltpu.make_async_copy(part(last), out_ref, local_sem)
         mine.start()
         mine.wait()
         for r in range(last):
@@ -363,11 +370,12 @@
         row_copy(0).wait_recv()
 
 
-def deliver_rows(row_parts, sections):
+def deliver_rows(row_parts, sections, own_rows):
     anywhere = pl.BlockSpec(memory_space=pl.ANY)
+    batches, _, blocks, _, lanes = row_parts.shape
     return pl.pallas_call(
         functools.partial(rows_kernel, sections),
-        out_shape=jax.ShapeDtypeStruct(row_parts.shape[1:], row_parts.dtype),
+        out_shape=jax.ShapeDtypeStruct((batches, blocks, own_rows, lanes), row_parts.dtype),
         in_specs=[anywhere],
         out_specs=anywhere,
         scratch_shapes=[
@@ -436,12 +444,10 @@
         owners,
     )
     finished = finished.reshape(batches, splits, blocks_own, piece_rows, block_size)
-    completed = finished.transpose(0, 1, 3, 2, 4).reshape(
-        batches, row_total, blocks_own * block_size
-    )
     own_rows = row_total // sections
-    outgoing_rows = completed.reshape(batches, sections, own_rows, blocks_own * block_size)
-    own_result = deliver_rows(outgoing_rows.transpose(1, 0, 2, 3), sections)
+    own_result = deliver_rows(finished, sections, own_rows).transpose(0, 2, 1, 3).reshape(
+        batches, own_rows, blocks_own * block_size
+    )
     row_ids = section_idx * own_rows + jnp.arange(own_rows, dtype=jnp.int32)
     row_mask = row_ids[None, :] < batch_rows[:, None]
     return jnp.where(row_mask[:, :, None], own_result, jnp.zeros_like(own_result))

time: 211 us -> 207 us (0.981)
  local copies, waits for them, and re-layouts: 12.5 us -> 8.66 us
    another operation x2 -> x0, local copies, waits for them, and re-layouts: 2.44 us -> none  [body(): completed.reshape(batches, sections, own_rows, blocks_own * block_size)]
where the time goes in v16:
time: 207 us
  Pallas kernels  194 us (94%)
  local copies, waits for them, and re-layouts  8.66 us (4%)
  other arithmetic  3.9 us (2%)
    pallas_call x1, Pallas kernels, run_pipeline(): pl.pallas_call(functools.partial(pipeline_kernel, sections, owners, batch...  132 us
    pallas_call x1, Pallas kernels, deliver_rows(): pl.pallas_call(functools.partial(rows_kernel, sections), out_shape=jax.Sh...  39 us
    pallas_call x1, Pallas kernels, exchange_patterns(): pl.pallas_call(functools.partial(pattern_kernel, sections, owners), out_s...  22.3 us

profile of v16, /device:TPU:28, one launch (start us, length us, event | category | flops | bytes accessed | tf_op | source)
XLA Modules:
  0.0 206.7 jit_solution(12906783892476425708)
XLA Ops:
  0.0 0.0 copy-start
  0.0 1.4 copy.21.src_ref
  1.4 22.3 %shard_map.55 = (s32[16,32,4]{2,1,0:T(8,128)}, s32[16,32,4]{2,1,0:T(8,128)}, bf16[4,16,2,4096]{3,2,1,0:T(2,128)(2,1)}) custom-call(s32[32,4]{1,0:T(8,128)} %copy.21.src_ref, bf16[4,2,4096]{2,1,0:T(2,128)(2,1)} %feat_ref.1), custom_call_target="tpu_custom_call" | custom-call | tf_op jit(solution)/shard_map/pallas_call | solution.py:307
  23.8 1.2 copy.24
  25.0 1.2 copy.25
  26.3 0.7 compare_reduce_fusion
  27.1 0.1 fusion
  27.2 0.2 select_reduce_fusion.1
  27.4 0.1 copy.28
  27.4 0.1 reshape_squeeze.14
  27.5 0.5 broadcast_select_fusion.1.next_ref
  28.1 0.1 copy.29
  28.1 0.6 reshape_squeeze.15.first_list_ref
  28.8 1.9 reshape_reshape.3
  30.6 1.5 copy.31
  32.1 0.0 copy-start.1
  32.1 0.0 copy-done
  32.1 0.1 copy.23
  32.2 0.1 eq.24
  32.3 0.1 fusion.3
  32.4 0.1 reshape.59
  32.5 0.1 fusion.2
  32.6 0.1 mul.34
  32.7 0.7 select_reduce_fusion.slot_ref
  33.5 132.5 %shard_map.56 = bf16[16,32,8,128]{3,2,1,0:T(8,128)(2,1)} custom-call(bf16[16,32,8,128]{3,2,1,0:T(8,128)(2,1)} %bitcast.21, bf16[32,512,128]{2,1,0:T(8,128)(2,1)} %bitcast.20, f32[32,1,128]{2,1,0:T(1,128)} %bitcast.25, s32[128]{0:T(128)} %select_reduce_fusion.slot_ref, s32[32]{0:T(128)} %broadcast_select_fusion.1.next_ref, s32[32]{0:T(128)} %reshape_squeeze.15.first_list_ref), custom_call_target="tpu_custom_call" | custom-call | tf_op jit(solution)/shard_map/pallas_call | solution.py:168
  165.9 39.0 %shard_map.57 = bf16[4,32,2,128]{3,2,1,0:T(2,128)(2,1)} custom-call(bf16[4,4,32,8,128]{4,3,2,1,0:T(8,128)(2,1)} %bitcast.22), custom_call_target="tpu_custom_call" | custom-call | tf_op jit(solution)/shard_map/pallas_call | solution.py:376
  205.0 0.0 copy-done.1
  205.0 0.1 broadcast_compare_fusion
  205.1 1.6 broadcast_select_fusion
  (7 shorter events, 0.1 us)
Async XLA Ops:
  0.0 32.1 %copy-start = (s32[1,32,4]{1,2,0:T(4,128)S(1)}, s32[1,32,4]{1,2,0:T(4,128)}, u32[]{:S(2)}) copy-start(s32[1,32,4]{1,2,0:T(4,128)} %param.7) | copy-start | bytes 1540
  32.1 172.9 %copy-start.1 = (s32[4]{0:T(128)S(1)}, s32[4]{0:T(128)}, u32[]{:S(2)}) copy-start(s32[4]{0:T(128)} %param.9) | copy-start | bytes 52

commit v17 on v16

--- a/solution.py
+++ b/solution.py
@@ -248,23 +248,32 @@
         for d in range(owners):
             nxt_copy(me_s - 1, d, me_c).start()
 
+    sent_rows = feat_ref.shape[2]
+    piece_rows = rows_ref.shape[3]
+
+    def rows_part(r):
+        first = r * sent_rows
+        return rows_ref.at[:, first // piece_rows, :, pl.ds(first % piece_rows, sent_rows), :]
+
     def rows_copy(r):
         return pltpu.make_async_remote_copy(
             src_ref=feat_ref,
-            dst_ref=rows_ref.at[:, r],
+            dst_ref=rows_part(r),
             send_sem=rows_send,
             recv_sem=rows_recv.at[r],
             device_id=(0, me_c),
             device_id_type=MESH_ID,
         )
 
-    @pl.when(me_s > 0)
-    def _():
-        rows_copy(me_s).start()
-
-    @pl.when(me_s == 0)
-    def _():
-        own_rows = pltpu.make_async_copy(feat_ref, rows_ref.at[:, 0], rows_sem)
+    for r in range(1, sections):
+
+        @pl.when(me_s == r)
+        def _():
+            rows_copy(r).start()
+
+    @pl.when(me_s == 0)
+    def _():
+        own_rows = pltpu.make_async_copy(feat_ref, rows_part(0), rows_sem)
         own_rows.start()
         own_rows.wait()
 
@@ -288,9 +297,11 @@
         for e in range(owners):
             nxt_copy(me_s + 1, e, e).wait_recv()
 
-    @pl.when(me_s > 0)
-    def _():
-        rows_copy(me_s).wait_send()
+    for r in range(1, sections):
+
+        @pl.when(me_s == r)
+        def _():
+            rows_copy(r).wait_send()
 
     @pl.when(me_s == 0)
     def _():
@@ -298,11 +309,14 @@
             rows_copy(r).wait_recv()
 
 
-def exchange_patterns(local_sources, features, sections, owners):
+def exchange_patterns(local_sources, features, sections, owners, piece_rows, lanes):
     table = jax.ShapeDtypeStruct((owners,) + local_sources.shape, local_sources.dtype)
+    batches, sent_rows, width = features.shape
+    row_total = sent_rows * sections
     rows = jax.ShapeDtypeStruct(
-        (features.shape[0], sections) + features.shape[1:], features.dtype
-    )
+        (batches, row_total // piece_rows, width // lanes, piece_rows, lanes), features.dtype
+    )
+    features = features.reshape(batches, sent_rows, width // lanes, lanes).transpose(0, 2, 1, 3)
     anywhere = pl.BlockSpec(memory_space=pl.ANY)
     return pl.pallas_call(
         functools.partial(pattern_kernel, sections, owners),
@@ -397,7 +411,9 @@
     nonzero_count = local_w.shape[1]
     block_size = local_w.shape[2]
     local_src = sources[0].reshape(blocks_own * nonzero_count)
-    own_table, next_table, row_parts = exchange_patterns(sources[0], features, sections, owners)
+    own_table, next_table, row_parts = exchange_patterns(
+        sources[0], features, sections, owners, 8, block_size
+    )
     local_rows = jnp.arange(blocks_own, dtype=jnp.int32)
     below = (local_rows[:, None] <= local_rows[None, :]).astype(jnp.float32)
     slot_ids = jnp.arange(CAP, dtype=jnp.int32)
@@ -428,11 +444,9 @@
     )
     batches = features.shape[0]
     row_total = features.shape[1] * sections
-    all_inputs = row_parts.reshape(batches, row_total, -1)
     piece_rows = 8
     splits = row_total // piece_rows
-    first_blocks = all_inputs.reshape(batches * splits, piece_rows, blocks_own, block_size)
-    first_blocks = first_blocks.transpose(0, 2, 1, 3)
+    first_blocks = row_parts.reshape(batches * splits, blocks_own, piece_rows, block_size)
     finished = run_pipeline(
         first_blocks,
         local_w.reshape(blocks_own, nonzero_count * block_size, block_size),

time: 207 us -> 205 us (level)
  local copies, waits for them, and re-layouts: 8.66 us -> 5.92 us
    another operation x2 -> x0, local copies, waits for them, and re-layouts: 3.33 us -> none  [body(): all_inputs.reshape(batches * splits, piece_rows, blocks_own, block_size)]
where the time goes in v17:
time: 205 us
  Pallas kernels  194 us (95%)
  local copies, waits for them, and re-layouts  5.92 us (3%)
  other arithmetic  4.56 us (2%)
    pallas_call x1, Pallas kernels, run_pipeline(): pl.pallas_call(functools.partial(pipeline_kernel, sections, owners, batch...  132 us
    pallas_call x1, Pallas kernels, deliver_rows(): pl.pallas_call(functools.partial(rows_kernel, sections), out_shape=jax.Sh...  39.1 us
    pallas_call x1, Pallas kernels, exchange_patterns(): pl.pallas_call(functools.partial(pattern_kernel, sections, owners), out_s...  22.3 us

profile of v17, /device:TPU:28, one launch (start us, length us, event | category | flops | bytes accessed | tf_op | source)
XLA Modules:
  0.0 204.5 jit_solution(8944406268119985835)
XLA Ops:
  0.0 0.7 broadcast_compare_fusion
  0.7 1.4 copy.19.src_ref
  2.1 0.8 copy.20
  2.9 0.1 eq.24
  3.0 0.1 fusion.3
  3.1 0.1 reshape.67
  3.2 0.1 fusion.2
  3.3 0.1 mul.34
  3.4 0.7 select_reduce_fusion.slot_ref
  4.1 22.3 %shard_map.55 = (s32[16,32,4]{2,1,0:T(8,128)}, s32[16,32,4]{2,1,0:T(8,128)}, bf16[4,4,32,8,128]{4,3,2,1,0:T(8,128)(2,1)}) custom-call(s32[32,4]{1,0:T(8,128)} %copy.19.src_ref, bf16[4,32,2,128]{3,2,1,0:T(2,128)(2,1)} %bitcast.26), custom_call_target="tpu_custom_call" | custom-call | tf_op jit(solution)/shard_map/pallas_call | solution.py:321
  26.4 1.2 copy.21
  27.7 1.2 copy.22
  29.0 0.7 compare_reduce_fusion
  29.7 0.1 fusion
  29.9 0.2 select_reduce_fusion.1
  30.0 0.1 copy.26
  30.1 0.6 reshape_squeeze.15.first_list_ref
  30.8 0.1 copy.25
  30.8 0.1 reshape_squeeze.14
  30.9 0.5 broadcast_select_fusion.1.next_ref
  31.5 132.3 %shard_map.56 = bf16[16,32,8,128]{3,2,1,0:T(8,128)(2,1)} custom-call(bf16[16,32,8,128]{3,2,1,0:T(8,128)(2,1)} %bitcast.23, bf16[32,512,128]{2,1,0:T(8,128)(2,1)} %bitcast.21, f32[32,1,128]{2,1,0:T(1,128)} %bitcast.27, s32[128]{0:T(128)} %select_reduce_fusion.slot_ref, s32[32]{0:T(128)} %broadcast_select_fusion.1.next_ref, s32[32]{0:T(128)} %reshape_squeeze.15.first_list_ref), custom_call_target="tpu_custom_call" | custom-call | tf_op jit(solution)/shard_map/pallas_call | solution.py:168
  163.8 39.1 %shard_map.57 = bf16[4,32,2,128]{3,2,1,0:T(2,128)(2,1)} custom-call(bf16[4,4,32,8,128]{4,3,2,1,0:T(8,128)(2,1)} %bitcast.22), custom_call_target="tpu_custom_call" | custom-call | tf_op jit(solution)/shard_map/pallas_call | solution.py:390
  202.9 1.6 broadcast_select_fusion
  (7 shorter events, 0.1 us)
